TPU v7x, 256 devices: a whole 4x4x8 slice. The times are simulated.
256 devices in a mesh: gy: 64 (over x, y, z_hi, core), gz: 4 (over z_lo).
Axes of the slice: x: 4, y: 4, z: 8 (z_hi: 2, z_lo: 4; z = z_hi * 4 + z_lo), core: 2. Of those that a mesh axis runs over, the one named last changes fastest.
Arguments:
- efield_check: bfloat16 [3, 2048, 8, 1024], P(None, 'gy', None, 'gz'), may hold values from -6 to 6
- hfield_check: bfloat16 [3, 2048, 8, 1024], P(None, 'gy', None, 'gz'), may hold values from -6 to 6
- polar_check: bfloat16 [3, 2048, 8, 1024], P(None, 'gy', None, 'gz'), may hold values from -4 to 4
- rate_check: bfloat16 [3, 2048, 8, 1024], P(None, 'gy', None, 'gz'), may hold values from -4 to 4
- levels_check: bfloat16 [2, 2048, 8, 1024], P(None, 'gy', None, 'gz'), may hold values from 0.049804688 to 0.5
- efield_seed: float32 [3, 2048, 8, 1024], P(None, 'gy', None, 'gz'), may hold values from -6 to 6
- hfield_seed: float32 [3, 2048, 8, 1024], P(None, 'gy', None, 'gz'), may hold values from -6 to 6
- polar_seed: float32 [3, 2048, 8, 1024], P(None, 'gy', None, 'gz'), may hold values from -6 to 6
- rate_seed: float32 [3, 2048, 8, 1024], P(None, 'gy', None, 'gz'), may hold values from -6 to 6
- levels_seed: float32 [2, 2048, 8, 1024], P(None, 'gy', None, 'gz'), may hold values from -6 to 6
- material_labels: int32 [2048, 8, 1024], P('gy', None, 'gz'), may hold values from 0 to 3
- gain_labels: int32 [2048, 8, 1024], P('gy', None, 'gz'), may hold values 0 or 1
- inverse_table: float32 [4], replicated, may hold values from 0.08 to 1
- source_field: float32 [2048, 8, 1024], P('gy', None, 'gz'), may hold values from -6 to 6
- start_step: int32 [1], replicated, may hold values from 0 to 255
Outputs:
- efield_grad: float32 [3, 2048, 8, 1024], P(None, 'gy', None, 'gz')
- hfield_grad: float32 [3, 2048, 8, 1024], P(None, 'gy', None, 'gz')
- polar_grad: float32 [3, 2048, 8, 1024], P(None, 'gy', None, 'gz')
- rate_grad: float32 [3, 2048, 8, 1024], P(None, 'gy', None, 'gz')
- levels_grad: float32 [2, 2048, 8, 1024], P(None, 'gy', None, 'gz')
- cell_grad: float32 [2048, 8, 1024], P('gy', None, 'gz')
- table_grad: float32 [4], replicated
All inputs are finite; a program needn't handle non-finite values. No bound on the sum of `gain_labels` on one device may be relied on, other than what follows from the above.
Results may differ from a plain program's by a relative error of at most 0.0003.
Values may be sent and summed in bfloat16 or wider, within the bound.
No kernel may reach another device: no remote copies, remote signals or barrier semaphores. Data moves between devices by JAX's collectives and lax.ppermute only.
A program may use at most 64 MiB of HBM per device.

v0:
```python
import math

import jax
import jax.numpy as jnp
from jax import lax
from jax.sharding import PartitionSpec as P

MAGNETIC_STEP = 0.5
ELECTRIC_STEP = 0.5
TIME_STEP = 0.5
DAMPING = 0.9
STIFFNESS = 0.3
COUPLING = 0.4
PUMPING = 0.05
UPPER_DECAY = 0.02
LOWER_DECAY = 0.3
STIMULATED = 0.2
SOURCE_OMEGA = 0.35


def shifted(block, axis, distance):
    devices = range(lax.axis_size(axis))
    route = [(i - distance, i) for i in devices if i - distance in devices]
    return lax.ppermute(block, axis, route)


def front(values, axis):
    rest = lax.slice_in_dim(values, 1, values.shape[axis], axis=axis)
    border = jnp.zeros_like(lax.slice_in_dim(values, 0, 1, axis=axis))
    return jnp.concatenate([rest, border], axis)


def behind(values, axis):
    rest = lax.slice_in_dim(values, 0, values.shape[axis] - 1, axis=axis)
    border = jnp.zeros_like(lax.slice_in_dim(values, 0, 1, axis=axis))
    return jnp.concatenate([border, rest], axis)


def curl_from(along_x, along_y, along_z):
    return jnp.stack([along_y[2] - along_z[1], along_z[0] - along_x[2], along_x[1] - along_y[0]])


def curl_forward(field):
    front_row = shifted(field[:, :1], "gy", -1)
    front_column = shifted(field[:, :, :, :1], "gz", -1)
    along_y = jnp.concatenate([field[:, 1:], front_row], 1) - field
    along_z = jnp.concatenate([field[:, :, :, 1:], front_column], 3) - field
    along_x = front(field, 2) - field
    return curl_from(along_x, along_y, along_z)


def curl_backward(field):
    back_row = shifted(field[:, -1:], "gy", 1)
    back_column = shifted(field[:, :, :, -1:], "gz", 1)
    along_y = field - jnp.concatenate([back_row, field[:, :-1]], 1)
    along_z = field - jnp.concatenate([back_column, field[:, :, :, :-1]], 3)
    along_x = field - behind(field, 2)
    return curl_from(along_x, along_y, along_z)


def local_update(
    efield, polar_field, polar_rate, levels, curl_field, inverse, gain_region, source_push
):
    rate_next = (
        DAMPING * polar_rate
        - STIFFNESS * polar_field
        + COUPLING * gain_region * (levels[0] - levels[1]) * efield
    )
    polar_next = polar_field + TIME_STEP * rate_next
    forcing = ELECTRIC_STEP * curl_field - (polar_next - polar_field)
    forcing = jnp.concatenate([forcing[:2], forcing[2:] - source_push[None]], 0)
    efield_next = efield + inverse * forcing
    stimulated = STIMULATED * gain_region * jnp.sum(efield_next * rate_next, axis=0)
    upper = (
        levels[0]
        + TIME_STEP * (PUMPING * (1.0 - levels[0] - levels[1]) - UPPER_DECAY * levels[0])
        - stimulated
    )
    lower = levels[1] + TIME_STEP * (UPPER_DECAY * levels[0] - LOWER_DECAY * levels[1]) + stimulated
    return (efield_next, polar_next, rate_next, jnp.stack([upper, lower]))


def reverse_local(
    efield, polar_field, polar_rate, levels, curl_field, inverse, gain_region, source_push, seeds
):

    def update(first, second, third, fourth, fifth, sixth):
        return local_update(first, second, third, fourth, fifth, sixth, gain_region, source_push)

    unused, pullback = jax.vjp(update, efield, polar_field, polar_rate, levels, curl_field, inverse)
    return pullback(seeds)


def material_map(material_labels, inverse_table):
    inverse = jnp.zeros(material_labels.shape, jnp.float32)
    for label in range(inverse_table.shape[0]):
        inverse = inverse + jnp.where(
            material_labels == label, inverse_table[label], jnp.float32(0.0)
        )
    return inverse


def label_sums(material_labels, values, count):
    return jnp.stack(
        [
            jnp.sum(jnp.where(material_labels == label, values, jnp.float32(0.0)))
            for label in range(count)
        ]
    )


def step_total(material_labels, values, count):
    return lax.psum(label_sums(material_labels, values, count), ("gy", "gz"))


def on_device(
    efield_check,
    hfield_check,
    polar_check,
    rate_check,
    levels_check,
    efield_seed,
    hfield_seed,
    polar_seed,
    rate_seed,
    levels_seed,
    material_labels,
    gain_labels,
    inverse_table,
    source_field,
    start_step,
):
    count = inverse_table.shape[0]
    inverse = material_map(material_labels, inverse_table)
    gain_region = gain_labels.astype(jnp.float32)
    start = start_step[0].astype(jnp.float32)
    first_sine = jnp.sin(SOURCE_OMEGA * start)
    push_first = first_sine * source_field
    push_second = jnp.sin(SOURCE_OMEGA * (start + 1.0)) * source_field
    efield = efield_check.astype(jnp.float32)
    polar_field = polar_check.astype(jnp.float32)
    polar_rate = rate_check.astype(jnp.float32)
    levels = levels_check.astype(jnp.float32)
    hfield = hfield_check.astype(jnp.float32)
    hfield_mid = hfield - MAGNETIC_STEP * curl_forward(efield)
    curl_first = curl_backward(hfield_mid)
    state_one = local_update(
        efield, polar_field, polar_rate, levels, curl_first, inverse, gain_region, push_first
    )
    hfield_next = hfield_mid - MAGNETIC_STEP * curl_forward(state_one[0])
    curl_second = curl_backward(hfield_next)
    back_e, back_p, back_q, back_n, back_c, grad_second = reverse_local(
        state_one[0],
        state_one[1],
        state_one[2],
        state_one[3],
        curl_second,
        inverse,
        gain_region,
        push_second,
        (efield_seed, polar_seed, rate_seed, levels_seed),
    )
    h_back = hfield_seed + curl_forward(back_c)
    e_back = back_e - MAGNETIC_STEP * curl_backward(h_back)
    last_e, polar_grad, rate_grad, levels_grad, last_c, grad_first = reverse_local(
        efield,
        polar_field,
        polar_rate,
        levels,
        curl_first,
        inverse,
        gain_region,
        push_first,
        (e_back, back_p, back_q, back_n),
    )
    hfield_grad = h_back + curl_forward(last_c)
    efield_grad = last_e - MAGNETIC_STEP * curl_backward(hfield_grad)
    cell_grad = grad_second + grad_first
    cells = (
        material_labels.shape[0]
        * material_labels.shape[1]
        * material_labels.shape[2]
        * lax.axis_size("gy")
        * lax.axis_size("gz")
    )
    totals = step_total(material_labels, grad_second, count) + step_total(
        material_labels, grad_first, count
    )
    table_grad = totals * (1.0 / math.sqrt(cells))
    return (efield_grad, hfield_grad, polar_grad, rate_grad, levels_grad, cell_grad, table_grad)


def solution(mesh):
    placed = (
        P(None, "gy", None, "gz"),
        P(None, "gy", None, "gz"),
        P(None, "gy", None, "gz"),
        P(None, "gy", None, "gz"),
        P(None, "gy", None, "gz"),
        P(None, "gy", None, "gz"),
        P(None, "gy", None, "gz"),
        P(None, "gy", None, "gz"),
        P(None, "gy", None, "gz"),
        P(None, "gy", None, "gz"),
        P("gy", None, "gz"),
        P("gy", None, "gz"),
        P(),
        P("gy", None, "gz"),
        P(),
    )
    return jax.shard_map(
        on_device,
        mesh=mesh,
        in_specs=placed,
        out_specs=(
            P(None, "gy", None, "gz"),
            P(None, "gy", None, "gz"),
            P(None, "gy", None, "gz"),
            P(None, "gy", None, "gz"),
            P(None, "gy", None, "gz"),
            P("gy", None, "gz"),
            P(),
        ),
        check_vma=False,
    )
```

profile of v0, /device:TPU:2, one launch (start us, length us, event | category | flops | bytes accessed | tf_op | source)
XLA Modules:
  0.0 215.5 jit_solution(16821565105719444470)
XLA Ops:
  1.7 1.3 collective-permute-start.1
  3.0 11.0 %collective-permute-start = (f32[3,1,8,256]{3,2,1,0:T(8,128)S(1)}, f32[3,1,8,256]{3,2,1,0:T(8,128)S(1)}, u32[]{:S(2)}, u32[]{:S(2)}) collective-permute-start(f32[3,1,8,256]{3,2,1,0:T(8,128)S(1)} %slice.410), channel_id=1, source_target_pairs={{4,0},{8,4},{12,8},{16,12},{20,16},{24,20},{28,24},{32,28},{36,32}... | collective-permute-start | bytes 73736 | tf_op jit(solution)/shard_map/ppermute | solution.py:24
  17.4 4.3 %collective-permute-start.3 = (f32[3,32,8,1]{3,2,1,0:T(8,128)S(1)}, f32[3,32,8,1]{3,2,1,0:T(8,128)S(1)}, u32[]{:S(2)}, u32[]{:S(2)}) collective-permute-start(f32[3,32,8,1]{3,2,1,0:T(8,128)S(1)} %slice.423), channel_id=1, source_target_pairs={{0,1},{1,2},{2,3},{4,5},{5,6},{6,7},{8,9},{9,10},{10,11},{12,13},{... | collective-permute-start | bytes 9224 | tf_op jit(solution)/shard_map/ppermute | solution.py:24
  21.7 5.1 %collective-permute-start.2 = (f32[3,1,8,256]{3,2,1,0:T(8,128)S(1)}, f32[3,1,8,256]{3,2,1,0:T(8,128)S(1)}, u32[]{:S(2)}, u32[]{:S(2)}) collective-permute-start(f32[3,1,8,256]{3,2,1,0:T(8,128)S(1)} %slice.420), channel_id=1, source_target_pairs={{0,4},{4,8},{8,12},{12,16},{16,20},{20,24},{24,28},{28,32},{32,36}... | collective-permute-start | bytes 73736 | tf_op jit(solution)/shard_map/ppermute | solution.py:24
  26.8 2.8 %select_add_fusion.2 = (f32[32,8,256]{2,1,0:T(8,128)S(1)}, pred[32,8,256]{2,1,0:T(8,128)(4,1)S(1)}, pred[32,8,256]{2,1,0:T(8,128)(4,1)S(1)}, pred[32,8,256]{2,1,...) fusion(f32[]{:T(128)} %bitcast.6, f32[]{:T(128)} %bitcast.5, f32[]{:T(128)} %bitcast.4, ...), kind=kLoop, calls=%fused_computation.118 | loop fusion | flops 983040 | bytes 1835024 | tf_op jit(solution)/shard_map/add | solution.py:97
  30.5 8.8 %collective-permute-done.2 = f32[3,1,8,256]{3,2,1,0:T(8,128)S(1)} collective-permute-done((f32[3,1,8,256]{3,2,1,0:T(8,128)S(1)}, f32[3,1,8,256]{3,2,1,0:T(8,128)S(1)}, u32[]{:S(2)}, u32[]{:S(2)}) %collective-permute-start.2) | collective-permute-done | bytes 24608 | tf_op jit(solution)/shard_map/ppermute | solution.py:24
  42.5 1.4 collective-permute-start.5
  43.9 1.9 collective-permute-start.4
  46.5 5.8 %collective-permute-done.5 = f32[3,32,8,1]{3,2,1,0:T(8,128)S(1)} collective-permute-done((f32[3,32,8,1]{3,2,1,0:T(8,128)S(1)}, f32[3,32,8,1]{3,2,1,0:T(8,128)S(1)}, u32[]{:S(2)}, u32[]{:S(2)}) %collective-permute-start.5) | collective-permute-done | bytes 3104 | tf_op jit(solution)/shard_map/ppermute | solution.py:24
  53.0 2.0 collective-permute-start.7
  55.0 1.9 collective-permute-start.6
  57.2 5.5 %collective-permute-done.7 = f32[3,32,8,1]{3,2,1,0:T(8,128)S(1)} collective-permute-done((f32[3,32,8,1]{3,2,1,0:T(8,128)S(1)}, f32[3,32,8,1]{3,2,1,0:T(8,128)S(1)}, u32[]{:S(2)}, u32[]{:S(2)}) %collective-permute-start.7) | collective-permute-done | bytes 3104 | tf_op jit(solution)/shard_map/ppermute | solution.py:24
  62.8 7.7 %collective-permute-done.6 = f32[3,1,8,256]{3,2,1,0:T(8,128)S(1)} collective-permute-done((f32[3,1,8,256]{3,2,1,0:T(8,128)S(1)}, f32[3,1,8,256]{3,2,1,0:T(8,128)S(1)}, u32[]{:S(2)}, u32[]{:S(2)}) %collective-permute-start.6) | collective-permute-done | bytes 24608 | tf_op jit(solution)/shard_map/ppermute | solution.py:24
  75.1 1.3 collective-permute-start.9
  76.4 1.9 collective-permute-start.8
  79.8 5.0 %collective-permute-done.9 = f32[3,32,8,1]{3,2,1,0:T(8,128)S(1)} collective-permute-done((f32[3,32,8,1]{3,2,1,0:T(8,128)S(1)}, f32[3,32,8,1]{3,2,1,0:T(8,128)S(1)}, u32[]{:S(2)}, u32[]{:S(2)}) %collective-permute-start.9) | collective-permute-done | bytes 3104 | tf_op jit(solution)/shard_map/ppermute | solution.py:24
  85.3 1.1 copy-done.2
  86.7 2.0 collective-permute-start.11
  88.8 1.9 collective-permute-start.10
  90.8 4.8 %collective-permute-done.11 = f32[3,32,8,1]{3,2,1,0:T(8,128)S(1)} collective-permute-done((f32[3,32,8,1]{3,2,1,0:T(8,128)S(1)}, f32[3,32,8,1]{3,2,1,0:T(8,128)S(1)}, u32[]{:S(2)}, u32[]{:S(2)}) %collective-permute-start.11) | collective-permute-done | bytes 3104 | tf_op jit(solution)/shard_map/ppermute | solution.py:24
  95.6 7.6 %collective-permute-done.10 = f32[3,1,8,256]{3,2,1,0:T(8,128)S(1)} collective-permute-done((f32[3,1,8,256]{3,2,1,0:T(8,128)S(1)}, f32[3,1,8,256]{3,2,1,0:T(8,128)S(1)}, u32[]{:S(2)}, u32[]{:S(2)}) %collective-permute-start.10) | collective-permute-done | bytes 24608 | tf_op jit(solution)/shard_map/ppermute | solution.py:24
  104.9 1.6 multiply_add_fusion
  107.4 1.3 collective-permute-start.13
  108.7 2.1 collective-permute-start.12
  110.8 1.6 select_reduce_fusion.7
  112.4 5.1 %maximum_add_fusion.2 = f32[4]{0:T(128)S(1)} fusion(f32[1]{0:T(128)} %bitcast.19, f32[1]{0:T(128)} %bitcast.18, f32[1]{0:T(128)} %bitcast.17, f32[1]{0:T(128)} %bitcast.16, f32[1]{0:T(128)} %bitcast.23, f32[1]{0:T(128)} %bitcast.22, f32[1]{0:T(128)} %bitcast.21, f32[1]{0:T(128)} %bitcast.20), kind=kLoop, calls=%fused_computation.132 | loop fusion | flops 28 | bytes 48 | tf_op jit(solution)/shard_map/add | solution.py:186
  118.7 76.3 %psum.16 = f32[4]{0:T(128)S(1)} all-reduce(f32[4]{0:T(128)S(1)} %maximum_add_fusion.2), channel_id=1, replica_groups=mesh['gy'=64,'gz'=4] {'gy','gz'}, use_global_device_ids=true, to_apply=%region_9.10 | all-reduce | flops 4 | bytes 32 | tf_op jit(solution)/shard_map/psum | solution.py:113
  195.4 1.3 maximum_subtract_fusion.11
  198.1 2.1 collective-permute-start.15
  200.2 1.9 collective-permute-start.14
  202.7 6.1 %collective-permute-done.15 = f32[3,32,8,1]{3,2,1,0:T(8,128)S(1)} collective-permute-done((f32[3,32,8,1]{3,2,1,0:T(8,128)S(1)}, f32[3,32,8,1]{3,2,1,0:T(8,128)S(1)}, u32[]{:S(2)}, u32[]{:S(2)}) %collective-permute-start.15) | collective-permute-done | bytes 3104 | tf_op jit(solution)/shard_map/ppermute | solution.py:24
  208.8 5.1 %collective-permute-done.14 = f32[3,1,8,256]{3,2,1,0:T(8,128)S(1)} collective-permute-done((f32[3,1,8,256]{3,2,1,0:T(8,128)S(1)}, f32[3,1,8,256]{3,2,1,0:T(8,128)S(1)}, u32[]{:S(2)}, u32[]{:S(2)}) %collective-permute-start.14) | collective-permute-done | bytes 24608 | tf_op jit(solution)/shard_map/ppermute | solution.py:24
  (130 shorter events, 23.5 us)
Async XLA Ops:
  0.6 2.3 %copy-start = (bf16[3,32,8,256]{3,2,1,0:T(8,128)(2,1)S(1)}, bf16[3,32,8,256]{3,2,1,0:T(8,128)(2,1)}, u32[]{:S(2)}) copy-start(bf16[3,32,8,256]{3,2,1,0:T(8,128)(2,1)} %param.15) | copy-start | bytes 1179652
  1.7 14.2 %collective-permute-start.1 = (f32[3,32,8,1]{3,2,1,0:T(8,128)S(1)}, f32[3,32,8,1]{3,2,1,0:T(8,128)S(1)}, u32[]{:S(2)}, u32[]{:S(2)}) collective-permute-start(f32[3,32,8,1]{3,2,1,0:T(8,128)S(1)} %slice.413), channel_id=1, source_target_pairs={{1,0},{2,1},{3,2},{5,4},{6,5},{7,6},{9,8},{10,9},{11,10},{13,12},{... | collective-permute-start | bytes 9224 | tf_op jit(solution)/shard_map/ppermute | solution.py:24
  3.0 11.0 %copy-start.20 = (f32[4]{0:T(128)S(1)}, f32[4]{0:T(128)}, u32[]{:S(2)}) copy-start(f32[4]{0:T(128)} %param.27) | copy-start | bytes 52
  3.0 12.8 %collective-permute-start = (f32[3,1,8,256]{3,2,1,0:T(8,128)S(1)}, f32[3,1,8,256]{3,2,1,0:T(8,128)S(1)}, u32[]{:S(2)}, u32[]{:S(2)}) collective-permute-start(f32[3,1,8,256]{3,2,1,0:T(8,128)S(1)} %slice.410), channel_id=1, source_target_pairs={{4,0},{8,4},{12,8},{16,12},{20,16},{24,20},{28,24},{32,28},{36,32}... | collective-permute-start | bytes 73736 | tf_op jit(solution)/shard_map/ppermute | solution.py:24
  17.2 9.6 %copy-start.13 = (s32[32,8,256]{2,1,0:T(8,128)S(1)}, s32[32,8,256]{2,1,0:T(8,128)}, u32[]{:S(2)}) copy-start(s32[32,8,256]{2,1,0:T(8,128)} %param.26) | copy-start | bytes 786436
  17.2 9.6 %copy-start.19 = (s32[32,8,256]{2,1,0:T(8,128)S(1)}, s32[32,8,256]{2,1,0:T(8,128)}, u32[]{:S(2)}) copy-start(s32[32,8,256]{2,1,0:T(8,128)} %param.25) | copy-start | bytes 786436
  17.4 13.0 %collective-permute-start.3 = (f32[3,32,8,1]{3,2,1,0:T(8,128)S(1)}, f32[3,32,8,1]{3,2,1,0:T(8,128)S(1)}, u32[]{:S(2)}, u32[]{:S(2)}) collective-permute-start(f32[3,32,8,1]{3,2,1,0:T(8,128)S(1)} %slice.423), channel_id=1, source_target_pairs={{0,1},{1,2},{2,3},{4,5},{5,6},{6,7},{8,9},{9,10},{10,11},{12,13},{... | collective-permute-start | bytes 9224 | tf_op jit(solution)/shard_map/ppermute | solution.py:24
  21.7 17.5 %collective-permute-start.2 = (f32[3,1,8,256]{3,2,1,0:T(8,128)S(1)}, f32[3,1,8,256]{3,2,1,0:T(8,128)S(1)}, u32[]{:S(2)}, u32[]{:S(2)}) collective-permute-start(f32[3,1,8,256]{3,2,1,0:T(8,128)S(1)} %slice.420), channel_id=1, source_target_pairs={{0,4},{4,8},{8,12},{12,16},{16,20},{20,24},{24,28},{28,32},{32,36}... | collective-permute-start | bytes 73736 | tf_op jit(solution)/shard_map/ppermute | solution.py:24
  39.6 1.1 copy-start.4
  42.4 3.4 %copy-start.5 = (f32[2,32,8,256]{3,2,1,0:T(8,128)S(1)}, f32[2,32,8,256]{3,2,1,0:T(8,128)}, u32[]{:S(2)}) copy-start(f32[2,32,8,256]{3,2,1,0:T(8,128)} %param.24) | copy-start | bytes 1572868
  42.5 9.8 %collective-permute-start.5 = (f32[3,32,8,1]{3,2,1,0:T(8,128)S(1)}, f32[3,32,8,1]{3,2,1,0:T(8,128)S(1)}, u32[]{:S(2)}, u32[]{:S(2)}) collective-permute-start(f32[3,32,8,1]{3,2,1,0:T(8,128)S(1)} %slice.437), channel_id=1, source_target_pairs={{1,0},{2,1},{3,2},{5,4},{6,5},{7,6},{9,8},{10,9},{11,10},{13,12},{... | collective-permute-start | bytes 9224 | tf_op jit(solution)/shard_map/ppermute | solution.py:24
  43.9 8.4 %collective-permute-start.4 = (f32[3,1,8,256]{3,2,1,0:T(8,128)S(1)}, f32[3,1,8,256]{3,2,1,0:T(8,128)S(1)}, u32[]{:S(2)}, u32[]{:S(2)}) collective-permute-start(f32[3,1,8,256]{3,2,1,0:T(8,128)S(1)} %slice.434), channel_id=1, source_target_pairs={{4,0},{8,4},{12,8},{16,12},{20,16},{24,20},{28,24},{32,28},{36,32}... | collective-permute-start | bytes 73736 | tf_op jit(solution)/shard_map/ppermute | solution.py:24
  53.0 9.7 %collective-permute-start.7 = (f32[3,32,8,1]{3,2,1,0:T(8,128)S(1)}, f32[3,32,8,1]{3,2,1,0:T(8,128)S(1)}, u32[]{:S(2)}, u32[]{:S(2)}) collective-permute-start(f32[3,32,8,1]{3,2,1,0:T(8,128)S(1)} %slice.447), channel_id=1, source_target_pairs={{0,1},{1,2},{2,3},{4,5},{5,6},{6,7},{8,9},{9,10},{10,11},{12,13},{... | collective-permute-start | bytes 9224 | tf_op jit(solution)/shard_map/ppermute | solution.py:24
  55.0 15.4 %collective-permute-start.6 = (f32[3,1,8,256]{3,2,1,0:T(8,128)S(1)}, f32[3,1,8,256]{3,2,1,0:T(8,128)S(1)}, u32[]{:S(2)}, u32[]{:S(2)}) collective-permute-start(f32[3,1,8,256]{3,2,1,0:T(8,128)S(1)} %slice.444), channel_id=1, source_target_pairs={{0,4},{4,8},{8,12},{12,16},{16,20},{20,24},{24,28},{28,32},{32,36}... | collective-permute-start | bytes 73736 | tf_op jit(solution)/shard_map/ppermute | solution.py:24
  71.6 1.1 copy-start.16
  73.2 1.1 copy-start.6
  73.2 1.4 copy-start.17
  73.3 1.3 copy-start.21
  75.1 9.7 %collective-permute-start.9 = (f32[3,32,8,1]{3,2,1,0:T(8,128)S(1)}, f32[3,32,8,1]{3,2,1,0:T(8,128)S(1)}, u32[]{:S(2)}, u32[]{:S(2)}) collective-permute-start(f32[3,32,8,1]{3,2,1,0:T(8,128)S(1)} %slice.461), channel_id=1, source_target_pairs={{1,0},{2,1},{3,2},{5,4},{6,5},{7,6},{9,8},{10,9},{11,10},{13,12},{... | collective-permute-start | bytes 9224 | tf_op jit(solution)/shard_map/ppermute | solution.py:24
  76.4 8.4 %collective-permute-start.8 = (f32[3,1,8,256]{3,2,1,0:T(8,128)S(1)}, f32[3,1,8,256]{3,2,1,0:T(8,128)S(1)}, u32[]{:S(2)}, u32[]{:S(2)}) collective-permute-start(f32[3,1,8,256]{3,2,1,0:T(8,128)S(1)} %slice.458), channel_id=1, source_target_pairs={{4,0},{8,4},{12,8},{16,12},{20,16},{24,20},{28,24},{32,28},{36,32}... | collective-permute-start | bytes 73736 | tf_op jit(solution)/shard_map/ppermute | solution.py:24
  85.1 1.3 copy-start.2
  85.3 17.9 %copy-start.7 = (f32[1,32,8,256]{3,2,1,0:T(8,128)}, f32[1,32,8,256]{3,2,1,0:T(8,128)S(1)}, u32[]{:S(2)}) copy-start(f32[1,32,8,256]{3,2,1,0:T(8,128)S(1)} %get-tuple-element.59) | copy-start | bytes 786436
  85.3 17.9 %copy-start.9 = (f32[1,32,8,256]{3,2,1,0:T(8,128)}, f32[1,32,8,256]{3,2,1,0:T(8,128)S(1)}, u32[]{:S(2)}) copy-start(f32[1,32,8,256]{3,2,1,0:T(8,128)S(1)} %get-tuple-element.60) | copy-start | bytes 786436
  85.3 17.9 %copy-start.11 = (f32[1,32,8,256]{3,2,1,0:T(8,128)}, f32[1,32,8,256]{3,2,1,0:T(8,128)S(1)}, u32[]{:S(2)}) copy-start(f32[1,32,8,256]{3,2,1,0:T(8,128)S(1)} %get-tuple-element.61) | copy-start | bytes 786436
  86.7 8.9 %collective-permute-start.11 = (f32[3,32,8,1]{3,2,1,0:T(8,128)S(1)}, f32[3,32,8,1]{3,2,1,0:T(8,128)S(1)}, u32[]{:S(2)}, u32[]{:S(2)}) collective-permute-start(f32[3,32,8,1]{3,2,1,0:T(8,128)S(1)} %slice.471), channel_id=1, source_target_pairs={{0,1},{1,2},{2,3},{4,5},{5,6},{6,7},{8,9},{9,10},{10,11},{12,13},{... | collective-permute-start | bytes 9224 | tf_op jit(solution)/shard_map/ppermute | solution.py:24
  88.8 14.5 %collective-permute-start.10 = (f32[3,1,8,256]{3,2,1,0:T(8,128)S(1)}, f32[3,1,8,256]{3,2,1,0:T(8,128)S(1)}, u32[]{:S(2)}, u32[]{:S(2)}) collective-permute-start(f32[3,1,8,256]{3,2,1,0:T(8,128)S(1)} %slice.468), channel_id=1, source_target_pairs={{0,4},{4,8},{8,12},{12,16},{16,20},{20,24},{24,28},{28,32},{32,36}... | collective-permute-start | bytes 73736 | tf_op jit(solution)/shard_map/ppermute | solution.py:24
  107.4 88.0 %collective-permute-start.13 = (f32[3,32,8,1]{3,2,1,0:T(8,128)}, f32[3,32,8,1]{3,2,1,0:T(8,128)}, u32[]{:S(2)}, u32[]{:S(2)}) collective-permute-start(f32[3,32,8,1]{3,2,1,0:T(8,128)} %slice.483), channel_id=1, source_target_pairs={{1,0},{2,1},{3,2},{5,4},{6,5},{7,6},{9,8},{10,9},{11,10},{13,12},{... | collective-permute-start | bytes 9224 | tf_op jit(solution)/shard_map/ppermute | solution.py:24
  108.7 86.7 %collective-permute-start.12 = (f32[3,1,8,256]{3,2,1,0:T(8,128)S(1)}, f32[3,1,8,256]{3,2,1,0:T(8,128)S(1)}, u32[]{:S(2)}, u32[]{:S(2)}) collective-permute-start(f32[3,1,8,256]{3,2,1,0:T(8,128)S(1)} %slice.480), channel_id=1, source_target_pairs={{4,0},{8,4},{12,8},{16,12},{20,16},{24,20},{28,24},{32,28},{36,32}... | collective-permute-start | bytes 73736 | tf_op jit(solution)/shard_map/ppermute | solution.py:24
  196.7 1.1 copy-start.12
  198.0 15.9 %copy-start.1 = (f32[3,32,8,256]{3,2,1,0:T(8,128)}, f32[3,32,8,256]{3,2,1,0:T(8,128)S(1)}, u32[]{:S(2)}) copy-start(f32[3,32,8,256]{3,2,1,0:T(8,128)S(1)} %maximum_add_fusion.1) | copy-start | bytes 2359300
  198.1 10.7 %collective-permute-start.15 = (f32[3,32,8,1]{3,2,1,0:T(8,128)S(1)}, f32[3,32,8,1]{3,2,1,0:T(8,128)S(1)}, u32[]{:S(2)}, u32[]{:S(2)}) collective-permute-start(f32[3,32,8,1]{3,2,1,0:T(8,128)S(1)} %slice.493), channel_id=1, source_target_pairs={{0,1},{1,2},{2,3},{4,5},{5,6},{6,7},{8,9},{9,10},{10,11},{12,13},{... | collective-permute-start | bytes 9224 | tf_op jit(solution)/shard_map/ppermute | solution.py:24
  200.2 13.7 %collective-permute-start.14 = (f32[3,1,8,256]{3,2,1,0:T(8,128)S(1)}, f32[3,1,8,256]{3,2,1,0:T(8,128)S(1)}, u32[]{:S(2)}, u32[]{:S(2)}) collective-permute-start(f32[3,1,8,256]{3,2,1,0:T(8,128)S(1)} %slice.490), channel_id=1, source_target_pairs={{0,4},{4,8},{8,12},{12,16},{16,20},{20,24},{24,28},{28,32},{32,36}... | collective-permute-start | bytes 73736 | tf_op jit(solution)/shard_map/ppermute | solution.py:24
  (7 other events, 6.5 us)
where the time goes:
time: 217 us; the launch traced here: 216 us
  blocking collectives  76.3 us (35%)
  waiting for transfers between devices  56.5 us (26%)
  starting transfers between devices  43.4 us (20%)
  other arithmetic  23.4 us (11%)
  local copies, waits for them, and re-layouts  13.7 us (6%)
  between operations  2.27 us (1%)
    psum x1, blocking collectives, step_total(): return lax.psum(label_sums(material_labels, values, count), ('gy', 'gz'))  76.3 us
    ppermute x16, waiting for transfers between devices, shifted(): return lax.ppermute(block, axis, route)  56.5 us
    ppermute x16, starting transfers between devices, shifted(): return lax.ppermute(block, axis, route)  43.4 us
    unnamed x46, local copies, waits for them, and re-layouts  8.78 us
    add x1, other arithmetic, on_device(): step_total(material_labels, grad_second, count)  5.11 us
  transfers between devices with their start and end apart: 16, of which 9 were waited for; matrix products, arithmetic and copies ran while one was open for 7% of the time, Pallas kernels for 0%

commit v1 on v0

--- a/solution.py
+++ b/solution.py
@@ -21,7 +21,17 @@
 def shifted(block, axis, distance):
     devices = range(lax.axis_size(axis))
     route = [(i - distance, i) for i in devices if i - distance in devices]
-    return lax.ppermute(block, axis, route)
+    inner = [pair for pair in route if min(pair) % 2 == 0]
+    outer = [pair for pair in route if min(pair) % 2 == 1]
+    far = lax.ppermute(block, axis, outer)
+    near = lax.ppermute(block, axis, inner)
+    return far + near
+
+
+def shifted_column(column, distance):
+    shape = column.shape
+    moved = shifted(column.reshape(shape[0], -1), "gz", distance)
+    return moved.reshape(shape)
 
 
 def front(values, axis):
@@ -42,7 +52,7 @@
 
 def curl_forward(field):
     front_row = shifted(field[:, :1], "gy", -1)
-    front_column = shifted(field[:, :, :, :1], "gz", -1)
+    front_column = shifted_column(field[:, :, :, :1], -1)
     along_y = jnp.concatenate([field[:, 1:], front_row], 1) - field
     along_z = jnp.concatenate([field[:, :, :, 1:], front_column], 3) - field
     along_x = front(field, 2) - field
@@ -51,7 +61,7 @@
 
 def curl_backward(field):
     back_row = shifted(field[:, -1:], "gy", 1)
-    back_column = shifted(field[:, :, :, -1:], "gz", 1)
+    back_column = shifted_column(field[:, :, :, -1:], 1)
     along_y = field - jnp.concatenate([back_row, field[:, :-1]], 1)
     along_z = field - jnp.concatenate([back_column, field[:, :, :, :-1]], 3)
     along_x = field - behind(field, 2)
@@ -109,8 +119,11 @@
     )
 
 
-def step_total(material_labels, values, count):
-    return lax.psum(label_sums(material_labels, values, count), ("gy", "gz"))
+def everywhere_sum(values):
+    axes = ("gy", "gz")
+    devices = lax.axis_size("gy") * lax.axis_size("gz")
+    sent = jnp.broadcast_to(values[None, None], (devices, 1, values.shape[0]))
+    return jnp.sum(lax.all_to_all(sent, axes, 0, 0), axis=(0, 1))
 
 
 def on_device(
@@ -183,9 +196,7 @@
         * lax.axis_size("gy")
         * lax.axis_size("gz")
     )
-    totals = step_total(material_labels, grad_second, count) + step_total(
-        material_labels, grad_first, count
-    )
+    totals = everywhere_sum(label_sums(material_labels, cell_grad, count))
     table_grad = totals * (1.0 / math.sqrt(cells))
     return (efield_grad, hfield_grad, polar_grad, rate_grad, levels_grad, cell_grad, table_grad)
 

time: 217 us -> 225 us (1.037)
  the two profiles are of different devices: /device:TPU:2 before, /device:TPU:1 now
where the time goes in v1:
time: 225 us; the launch traced here: 222 us
  starting transfers between devices  110 us (49%)
  other arithmetic  55.8 us (25%)
  local copies, waits for them, and re-layouts  46.3 us (21%)
  waiting for transfers between devices  7.91 us (4%)
  between operations  2.65 us (1%)
    ppermute x16, starting transfers between devices, shifted(): near = lax.ppermute(block, axis, inner)  52.2 us
    ppermute x16, starting transfers between devices, shifted(): far = lax.ppermute(block, axis, outer)  36.2 us
    all_to_all x1, starting transfers between devices, everywhere_sum(): return jnp.sum(lax.all_to_all(sent, axes, 0, 0), axis=(0, 1))  21.1 us
    unnamed x128, local copies, waits for them, and re-layouts  16.1 us
    sub x4, other arithmetic, curl_backward(): along_z = field - jnp.concatenate([back_column, field[:, :, :, :-1]], 3)  7.43 us
    reshape x8, local copies, waits for them, and re-layouts, shifted_column(): return moved.reshape(shape)  6.73 us
    sub x4, other arithmetic, curl_forward(): along_z = jnp.concatenate([field[:, :, :, 1:], front_column], 3) - field  6.61 us
    all_to_all x1, waiting for transfers between devices, everywhere_sum(): return jnp.sum(lax.all_to_all(sent, axes, 0, 0), axis=(0, 1))  6.24 us
  transfers between devices with their start and end apart: 33, of which 2 were waited for; matrix products, arithmetic and copies ran while one was open for 23% of the time, Pallas kernels for 0%

profile of v1, /device:TPU:1, one launch (start us, length us, event | category | flops | bytes accessed | tf_op | source)
XLA Modules:
  0.0 222.1 jit_solution(6320165887700405740)
XLA Ops:
  5.3 4.5 %collective-permute-start.1 = (f32[3,1,8,256]{3,2,1,0:T(8,128)S(1)}, f32[3,1,8,256]{3,2,1,0:T(8,128)S(1)}, u32[]{:S(2)}, u32[]{:S(2)}) collective-permute-start(f32[3,1,8,256]{3,2,1,0:T(8,128)S(1)} %slice.410), channel_id=1, source_target_pairs={{4,0},{12,8},{20,16},{28,24},{36,32},{44,40},{52,48},{60,56},{68,6... | collective-permute-start | bytes 73736 | tf_op jit(solution)/shard_map/ppermute | solution.py:27
  13.5 1.6 collective-permute-done
  18.1 6.2 %collective-permute-start.4 = (f32[3,1,8,256]{3,2,1,0:T(8,128)}, f32[3,1,8,256]{3,2,1,0:T(8,128)}, u32[]{:S(2)}, u32[]{:S(2)}) collective-permute-start(f32[3,1,8,256]{3,2,1,0:T(8,128)} %slice.420), channel_id=1, source_target_pairs={{4,8},{12,16},{20,24},{28,32},{36,40},{44,48},{52,56},{60,64},{68,... | collective-permute-start | bytes 73736 | tf_op jit(solution)/shard_map/ppermute | solution.py:26
  26.6 6.9 %collective-permute-start.7 = (f32[3,256]{1,0:T(4,128)S(1)}, f32[3,256]{1,0:T(4,128)S(1)}, u32[]{:S(2)}, u32[]{:S(2)}) collective-permute-start(f32[3,256]{1,0:T(4,128)S(1)} %reshape.95), channel_id=1, source_target_pairs={{0,1},{2,3},{4,5},{6,7},{8,9},{10,11},{12,13},{14,15},{16,17},{18,... | collective-permute-start | bytes 9224 | tf_op jit(solution)/shard_map/ppermute | solution.py:27
  33.5 4.6 %select_add_fusion.2 = (f32[32,8,256]{2,1,0:T(8,128)S(1)}, pred[32,8,256]{2,1,0:T(8,128)(4,1)}, pred[32,8,256]{2,1,0:T(8,128)(4,1)}, pred[32,8,256]{2,1,0:T(8,12...) fusion(f32[]{:T(128)} %bitcast.6, f32[]{:T(128)} %bitcast.5, f32[]{:T(128)} %bitcast.4, f32[]{:T(128)} %bitcast.3, ...), kind=kLoop, calls=%fused_computation.122 | loop fusion | flops 983040 | bytes 1835024 | tf_op jit(solution)/shard_map/add | solution.py:107
  40.8 1.5 maximum_subtract_fusion.1
  47.7 4.8 %collective-permute-start.9 = (f32[3,1,8,256]{3,2,1,0:T(8,128)}, f32[3,1,8,256]{3,2,1,0:T(8,128)}, u32[]{:S(2)}, u32[]{:S(2)}) collective-permute-start(f32[3,1,8,256]{3,2,1,0:T(8,128)} %slice.434), channel_id=1, source_target_pairs={{4,0},{12,8},{20,16},{28,24},{36,32},{44,40},{52,48},{60,56},{68,6... | collective-permute-start | bytes 73736 | tf_op jit(solution)/shard_map/ppermute | solution.py:27
  59.9 1.7 maximum_subtract_fusion.3
  63.8 9.0 %collective-permute-start.12 = (f32[3,1,8,256]{3,2,1,0:T(8,128)}, f32[3,1,8,256]{3,2,1,0:T(8,128)}, u32[]{:S(2)}, u32[]{:S(2)}) collective-permute-start(f32[3,1,8,256]{3,2,1,0:T(8,128)} %slice.444), channel_id=1, source_target_pairs={{4,8},{12,16},{20,24},{28,32},{36,40},{44,48},{52,56},{60,64},{68,... | collective-permute-start | bytes 73736 | tf_op jit(solution)/shard_map/ppermute | solution.py:26
  76.5 5.2 %collective-permute-start.15 = (f32[3,256]{1,0:T(4,128)S(1)}, f32[3,256]{1,0:T(4,128)S(1)}, u32[]{:S(2)}, u32[]{:S(2)}) collective-permute-start(f32[3,256]{1,0:T(4,128)S(1)} %reshape.99), channel_id=1, source_target_pairs={{0,1},{2,3},{4,5},{6,7},{8,9},{10,11},{12,13},{14,15},{16,17},{18,... | collective-permute-start | bytes 9224 | tf_op jit(solution)/shard_map/ppermute | solution.py:27
  81.8 2.3 %bitcast_multiply_fusion.1 = (f32[32,8,256]{2,1,0:T(8,128)}, f32[32,8,256]{2,1,0:T(8,128)}) fusion(s32[32,8,256]{2,1,0:T(8,128)} %param.26, f32[2,32,8,256]{3,2,1,0:T(8,128)} %param.24, f32[32,8,256]{2,1,0:T(8,128)} %get-tuple-element.20, f32[2,32,8,256]{3,2,1,0:T(8,128)} %convert_element_type.25), kind=kLoop, calls=%fused_computation.108 | loop fusion | flops 1441792 | bytes 2097152 | tf_op jit(solution)/shard_map/transpose(jvp())/mul | solution.py:83
  86.9 2.1 maximum_subtract_fusion.5
  95.2 2.0 multiply_reduce_fusion.2
  99.1 4.7 %collective-permute-start.17 = (f32[3,1,8,256]{3,2,1,0:T(8,128)}, f32[3,1,8,256]{3,2,1,0:T(8,128)}, u32[]{:S(2)}, u32[]{:S(2)}) collective-permute-start(f32[3,1,8,256]{3,2,1,0:T(8,128)} %slice.458), channel_id=1, source_target_pairs={{4,0},{12,8},{20,16},{28,24},{36,32},{44,40},{52,48},{60,56},{68,6... | collective-permute-start | bytes 73736 | tf_op jit(solution)/shard_map/ppermute | solution.py:27
  109.5 1.4 pad_add_fusion.1
  116.9 2.0 maximum_subtract_fusion.7
  121.0 7.1 %collective-permute-start.20 = (f32[3,1,8,256]{3,2,1,0:T(8,128)}, f32[3,1,8,256]{3,2,1,0:T(8,128)}, u32[]{:S(2)}, u32[]{:S(2)}) collective-permute-start(f32[3,1,8,256]{3,2,1,0:T(8,128)} %slice.468), channel_id=1, source_target_pairs={{4,8},{12,16},{20,24},{28,32},{36,40},{44,48},{52,56},{60,64},{68,... | collective-permute-start | bytes 73736 | tf_op jit(solution)/shard_map/ppermute | solution.py:26
  132.0 6.2 %collective-permute-start.23 = (f32[3,256]{1,0:T(4,128)S(1)}, f32[3,256]{1,0:T(4,128)S(1)}, u32[]{:S(2)}, u32[]{:S(2)}) collective-permute-start(f32[3,256]{1,0:T(4,128)S(1)} %reshape.103), channel_id=1, source_target_pairs={{0,1},{2,3},{4,5},{6,7},{8,9},{10,11},{12,13},{14,15},{16,17},{18,... | collective-permute-start | bytes 9224 | tf_op jit(solution)/shard_map/ppermute | solution.py:27
  138.2 1.9 bitcast_multiply_fusion
  142.8 2.0 maximum_subtract_fusion.9
  150.1 1.6 multiply_add_fusion
  152.3 1.4 collective-permute-start.24
  153.7 4.8 %collective-permute-start.25 = (f32[3,1,8,256]{3,2,1,0:T(8,128)}, f32[3,1,8,256]{3,2,1,0:T(8,128)}, u32[]{:S(2)}, u32[]{:S(2)}) collective-permute-start(f32[3,1,8,256]{3,2,1,0:T(8,128)} %slice.480), channel_id=1, source_target_pairs={{4,0},{12,8},{20,16},{28,24},{36,32},{44,40},{52,48},{60,56},{68,6... | collective-permute-start | bytes 73736 | tf_op jit(solution)/shard_map/ppermute | solution.py:27
  160.8 2.4 %select_reduce_fusion.3 = (f32[]{:T(128)}, f32[]{:T(128)}, f32[]{:T(128)}, f32[]{:T(128)}, f32[32,8,256]{2,1,0:T(8,128)}) fusion(pred[32,8,256]{2,1,0:T(8,128)(4,1)} %get-tuple-element.23, pred[32,8,256]{2,1,0:T(8,128)(4,1)} %get-tuple-element.26, pred[32,8,256]{2,1,0:T(8,128)(4,1)} %get-tuple-element.25, pred[32,8,256]{2,1,0:T(8,128)(4,1)} %get-tuple-element.24, ...), kind=kLoop, calls=%fused_computation.112 | loop fusion | flops 589820 | bytes 1048592 | tf_op jit(solution)/shard_map/reduce_sum | solution.py:116
  163.2 2.6 %pad_maximum_fusion.2 = f32[4]{0:T(128)S(1)} fusion(f32[1]{0:T(128)} %bitcast.19, f32[1]{0:T(128)} %bitcast.18, f32[1]{0:T(128)} %bitcast.17, f32[1]{0:T(128)} %bitcast.16), kind=kLoop, calls=%fused_computation.136 | loop fusion | flops 12 | bytes 32 | tf_op jit(solution)/shard_map/stack | solution.py:114
  166.5 21.1 %all-to-all-start = ((f32[256,1,4]{2,1,0:T(1,128)}), f32[256,1,4]{2,1,0:T(1,128)S(1)}, u32[]{:S(2)}, u32[]{:S(2)}) async-start(f32[256,1,4]{2,1,0:T(1,128)} %broadcast_in_dim.85), calls=%async_computation | async-start | bytes 262144 | tf_op jit(solution)/shard_map/all_to_all | solution.py:126
  188.9 3.0 %pad_add_fusion = f32[2,32,8,256]{3,2,1,0:T(8,128)} fusion(f32[1,32,8,256]{3,2,1,0:T(8,128)S(1)} %get-tuple-element.82, f32[1,32,8,256]{3,2,1,0:T(8,128)S(1)} %get-tuple-element.81, f32[1,32,8,256]{3,2,1,0:T(8,128)} %get-tuple-element.79, f32[1,32,8,256]{3,2,1,0:T(8,128)} %get-tuple-element.78, f32[1,32,8,256]{3,2,1,0:T(8,128)} %get-tuple-element.80, ...), kind=kLoop, calls=%fused_computation.64 | loop fusion | flops 2359296 | bytes 4718594 | tf_op jit(solution)/shard_map/transpose(jvp())/add_any | solution.py:77
  194.3 6.2 %all-to-all-done = f32[256,1,4]{2,1,0:T(1,128)S(1)} async-done(((f32[256,1,4]{2,1,0:T(1,128)}), f32[256,1,4]{2,1,0:T(1,128)S(1)}, u32[]{:S(2)}, u32[]{:S(2)}) %all-to-all-start) | async-done | bytes 4128 | tf_op jit(solution)/shard_map/all_to_all | solution.py:126
  201.6 1.6 maximum_subtract_fusion.11
  205.0 3.3 %collective-permute-start.28 = (f32[3,1,8,256]{3,2,1,0:T(8,128)S(1)}, f32[3,1,8,256]{3,2,1,0:T(8,128)S(1)}, u32[]{:S(2)}, u32[]{:S(2)}) collective-permute-start(f32[3,1,8,256]{3,2,1,0:T(8,128)S(1)} %slice.490), channel_id=1, source_target_pairs={{4,8},{12,16},{20,24},{28,32},{36,40},{44,48},{52,56},{60,64},{68,... | collective-permute-start | bytes 73736 | tf_op jit(solution)/shard_map/ppermute | solution.py:26
  210.7 4.9 %collective-permute-start.31 = (f32[3,256]{1,0:T(4,128)S(1)}, f32[3,256]{1,0:T(4,128)S(1)}, u32[]{:S(2)}, u32[]{:S(2)}) collective-permute-start(f32[3,256]{1,0:T(4,128)S(1)} %reshape.107), channel_id=1, source_target_pairs={{0,1},{2,3},{4,5},{6,7},{8,9},{10,11},{12,13},{14,15},{16,17},{18,... | collective-permute-start | bytes 9224 | tf_op jit(solution)/shard_map/ppermute | solution.py:27
  218.1 1.8 maximum_subtract_fusion.13
  (280 shorter events, 87.2 us)
Async XLA Ops:
  2.0 10.4 %collective-permute-start.2 = (f32[3,256]{1,0:T(4,128)S(1)}, f32[3,256]{1,0:T(4,128)S(1)}, u32[]{:S(2)}, u32[]{:S(2)}) collective-permute-start(f32[3,256]{1,0:T(4,128)S(1)} %reshape.93), channel_id=1, source_target_pairs={{2,1},{6,5},{10,9},{14,13},{18,17},{22,21},{26,25},{30,29},{34,33}... | collective-permute-start | bytes 9224 | tf_op jit(solution)/shard_map/ppermute | solution.py:26
  2.7 9.8 %collective-permute-start.3 = (f32[3,256]{1,0:T(4,128)S(1)}, f32[3,256]{1,0:T(4,128)S(1)}, u32[]{:S(2)}, u32[]{:S(2)}) collective-permute-start(f32[3,256]{1,0:T(4,128)S(1)} %reshape.93), channel_id=1, source_target_pairs={{1,0},{3,2},{5,4},{7,6},{9,8},{11,10},{13,12},{15,14},{17,16},{19,... | collective-permute-start | bytes 9224 | tf_op jit(solution)/shard_map/ppermute | solution.py:27
  4.0 11.1 %collective-permute-start = (f32[3,1,8,256]{3,2,1,0:T(8,128)S(1)}, f32[3,1,8,256]{3,2,1,0:T(8,128)S(1)}, u32[]{:S(2)}, u32[]{:S(2)}) collective-permute-start(f32[3,1,8,256]{3,2,1,0:T(8,128)S(1)} %slice.410), channel_id=1, source_target_pairs={{8,4},{16,12},{24,20},{32,28},{40,36},{48,44},{56,52},{64,60},{72,... | collective-permute-start | bytes 73736 | tf_op jit(solution)/shard_map/ppermute | solution.py:26
  5.3 9.8 %collective-permute-start.1 = (f32[3,1,8,256]{3,2,1,0:T(8,128)S(1)}, f32[3,1,8,256]{3,2,1,0:T(8,128)S(1)}, u32[]{:S(2)}, u32[]{:S(2)}) collective-permute-start(f32[3,1,8,256]{3,2,1,0:T(8,128)S(1)} %slice.410), channel_id=1, source_target_pairs={{4,0},{12,8},{20,16},{28,24},{36,32},{44,40},{52,48},{60,56},{68,6... | collective-permute-start | bytes 73736 | tf_op jit(solution)/shard_map/ppermute | solution.py:27
  18.1 21.9 %collective-permute-start.4 = (f32[3,1,8,256]{3,2,1,0:T(8,128)}, f32[3,1,8,256]{3,2,1,0:T(8,128)}, u32[]{:S(2)}, u32[]{:S(2)}) collective-permute-start(f32[3,1,8,256]{3,2,1,0:T(8,128)} %slice.420), channel_id=1, source_target_pairs={{4,8},{12,16},{20,24},{28,32},{36,40},{44,48},{52,56},{60,64},{68,... | collective-permute-start | bytes 73736 | tf_op jit(solution)/shard_map/ppermute | solution.py:26
  24.2 15.8 %collective-permute-start.5 = (f32[3,1,8,256]{3,2,1,0:T(8,128)}, f32[3,1,8,256]{3,2,1,0:T(8,128)}, u32[]{:S(2)}, u32[]{:S(2)}) collective-permute-start(f32[3,1,8,256]{3,2,1,0:T(8,128)} %slice.420), channel_id=1, source_target_pairs={{0,4},{8,12},{16,20},{24,28},{32,36},{40,44},{48,52},{56,60},{64,6... | collective-permute-start | bytes 73736 | tf_op jit(solution)/shard_map/ppermute | solution.py:27
  25.9 13.8 %collective-permute-start.6 = (f32[3,256]{1,0:T(4,128)S(1)}, f32[3,256]{1,0:T(4,128)S(1)}, u32[]{:S(2)}, u32[]{:S(2)}) collective-permute-start(f32[3,256]{1,0:T(4,128)S(1)} %reshape.95), channel_id=1, source_target_pairs={{1,2},{5,6},{9,10},{13,14},{17,18},{21,22},{25,26},{29,30},{33,34}... | collective-permute-start | bytes 9224 | tf_op jit(solution)/shard_map/ppermute | solution.py:26
  26.6 13.1 %collective-permute-start.7 = (f32[3,256]{1,0:T(4,128)S(1)}, f32[3,256]{1,0:T(4,128)S(1)}, u32[]{:S(2)}, u32[]{:S(2)}) collective-permute-start(f32[3,256]{1,0:T(4,128)S(1)} %reshape.95), channel_id=1, source_target_pairs={{0,1},{2,3},{4,5},{6,7},{8,9},{10,11},{12,13},{14,15},{16,17},{18,... | collective-permute-start | bytes 9224 | tf_op jit(solution)/shard_map/ppermute | solution.py:27
  46.4 12.7 %collective-permute-start.8 = (f32[3,1,8,256]{3,2,1,0:T(8,128)}, f32[3,1,8,256]{3,2,1,0:T(8,128)}, u32[]{:S(2)}, u32[]{:S(2)}) collective-permute-start(f32[3,1,8,256]{3,2,1,0:T(8,128)} %slice.434), channel_id=1, source_target_pairs={{8,4},{16,12},{24,20},{32,28},{40,36},{48,44},{56,52},{64,60},{72,... | collective-permute-start | bytes 73736 | tf_op jit(solution)/shard_map/ppermute | solution.py:26
  47.7 11.4 %collective-permute-start.9 = (f32[3,1,8,256]{3,2,1,0:T(8,128)}, f32[3,1,8,256]{3,2,1,0:T(8,128)}, u32[]{:S(2)}, u32[]{:S(2)}) collective-permute-start(f32[3,1,8,256]{3,2,1,0:T(8,128)} %slice.434), channel_id=1, source_target_pairs={{4,0},{12,8},{20,16},{28,24},{36,32},{44,40},{52,48},{60,56},{68,6... | collective-permute-start | bytes 73736 | tf_op jit(solution)/shard_map/ppermute | solution.py:27
  52.7 5.3 %collective-permute-start.10 = (f32[3,256]{1,0:T(4,128)S(1)}, f32[3,256]{1,0:T(4,128)S(1)}, u32[]{:S(2)}, u32[]{:S(2)}) collective-permute-start(f32[3,256]{1,0:T(4,128)S(1)} %reshape.97), channel_id=1, source_target_pairs={{2,1},{6,5},{10,9},{14,13},{18,17},{22,21},{26,25},{30,29},{34,33}... | collective-permute-start | bytes 9224 | tf_op jit(solution)/shard_map/ppermute | solution.py:26
  63.8 22.3 %collective-permute-start.12 = (f32[3,1,8,256]{3,2,1,0:T(8,128)}, f32[3,1,8,256]{3,2,1,0:T(8,128)}, u32[]{:S(2)}, u32[]{:S(2)}) collective-permute-start(f32[3,1,8,256]{3,2,1,0:T(8,128)} %slice.444), channel_id=1, source_target_pairs={{4,8},{12,16},{20,24},{28,32},{36,40},{44,48},{52,56},{60,64},{68,... | collective-permute-start | bytes 73736 | tf_op jit(solution)/shard_map/ppermute | solution.py:26
  72.8 13.3 %collective-permute-start.13 = (f32[3,1,8,256]{3,2,1,0:T(8,128)}, f32[3,1,8,256]{3,2,1,0:T(8,128)}, u32[]{:S(2)}, u32[]{:S(2)}) collective-permute-start(f32[3,1,8,256]{3,2,1,0:T(8,128)} %slice.444), channel_id=1, source_target_pairs={{0,4},{8,12},{16,20},{24,28},{32,36},{40,44},{48,52},{56,60},{64,6... | collective-permute-start | bytes 73736 | tf_op jit(solution)/shard_map/ppermute | solution.py:27
  75.9 9.2 %collective-permute-start.14 = (f32[3,256]{1,0:T(4,128)S(1)}, f32[3,256]{1,0:T(4,128)S(1)}, u32[]{:S(2)}, u32[]{:S(2)}) collective-permute-start(f32[3,256]{1,0:T(4,128)S(1)} %reshape.99), channel_id=1, source_target_pairs={{1,2},{5,6},{9,10},{13,14},{17,18},{21,22},{25,26},{29,30},{33,34}... | collective-permute-start | bytes 9224 | tf_op jit(solution)/shard_map/ppermute | solution.py:26
  76.5 8.5 %collective-permute-start.15 = (f32[3,256]{1,0:T(4,128)S(1)}, f32[3,256]{1,0:T(4,128)S(1)}, u32[]{:S(2)}, u32[]{:S(2)}) collective-permute-start(f32[3,256]{1,0:T(4,128)S(1)} %reshape.99), channel_id=1, source_target_pairs={{0,1},{2,3},{4,5},{6,7},{8,9},{10,11},{12,13},{14,15},{16,17},{18,... | collective-permute-start | bytes 9224 | tf_op jit(solution)/shard_map/ppermute | solution.py:27
  97.8 18.3 %collective-permute-start.16 = (f32[3,1,8,256]{3,2,1,0:T(8,128)}, f32[3,1,8,256]{3,2,1,0:T(8,128)}, u32[]{:S(2)}, u32[]{:S(2)}) collective-permute-start(f32[3,1,8,256]{3,2,1,0:T(8,128)} %slice.458), channel_id=1, source_target_pairs={{8,4},{16,12},{24,20},{32,28},{40,36},{48,44},{56,52},{64,60},{72,... | collective-permute-start | bytes 73736 | tf_op jit(solution)/shard_map/ppermute | solution.py:26
  99.1 17.1 %collective-permute-start.17 = (f32[3,1,8,256]{3,2,1,0:T(8,128)}, f32[3,1,8,256]{3,2,1,0:T(8,128)}, u32[]{:S(2)}, u32[]{:S(2)}) collective-permute-start(f32[3,1,8,256]{3,2,1,0:T(8,128)} %slice.458), channel_id=1, source_target_pairs={{4,0},{12,8},{20,16},{28,24},{36,32},{44,40},{52,48},{60,56},{68,6... | collective-permute-start | bytes 73736 | tf_op jit(solution)/shard_map/ppermute | solution.py:27
  105.5 9.6 %collective-permute-start.18 = (f32[3,256]{1,0:T(4,128)S(1)}, f32[3,256]{1,0:T(4,128)S(1)}, u32[]{:S(2)}, u32[]{:S(2)}) collective-permute-start(f32[3,256]{1,0:T(4,128)S(1)} %reshape.101), channel_id=1, source_target_pairs={{2,1},{6,5},{10,9},{14,13},{18,17},{22,21},{26,25},{30,29},{34,33}... | collective-permute-start | bytes 9224 | tf_op jit(solution)/shard_map/ppermute | solution.py:26
  106.2 8.9 %collective-permute-start.19 = (f32[3,256]{1,0:T(4,128)S(1)}, f32[3,256]{1,0:T(4,128)S(1)}, u32[]{:S(2)}, u32[]{:S(2)}) collective-permute-start(f32[3,256]{1,0:T(4,128)S(1)} %reshape.101), channel_id=1, source_target_pairs={{1,0},{3,2},{5,4},{7,6},{9,8},{11,10},{13,12},{15,14},{17,16},{19,... | collective-permute-start | bytes 9224 | tf_op jit(solution)/shard_map/ppermute | solution.py:27
  121.0 21.0 %collective-permute-start.20 = (f32[3,1,8,256]{3,2,1,0:T(8,128)}, f32[3,1,8,256]{3,2,1,0:T(8,128)}, u32[]{:S(2)}, u32[]{:S(2)}) collective-permute-start(f32[3,1,8,256]{3,2,1,0:T(8,128)} %slice.468), channel_id=1, source_target_pairs={{4,8},{12,16},{20,24},{28,32},{36,40},{44,48},{52,56},{60,64},{68,... | collective-permute-start | bytes 73736 | tf_op jit(solution)/shard_map/ppermute | solution.py:26
  128.1 14.0 %collective-permute-start.21 = (f32[3,1,8,256]{3,2,1,0:T(8,128)}, f32[3,1,8,256]{3,2,1,0:T(8,128)}, u32[]{:S(2)}, u32[]{:S(2)}) collective-permute-start(f32[3,1,8,256]{3,2,1,0:T(8,128)} %slice.468), channel_id=1, source_target_pairs={{0,4},{8,12},{16,20},{24,28},{32,36},{40,44},{48,52},{56,60},{64,6... | collective-permute-start | bytes 73736 | tf_op jit(solution)/shard_map/ppermute | solution.py:27
  131.2 9.8 %collective-permute-start.22 = (f32[3,256]{1,0:T(4,128)S(1)}, f32[3,256]{1,0:T(4,128)S(1)}, u32[]{:S(2)}, u32[]{:S(2)}) collective-permute-start(f32[3,256]{1,0:T(4,128)S(1)} %reshape.103), channel_id=1, source_target_pairs={{1,2},{5,6},{9,10},{13,14},{17,18},{21,22},{25,26},{29,30},{33,34}... | collective-permute-start | bytes 9224 | tf_op jit(solution)/shard_map/ppermute | solution.py:26
  132.0 9.0 %collective-permute-start.23 = (f32[3,256]{1,0:T(4,128)S(1)}, f32[3,256]{1,0:T(4,128)S(1)}, u32[]{:S(2)}, u32[]{:S(2)}) collective-permute-start(f32[3,256]{1,0:T(4,128)S(1)} %reshape.103), channel_id=1, source_target_pairs={{0,1},{2,3},{4,5},{6,7},{8,9},{10,11},{12,13},{14,15},{16,17},{18,... | collective-permute-start | bytes 9224 | tf_op jit(solution)/shard_map/ppermute | solution.py:27
  152.3 48.5 %collective-permute-start.24 = (f32[3,1,8,256]{3,2,1,0:T(8,128)}, f32[3,1,8,256]{3,2,1,0:T(8,128)}, u32[]{:S(2)}, u32[]{:S(2)}) collective-permute-start(f32[3,1,8,256]{3,2,1,0:T(8,128)} %slice.480), channel_id=1, source_target_pairs={{8,4},{16,12},{24,20},{32,28},{40,36},{48,44},{56,52},{64,60},{72,... | collective-permute-start | bytes 73736 | tf_op jit(solution)/shard_map/ppermute | solution.py:26
  153.7 47.1 %collective-permute-start.25 = (f32[3,1,8,256]{3,2,1,0:T(8,128)}, f32[3,1,8,256]{3,2,1,0:T(8,128)}, u32[]{:S(2)}, u32[]{:S(2)}) collective-permute-start(f32[3,1,8,256]{3,2,1,0:T(8,128)} %slice.480), channel_id=1, source_target_pairs={{4,0},{12,8},{20,16},{28,24},{36,32},{44,40},{52,48},{60,56},{68,6... | collective-permute-start | bytes 73736 | tf_op jit(solution)/shard_map/ppermute | solution.py:27
  158.8 35.2 %collective-permute-start.26 = (f32[3,256]{1,0:T(4,128)S(1)}, f32[3,256]{1,0:T(4,128)S(1)}, u32[]{:S(2)}, u32[]{:S(2)}) collective-permute-start(f32[3,256]{1,0:T(4,128)S(1)} %reshape.105), channel_id=1, source_target_pairs={{2,1},{6,5},{10,9},{14,13},{18,17},{22,21},{26,25},{30,29},{34,33}... | collective-permute-start | bytes 9224 | tf_op jit(solution)/shard_map/ppermute | solution.py:26
  159.4 34.6 %collective-permute-start.27 = (f32[3,256]{1,0:T(4,128)S(1)}, f32[3,256]{1,0:T(4,128)S(1)}, u32[]{:S(2)}, u32[]{:S(2)}) collective-permute-start(f32[3,256]{1,0:T(4,128)S(1)} %reshape.105), channel_id=1, source_target_pairs={{1,0},{3,2},{5,4},{7,6},{9,8},{11,10},{13,12},{15,14},{17,16},{19,... | collective-permute-start | bytes 9224 | tf_op jit(solution)/shard_map/ppermute | solution.py:27
  166.5 34.0 %all-to-all-start = ((f32[256,1,4]{2,1,0:T(1,128)}), f32[256,1,4]{2,1,0:T(1,128)S(1)}, u32[]{:S(2)}, u32[]{:S(2)}) async-start(f32[256,1,4]{2,1,0:T(1,128)} %broadcast_in_dim.85), calls=%async_computation | async-start | bytes 262144 | tf_op jit(solution)/shard_map/all_to_all | solution.py:126
  205.0 13.1 %collective-permute-start.28 = (f32[3,1,8,256]{3,2,1,0:T(8,128)S(1)}, f32[3,1,8,256]{3,2,1,0:T(8,128)S(1)}, u32[]{:S(2)}, u32[]{:S(2)}) collective-permute-start(f32[3,1,8,256]{3,2,1,0:T(8,128)S(1)} %slice.490), channel_id=1, source_target_pairs={{4,8},{12,16},{20,24},{28,32},{36,40},{44,48},{52,56},{60,64},{68,... | collective-permute-start | bytes 73736 | tf_op jit(solution)/shard_map/ppermute | solution.py:26
  208.3 9.8 %collective-permute-start.29 = (f32[3,1,8,256]{3,2,1,0:T(8,128)S(1)}, f32[3,1,8,256]{3,2,1,0:T(8,128)S(1)}, u32[]{:S(2)}, u32[]{:S(2)}) collective-permute-start(f32[3,1,8,256]{3,2,1,0:T(8,128)S(1)} %slice.490), channel_id=1, source_target_pairs={{0,4},{8,12},{16,20},{24,28},{32,36},{40,44},{48,52},{56,60},{64,6... | collective-permute-start | bytes 73736 | tf_op jit(solution)/shard_map/ppermute | solution.py:27
  210.0 7.0 %collective-permute-start.30 = (f32[3,256]{1,0:T(4,128)S(1)}, f32[3,256]{1,0:T(4,128)S(1)}, u32[]{:S(2)}, u32[]{:S(2)}) collective-permute-start(f32[3,256]{1,0:T(4,128)S(1)} %reshape.107), channel_id=1, source_target_pairs={{1,2},{5,6},{9,10},{13,14},{17,18},{21,22},{25,26},{29,30},{33,34}... | collective-permute-start | bytes 9224 | tf_op jit(solution)/shard_map/ppermute | solution.py:26
  210.7 6.4 %collective-permute-start.31 = (f32[3,256]{1,0:T(4,128)S(1)}, f32[3,256]{1,0:T(4,128)S(1)}, u32[]{:S(2)}, u32[]{:S(2)}) collective-permute-start(f32[3,256]{1,0:T(4,128)S(1)} %reshape.107), channel_id=1, source_target_pairs={{0,1},{2,3},{4,5},{6,7},{8,9},{10,11},{12,13},{14,15},{16,17},{18,... | collective-permute-start | bytes 9224 | tf_op jit(solution)/shard_map/ppermute | solution.py:27
  (65 other events, 247.5 us)

commit v2 on v0

v2 whole, which is shorter than its diff:
```python
import math

import jax
import jax.numpy as jnp
import numpy as np
from jax import lax
from jax.experimental import pallas as pl
from jax.experimental.pallas import tpu as pltpu
from jax.sharding import PartitionSpec as P

SOURCE_OMEGA = 0.35
F32 = jnp.float32
BF16 = jnp.bfloat16
NAMES = ("E", "H", "P", "Q", "N", "lab", "gain", "src", "Es", "Ns", "Hs", "Ps", "Qs")
COUNT = dict(E=3, H=3, P=3, Q=3, N=2, lab=1, gain=1, src=1, Es=3, Ns=2, Hs=3, Ps=3, Qs=3)
WIDTH = dict(E=3, H=3, P=2, Q=2, N=2, lab=2, gain=2, src=2, Es=2, Ns=2, Hs=2, Ps=1, Qs=1)
HALF = ("E", "H", "P", "Q", "N")
COMPS = [(name, c) for name in NAMES for c in range(COUNT[name])]
INDEX = {comp: i for i, comp in enumerate(COMPS)}
SPOT, PLANE, IS_FRONT = {}, {}, np.zeros((1, 128), np.int32)
_lane, _plane = 0, 0
for _comp in COMPS:
    _w = WIDTH[_comp[0]]
    SPOT[_comp] = _lane + _w
    IS_FRONT[0, _lane + _w : _lane + 2 * _w] = 1
    PLANE[_comp] = _plane
    _lane += 2 * _w
    _plane += _w
PLANES = _plane
LANES = 384
EDGE = 9


def lane_of(shape):
    return lax.broadcasted_iota(jnp.int32, shape, 1)


def pull(ref, comp, index):
    name, c = comp
    if COUNT[name] == 1:
        value = ref[index].astype(F32)
        return value + 1.0 if name == "lab" else value
    return ref[c, index].astype(F32)


def take(ref, comp, start, count):
    if COUNT[comp[0]] == 1:
        return ref.at[pl.ds(start, count)]
    return ref.at[comp[1], pl.ds(start, count)]


def pack_rows(rows, *refs):
    given = dict(zip(NAMES, refs[: len(NAMES)]))
    messages = refs[len(NAMES) : len(NAMES) + 2]
    floats, ints, sems = refs[len(NAMES) + 2 :]
    even = lax.rem(lax.axis_index("gy"), 2) == 0
    started, later = [], []
    for side in range(2):
        last = even if side == 0 else jnp.logical_not(even)
        wide = ints_at = 0
        for comp in COMPS:
            w = WIDTH[comp[0]]
            start = jnp.where(last, rows - w, 0)
            source = take(given[comp[0]], comp, start, w)
            if comp[0] in HALF:
                target = messages[side].at[pl.ds(PLANE[comp], w)]
            elif comp[0] in ("lab", "gain"):
                target = ints.at[side, pl.ds(ints_at, w)]
                later.append((side, comp, ints, ints_at))
                ints_at += w
            else:
                target = floats.at[side, pl.ds(wide, w)]
                later.append((side, comp, floats, wide))
                wide += w
            copy = pltpu.make_async_copy(source, target, sems.at[side, INDEX[comp]])
            copy.start()
            started.append(copy)
    for copy in started:
        copy.wait()
    for side, comp, held, at in later:
        for k in range(WIDTH[comp[0]]):
            value = held[side, at + k].astype(F32)
            if comp[0] == "lab":
                value = value + 1.0
            messages[side][PLANE[comp] + k] = value.astype(BF16)


def pack_columns(*refs):
    given = dict(zip(NAMES, refs[: len(NAMES)]))
    first, second = refs[len(NAMES) :]
    even = lax.rem(lax.axis_index("gz"), 2) == 0
    lane = lane_of((8, 128))

    def row(y, carry):
        low = jnp.zeros((8, 128), F32)
        high = jnp.zeros((8, 128), F32)
        for comp in reversed(COMPS):
            value = pull(given[comp[0]], comp, y)
            inside = lane < SPOT[comp] + WIDTH[comp[0]]
            low = jnp.where(inside, pltpu.roll(value[:, :128], SPOT[comp], 1), low)
            high = jnp.where(inside, pltpu.roll(value[:, 128:], SPOT[comp], 1), high)
        first[y] = jnp.where(even, high, low).astype(BF16)
        second[y] = jnp.where(even, low, high).astype(BF16)
        return carry

    lax.fori_loop(0, first.shape[0], row, 0)


def curl_ahead(v, above):
    inside = lax.broadcasted_iota(jnp.int32, v[0].shape, 0) < 7
    size = v[0].shape[1]

    def dz(c):
        return pltpu.roll(v[c], size - 1, 1) - v[c]

    def dx(c):
        return jnp.where(inside, pltpu.roll(v[c], 7, 0), 0.0) - v[c]

    return [
        (above[2] - v[2]) - dz(1),
        dz(0) - dx(2),
        dx(1) - (above[0] - v[0]),
    ]


def curl_back(v, below):
    inside = lax.broadcasted_iota(jnp.int32, v[0].shape, 0) > 0

    def dz(c):
        return v[c] - pltpu.roll(v[c], 1, 1)

    def dx(c):
        return v[c] - jnp.where(inside, pltpu.roll(v[c], 1, 0), 0.0)

    return [
        (v[2] - below[2]) - dz(1),
        dz(0) - dx(2),
        dx(1) - (v[0] - below[0]),
    ]


SCRATCH = dict(M=3, E1=3, Q1=3, F1=3, Q2=3, aE=3, aC=3, bH=3, cC=3, cE=3, hg=3, inv=1, g2=1, k0=1, k1=1)


def six_stages(get, put, held, bases, count, table, push_first, push_second, keep_row, keep_lane):
    def load(name, row):
        return [held[name][c, row] for c in range(SCRATCH[name])]

    def store(name, row, values):
        for c, value in enumerate(values):
            held[name][c, row] = value

    def kept(values, row):
        return [value * (keep_lane * keep_row(row)) for value in values]

    def trio(name, row):
        return [get((name, c), row) for c in range(3)]

    def over(low, high, body):
        if len(bases) == 1:
            lax.fori_loop(low, high, lambda r, carry: (body(r), carry)[1], 0)
        else:
            span = high - low
            step = bases[1] - bases[0]

            def walk(i, carry):
                chunk = i // span
                body(chunk * step + (i - chunk * span) + low + bases[0])
                return carry

            lax.fori_loop(0, span * len(bases), walk, 0)

    def stage_one(r):
        above = {0: get(("E", 0), r + 1), 2: get(("E", 2), r + 1)}
        curl = curl_ahead(trio("E", r), above)
        store("M", r, kept([h - 0.5 * c for h, c in zip(trio("H", r), curl)], r))

    def stage_two(r):
        electric, polar, rate = trio("E", r), trio("P", r), trio("Q", r)
        upper, lower = get(("N", 0), r), get(("N", 1), r)
        label, gain, source = get(("lab", 0), r), get(("gain", 0), r), get(("src", 0), r)
        inverse = jnp.zeros_like(label)
        for m, value in enumerate(table):
            inverse = jnp.where(label == m + 1.0, value, inverse)
        g2, g4 = 0.2 * gain, 0.4 * gain
        k0 = g4 * (upper - lower)
        q1 = [0.9 * q - 0.3 * p + k0 * e for q, p, e in zip(rate, polar, electric)]
        p1 = [p + 0.5 * q for p, q in zip(polar, q1)]
        curl = curl_back(load("M", r), {0: held["M"][0, r - 1], 2: held["M"][2, r - 1]})
        f1 = [0.5 * (c - q) for c, q in zip(curl, q1)]
        f1[2] = f1[2] - push_first * source
        e1 = [e + inverse * f for e, f in zip(electric, f1)]
        s1 = g2 * sum(e * q for e, q in zip(e1, q1))
        up = upper + 0.5 * (0.05 * (1.0 - upper - lower) - 0.02 * upper)
        low = lower + 0.5 * (0.02 * upper - 0.3 * lower)
        k1 = g4 * (up - low - 2.0 * s1)
        q2 = [0.9 * q - 0.3 * p + k1 * e for q, p, e in zip(q1, p1, e1)]
        sb = g2 * (get(("Ns", 1), r) - get(("Ns", 0), r))
        a_e = [e + sb * q for e, q in zip(trio("Es", r), q2)]
        half = 0.5 * inverse
        store("E1", r, e1)
        store("Q1", r, q1)
        store("F1", r, f1)
        store("Q2", r, q2)
        store("aE", r, a_e)
        store("aC", r, [half * a for a in a_e])
        store("inv", r, [inverse])
        store("g2", r, [g2])
        store("k0", r, [k0])
        store("k1", r, [k1])

    def stage_three(r):
        e1 = curl_ahead(load("E1", r), {0: held["E1"][0, r + 1], 2: held["E1"][2, r + 1]})
        store("M", r, kept([m - 0.5 * c for m, c in zip(load("M", r), e1)], r))
        a_c = curl_ahead(load("aC", r), {0: held["aC"][0, r + 1], 2: held["aC"][2, r + 1]})
        store("bH", r, kept([h + c for h, c in zip(trio("Hs", r), a_c)], r))

    def stage_four(r):
        (inverse,), (g2,), (k0,), (k1,) = load("inv", r), load("g2", r), load("k0", r), load("k1", r)
        up, low = get(("Ns", 0), r), get(("Ns", 1), r)
        sb = g2 * (low - up)
        curl = curl_back(load("M", r), {0: held["M"][0, r - 1], 2: held["M"][2, r - 1]})
        q2, e1, a_e = load("Q2", r), load("E1", r), load("aE", r)
        f2 = [0.5 * (c - q) for c, q in zip(curl, q2)]
        f2[2] = f2[2] - push_second * get(("src", 0), r)
        e2 = [e + inverse * f for e, f in zip(e1, f2)]
        grad = sum(a * f for a, f in zip(a_e, f2))
        p_seed = trio("Ps", r)
        qt = [
            q + sb * e + 0.5 * (p - inverse * a)
            for q, e, p, a in zip(trio("Qs", r), e2, p_seed, a_e)
        ]
        a_p = [p - 0.3 * q for p, q in zip(p_seed, qt)]
        dn = 2.0 * g2 * sum(q * e for q, e in zip(qt, e1))
        a_up = 0.965 * up + 0.01 * low + dn
        a_low = 0.85 * low - 0.025 * up - dn
        curl = curl_back(load("bH", r), {0: held["bH"][0, r - 1], 2: held["bH"][2, r - 1]})
        sb = g2 * (a_low - a_up)
        q1 = load("Q1", r)
        c_e = [
            a + k1 * q - 0.5 * c + sb * p for a, q, c, p in zip(a_e, qt, curl, q1)
        ]
        half = 0.5 * inverse
        store("cC", r, [half * c for c in c_e])
        grad = grad + sum(c * f for c, f in zip(c_e, load("F1", r)))

        def own(value):
            return value[:, :256]

        inverse, g2, k0, sb = own(inverse), own(g2), own(k0), own(sb)
        q_out, e_out = [], []
        dn = 0.0
        for c in range(3):
            pt = own(a_p[c]) - inverse * own(c_e[c])
            q = 0.9 * own(qt[c]) + sb * own(e1[c]) + 0.5 * pt
            q_out.append(q)
            dn = dn + q * own(get(("E", c), r))
            held["cE"][c, r] = own(c_e[c]) + k0 * q
        dn = 2.0 * g2 * dn
        a_up, a_low = own(a_up), own(a_low)
        put("polar", r, [own(p) - 0.3 * q for p, q in zip(a_p, q_out)])
        put("rate", r, [0.9 * q for q in q_out])
        put("levels", r, [0.965 * a_up + 0.01 * a_low + dn, 0.85 * a_low - 0.025 * a_up - dn])
        put("cell", r, [own(grad)])

    def stage_five(r):
        curl = curl_ahead(load("cC", r), {0: held["cC"][0, r + 1], 2: held["cC"][2, r + 1]})
        hg = kept([h + c for h, c in zip(load("bH", r), curl)], r)
        store("hg", r, hg)

    def stage_six(r):
        hg = load("hg", r)
        curl = curl_back(hg, {0: held["hg"][0, r - 1], 2: held["hg"][2, r - 1]})
        put("h", r, [h[:, :256] for h in hg])
        put("e", r, [held["cE"][c, r] - 0.5 * curl[c][:, :256] for c in range(3)])

    over(0, count - 1, stage_one)
    over(1, count - 1, stage_two)
    over(1, count - 2, stage_three)
    over(2, count - 2, stage_four)
    over(2, count - 3, stage_five)
    over(3, count - 3, stage_six)


OUTS = ("e", "h", "polar", "rate", "levels", "cell")
OUT_COMPS = dict(e=3, h=3, polar=3, rate=3, levels=2, cell=1)
HELD = tuple(SCRATCH)


def lane_keep():
    lane = lane_of((1, LANES))
    outside = jnp.logical_and(lax.axis_index("gz") == 0, lane >= 320)
    return jnp.where(outside, 0.0, 1.0).astype(F32)


def material_sums(totals, label, value):
    for m in range(totals.shape[0]):
        totals[m] = totals[m] + jnp.where(label == m + 1.0, value, 0.0)


def inner_kernel(rows, *refs):
    n = len(NAMES)
    given = dict(zip(NAMES, refs[:n]))
    tiles, table_ref, push_ref = refs[n : n + 3]
    outs = dict(zip(OUTS, refs[n + 3 : n + 3 + len(OUTS)]))
    totals = refs[n + 3 + len(OUTS)]
    held = dict(zip(HELD, refs[n + 4 + len(OUTS) :]))
    totals[...] = jnp.zeros_like(totals)

    def get(comp, r):
        third = pltpu.roll(tiles[r], 128 - SPOT[comp], 1)
        return jnp.concatenate([pull(given[comp[0]], comp, r), third], 1)

    def put(name, r, values):
        if OUT_COMPS[name] == 1:
            outs[name][r] = values[0]
        else:
            for c, value in enumerate(values):
                outs[name][c, r] = value

    table = [table_ref[m] for m in range(table_ref.shape[0])]
    six_stages(
        get, put, held, (0,), rows, table, push_ref[0], push_ref[1], lambda r: 1.0, lane_keep()
    )

    def add(r, carry):
        material_sums(totals, given["lab"][r].astype(F32) + 1.0, outs["cell"][r])
        return carry

    lax.fori_loop(3, rows - 3, add, 0)


def edge_kernel(rows, *refs):
    n = len(NAMES)
    given = dict(zip(NAMES, refs[:n]))
    tiles, near, far, near_tiles, far_tiles, table_ref, push_ref, inner_totals = refs[n : n + 8]
    at = n + 8 + len(OUTS)
    outs = dict(zip(OUTS, refs[at : at + len(OUTS)]))
    totals = refs[at + len(OUTS)]
    at += len(OUTS) + 1
    ext = refs[at]
    staged = dict(zip(OUTS, refs[at + 1 : at + 1 + len(OUTS)]))
    at += 1 + len(OUTS)
    held = dict(zip(HELD, refs[at : at + len(HELD)]))
    sems = refs[at + len(HELD)]
    even = lax.rem(lax.axis_index("gy"), 2) == 0
    top = lax.axis_index("gy") == 0

    for side in range(2):
        for comp in COMPS:
            w = WIDTH[comp[0]]
            for r in range(EDGE):
                own = r - 3 if side == 0 else rows - 6 + r
                if 0 <= own < rows:
                    main = pull(given[comp[0]], comp, own)
                    tile = tiles[own]
                else:
                    k = r - (3 - w) if side == 0 else r - 6
                    if not 0 <= k < w:
                        continue
                    at_plane = PLANE[comp] + k
                    main_near = near[at_plane].astype(F32)
                    main_far = far[at_plane].astype(F32)
                    t = r if side == 0 else r - 6
                    tile_near, tile_far = near_tiles[t].astype(F32), far_tiles[t].astype(F32)
                    use_far = even if side == 0 else jnp.logical_not(even)
                    main = jnp.where(use_far, main_far, main_near)
                    tile = jnp.where(use_far, tile_far, tile_near)
                third = pltpu.roll(tile, 128 - SPOT[comp], 1)
                ext[INDEX[comp], side * EDGE + r] = jnp.concatenate([main, third], 1)

    def get(comp, r):
        return ext[INDEX[comp], r]

    def put(name, r, values):
        for c, value in enumerate(values):
            staged[name][c, r] = value

    def keep_row(r):
        return jnp.where(jnp.logical_and(top, r < 3), 0.0, 1.0).astype(F32)

    table = [table_ref[m] for m in range(table_ref.shape[0])]
    six_stages(
        get, put, held, (0, EDGE), EDGE, table, push_ref[0], push_ref[1], keep_row, lane_keep()
    )
    copies = []
    for side in range(2):
        for i, name in enumerate(OUTS):
            source = staged[name].at[:, pl.ds(side * EDGE + 3, 3)]
            start = 0 if side == 0 else rows - 3
            if OUT_COMPS[name] == 1:
                source = staged[name].at[0, pl.ds(side * EDGE + 3, 3)]
                target = outs[name].at[pl.ds(start, 3)]
            else:
                target = outs[name].at[:, pl.ds(start, 3)]
            copy = pltpu.make_async_copy(source, target, sems.at[side, i])
            copy.start()
            copies.append(copy)
    totals[...] = inner_totals[...]
    for side in range(2):
        for k in range(3):
            r = side * EDGE + 3 + k
            material_sums(totals, ext[INDEX[("lab", 0)], r, :, :256], staged["cell"][0, r])
    for copy in copies:
        copy.wait()


def swapped(block, axes, reach, odd):
    size = [lax.axis_size(a) for a in ("gy", "gz")]
    pairs = []
    for y in range(size[0]):
        for z in range(size[1]):
            y2, z2 = (y + 1, z) if axes == "gy" else (y, z + 1)
            at = y if axes == "gy" else z
            if at % 2 == odd and y2 < size[0] and z2 < size[1]:
                one, two = y * size[1] + z, y2 * size[1] + z2
                pairs += [(one, two), (two, one)]
    return lax.ppermute(block, ("gy", "gz"), pairs)


def on_device(
    efield_check,
    hfield_check,
    polar_check,
    rate_check,
    levels_check,
    efield_seed,
    hfield_seed,
    polar_seed,
    rate_seed,
    levels_seed,
    material_labels,
    gain_labels,
    inverse_table,
    source_field,
    start_step,
):
    given = (
        efield_check,
        hfield_check,
        polar_check,
        rate_check,
        levels_check,
        material_labels,
        gain_labels,
        source_field,
        efield_seed,
        levels_seed,
        hfield_seed,
        polar_seed,
        rate_seed,
    )
    rows = material_labels.shape[0]
    count = inverse_table.shape[0]
    start = start_step[0].astype(F32)
    pushes = jnp.stack([jnp.sin(SOURCE_OMEGA * start), jnp.sin(SOURCE_OMEGA * (start + 1.0))])
    anywhere = pl.BlockSpec(memory_space=pl.ANY)
    vmem = pl.BlockSpec(memory_space=pltpu.VMEM)
    smem = pl.BlockSpec(memory_space=pltpu.SMEM)
    message = jax.ShapeDtypeStruct((PLANES, 8, 256), BF16)
    limit = pltpu.CompilerParams(vmem_limit_bytes=60 * 1024 * 1024)

    send_near, send_far = pl.pallas_call(
        lambda *refs: pack_rows(rows, *refs),
        out_shape=(message, message),
        in_specs=[anywhere] * len(given),
        out_specs=(vmem, vmem),
        scratch_shapes=[
            pltpu.VMEM((2, 26, 8, 256), F32),
            pltpu.VMEM((2, 4, 8, 256), jnp.int32),
            pltpu.SemaphoreType.DMA((2, len(COMPS))),
        ],
        name="pack_rows",
    )(*given)
    far = swapped(send_far, "gy", 1, 1)
    near = swapped(send_near, "gy", 1, 0)

    tile_shape = jax.ShapeDtypeStruct((rows, 8, 128), BF16)
    send_first, send_second = pl.pallas_call(
        pack_columns,
        out_shape=(tile_shape, tile_shape),
        in_specs=[vmem] * len(given),
        out_specs=(vmem, vmem),
        compiler_params=limit,
        name="pack_columns",
    )(*given)
    first = swapped(send_first, "gz", 1, 0)
    second = swapped(send_second, "gz", 1, 1)
    even_z = lax.rem(lax.axis_index("gz"), 2) == 0
    even_y = lax.rem(lax.axis_index("gy"), 2) == 0
    tiles = jnp.where((IS_FRONT[None] == 1) == even_z, first, second)
    last, begin = tiles[rows - 3 :], tiles[:3]
    far_tiles = swapped(jnp.where(even_y, begin, last), "gy", 1, 1)
    near_tiles = swapped(jnp.where(even_y, last, begin), "gy", 1, 0)
    tiles = tiles.astype(F32)

    def out_shape(name):
        dims = (rows, 8, 256)
        return jax.ShapeDtypeStruct(dims if OUT_COMPS[name] == 1 else (OUT_COMPS[name],) + dims, F32)

    def held(size):
        return [
            pltpu.VMEM((SCRATCH[name], size, 8, 256 if name == "cE" else LANES), F32)
            for name in HELD
        ]

    sums = jax.ShapeDtypeStruct((count, 8, 256), F32)
    *inner, totals = pl.pallas_call(
        lambda *refs: inner_kernel(rows, *refs),
        out_shape=tuple(out_shape(name) for name in OUTS) + (sums,),
        in_specs=[vmem] * (len(given) + 1) + [smem, smem],
        out_specs=(vmem,) * (len(OUTS) + 1),
        scratch_shapes=held(rows),
        compiler_params=limit,
        cost_estimate=pl.CostEstimate(flops=40_000_000, bytes_accessed=12_000_000, transcendentals=0),
        name="inner_rows",
    )(*given, tiles, inverse_table, pushes)

    n = len(given) + 8
    *outs, totals = pl.pallas_call(
        lambda *refs: edge_kernel(rows, *refs),
        out_shape=tuple(out_shape(name) for name in OUTS) + (sums,),
        in_specs=[vmem] * (len(given) + 5) + [smem, smem, vmem] + [anywhere] * len(OUTS),
        out_specs=(anywhere,) * len(OUTS) + (vmem,),
        scratch_shapes=[pltpu.VMEM((len(COMPS), 2 * EDGE, 8, LANES), F32)]
        + [pltpu.VMEM((OUT_COMPS[name], 2 * EDGE, 8, 256), F32) for name in OUTS]
        + held(2 * EDGE)
        + [pltpu.SemaphoreType.DMA((2, len(OUTS)))],
        input_output_aliases={n + i: i for i in range(len(OUTS))},
        compiler_params=limit,
        cost_estimate=pl.CostEstimate(flops=16_000_000, bytes_accessed=6_000_000, transcendentals=0),
        name="edge_rows",
    )(*given, tiles, near, far, near_tiles, far_tiles, inverse_table, pushes, totals, *inner)

    devices = lax.axis_size("gy") * lax.axis_size("gz")
    cells = rows * material_labels.shape[1] * material_labels.shape[2] * devices
    part = jnp.sum(totals, axis=(1, 2))
    sent = jnp.broadcast_to(part[None, None], (devices, 1, count))
    table_grad = jnp.sum(lax.all_to_all(sent, ("gy", "gz"), 0, 0), axis=(0, 1)) * (
        1.0 / math.sqrt(cells)
    )
    return (*outs, table_grad)


def solution(mesh):
    field = P(None, "gy", None, "gz")
    cell = P("gy", None, "gz")
    return jax.shard_map(
        on_device,
        mesh=mesh,
        in_specs=(field,) * 10 + (cell, cell, P(), cell, P()),
        out_specs=(field,) * 5 + (cell, P()),
        check_vma=False,
    )
```

time: 217 us -> 95.4 us (0.44)
  the two profiles are of different devices: /device:TPU:2 before, /device:TPU:1 now
where the time goes in v2:
time: 95.4 us; the launch traced here: 95 us
  Pallas kernels  44.2 us (46%)
  blocking collectives  30.9 us (32%)
  starting transfers between devices  14 us (15%)
  other arithmetic  2.94 us (3%)
  between operations  1.59 us (2%)
  local copies, waits for them, and re-layouts  1.49 us (2%)
    all_to_all x1, blocking collectives, on_device(): lax.all_to_all(sent, ('gy', 'gz'), 0, 0)  30.9 us
    pallas_call x1, Pallas kernels, on_device(): pl.pallas_call(lambda *refs: inner_kernel(rows, *refs), out_shape=tuple((...  23.2 us
    ppermute x6, starting transfers between devices, swapped(): return lax.ppermute(block, ('gy', 'gz'), pairs)  14 us
    pallas_call x1, Pallas kernels, on_device(): pl.pallas_call(lambda *refs: edge_kernel(rows, *refs), out_shape=tuple((o...  11.6 us
    pallas_call x1, Pallas kernels, on_device(): pl.pallas_call(pack_columns, out_shape=(tile_shape, tile_shape), in_specs...  6.83 us
    pallas_call x1, Pallas kernels, on_device(): pl.pallas_call(lambda *refs: pack_rows(rows, *refs), out_shape=(message,...  2.48 us
  transfers between devices with their start and end apart: 6, of which 0 were waited for; matrix products, arithmetic and copies ran while one was open for 1% of the time, Pallas kernels for 27%

profile of v2, /device:TPU:1, one launch (start us, length us, event | category | flops | bytes accessed | tf_op | source)
XLA Modules:
  0.0 95.0 jit_solution(6001611533591254051)
XLA Ops:
  0.6 6.8 %pack_columns.1 = (bf16[32,8,128]{2,1,0:T(8,128)(2,1)}, bf16[32,8,128]{2,1,0:T(8,128)(2,1)}) custom-call(bf16[3,32,8,256]{3,2,1,0:T(8,128)(2,1)} %refs_0_.7, bf16[3,32,8,256]{3,2,1,0:T(8,128)(2,1)} %refs_1_.7, bf16[3,32,8,256]{3,2,1,0:T(8,128)(2,1)} %refs_2_.7, bf16[3,32,8,256]{3,2,1,0:T(8,128)(2,1)} %refs_3_.7, bf16[2,32,8,256]{3,2,1,0:T(8,128)(2,1)} %refs_4_.7, ...), custom_call_target="tpu_custom_call" | custom-call | tf_op jit(solution)/shard_map/pack_columns/pallas_call | solution.py:479
  7.5 2.5 %collective-permute-start = (bf16[32,8,128]{2,1,0:T(8,128)(2,1)}, bf16[32,8,128]{2,1,0:T(8,128)(2,1)S(1)}, u32[]{:S(2)}, u32[]{:S(2)}) collective-permute-start(bf16[32,8,128]{2,1,0:T(8,128)(2,1)} %get-tuple-element.25), channel_id=1, source_target_pairs={{0,1},{1,0},{2,3},{3,2},{4,5},{5,4},{6,7},{7,6},{8,9},{9,8},{10,11... | collective-permute-start | bytes 196616 | tf_op jit(solution)/shard_map/ppermute | solution.py:418
  9.9 0.7 collective-permute-start.1
  10.6 2.5 %pack_rows.1 = (bf16[62,8,256]{2,1,0:T(8,128)(2,1)}, bf16[62,8,256]{2,1,0:T(8,128)(2,1)}) custom-call(bf16[3,32,8,256]{3,2,1,0:T(8,128)(2,1)} %refs_0_.7, bf16[3,32,8,256]{3,2,1,0:T(8,128)(2,1)} %refs_1_.7, bf16[3,32,8,256]{3,2,1,0:T(8,128)(2,1)} %refs_2_.7, bf16[3,32,8,256]{3,2,1,0:T(8,128)(2,1)} %refs_3_.7, bf16[2,32,8,256]{3,2,1,0:T(8,128)(2,1)} %refs_4_.7, ...), custom_call_target="tpu_custom_call" | custom-call | tf_op jit(solution)/shard_map/pack_rows/pallas_call | solution.py:463
  13.1 1.0 %collective-permute-start.2 = (bf16[62,8,256]{2,1,0:T(8,128)(2,1)}, bf16[62,8,256]{2,1,0:T(8,128)(2,1)S(1)}, u32[]{:S(2)}, u32[]{:S(2)}) collective-permute-start(bf16[62,8,256]{2,1,0:T(8,128)(2,1)} %get-tuple-element.27), channel_id=1, source_target_pairs={{0,4},{4,0},{1,5},{5,1},{2,6},{6,2},{3,7},{7,3},{8,12},{12,8},{9,1... | collective-permute-start | bytes 761864 | tf_op jit(solution)/shard_map/ppermute | solution.py:418
  14.1 7.8 %collective-permute-start.3 = (bf16[62,8,256]{2,1,0:T(8,128)(2,1)}, bf16[62,8,256]{2,1,0:T(8,128)(2,1)S(1)}, u32[]{:S(2)}, u32[]{:S(2)}) collective-permute-start(bf16[62,8,256]{2,1,0:T(8,128)(2,1)} %get-tuple-element.28), channel_id=1, source_target_pairs={{4,8},{8,4},{5,9},{9,5},{6,10},{10,6},{7,11},{11,7},{12,16},{16,12... | collective-permute-start | bytes 761864 | tf_op jit(solution)/shard_map/ppermute | solution.py:418
  21.9 0.0 copy-start.4
  21.9 0.6 copy-done.4
  23.4 0.0 collective-permute-done
  23.4 0.0 collective-permute-done.1
  23.4 0.7 fusion
  24.1 1.9 %collective-permute-start.5 = (bf16[3,8,128]{2,1,0:T(8,128)(2,1)S(1)}, bf16[3,8,128]{2,1,0:T(8,128)(2,1)S(1)}, u32[]{:S(2)}, u32[]{:S(2)}) collective-permute-start(bf16[3,8,128]{2,1,0:T(8,128)(2,1)S(1)} %get-tuple-element.45), channel_id=1, source_target_pairs={{4,8},{8,4},{5,9},{9,5},{6,10},{10,6},{7,11},{11,7},{12,16},{16,12... | collective-permute-start | bytes 18440 | tf_op jit(solution)/shard_map/ppermute | solution.py:418
  26.0 0.1 collective-permute-start.4
  26.1 0.6 pad_maximum_fusion.refs_15_.refs_19_
  26.7 23.2 %inner_rows.1 = (f32[3,32,8,256]{3,2,1,0:T(8,128)}, f32[3,32,8,256]{3,2,1,0:T(8,128)}, f32[3,32,8,256]{3,2,1,0:T(8,128)}, f32[3,32,8,256]{3,2,1,0:T(8,128)}, f32...) custom-call(bf16[3,32,8,256]{3,2,1,0:T(8,128)(2,1)} %refs_0_.7, ...), custom_call_target="tpu_custom_call" | custom-call | flops 40000000 | bytes 12000000 | tf_op jit(solution)/shard_map/inner_rows/pallas_call | solution.py:508
  49.9 0.0 collective-permute-done.5.refs_17_
  49.9 0.0 copy-start.2
  50.0 0.0 collective-permute-done.4.refs_16_
  50.0 0.0 copy-start.3
  50.0 0.0 collective-permute-done.2.refs_14_
  50.0 0.0 copy-start
  50.0 0.0 collective-permute-done.3.refs_15_
  50.0 0.5 copy-done.2
  50.5 0.0 copy-done.3
  50.6 0.1 copy-done
  50.7 0.1 copy-done.1
  50.8 11.6 %edge_rows.1 = (f32[3,32,8,256]{3,2,1,0:T(8,128)}, f32[3,32,8,256]{3,2,1,0:T(8,128)}, f32[3,32,8,256]{3,2,1,0:T(8,128)}, f32[3,32,8,256]{3,2,1,0:T(8,128)}, f32[...) custom-call(bf16[3,32,8,256]{3,2,1,0:T(8,128)(2,1)} %refs_0_.7, ...), custom_call_target="tpu_custom_call", output_to_operand_aliasing={{0}: (21, {}), {1}: (22, {}), {2}: (23, {}), {3}: (24, {}),... | custom-call | flops 16000000 | bytes 6000000 | tf_op jit(solution)/shard_map/edge_rows/pallas_call | solution.py:520
  62.4 0.9 reduce_sum.18
  63.3 0.1 broadcast_in_dim.18
  63.4 30.9 %all_to_all.5 = f32[256,1,4]{2,1,0:T(1,128)S(1)} all-to-all(f32[256,1,4]{2,1,0:T(1,128)S(1)} %broadcast_in_dim.18), channel_id=1, replica_groups=mesh['gy'=64,'gz'=4] {'gy','gz'}, dimensions={0} | all-to-all | bytes 8192 | tf_op jit(solution)/shard_map/all_to_all | solution.py:539
  94.2 0.3 reduce_sum.19
  94.5 0.5 broadcast_multiply_fusion
  (3 shorter events, 0.0 us)
Async XLA Ops:
  7.5 15.9 %collective-permute-start = (bf16[32,8,128]{2,1,0:T(8,128)(2,1)}, bf16[32,8,128]{2,1,0:T(8,128)(2,1)S(1)}, u32[]{:S(2)}, u32[]{:S(2)}) collective-permute-start(bf16[32,8,128]{2,1,0:T(8,128)(2,1)} %get-tuple-element.25), channel_id=1, source_target_pairs={{0,1},{1,0},{2,3},{3,2},{4,5},{5,4},{6,7},{7,6},{8,9},{9,8},{10,11... | collective-permute-start | bytes 196616 | tf_op jit(solution)/shard_map/ppermute | solution.py:418
  9.9 13.5 %collective-permute-start.1 = (bf16[32,8,128]{2,1,0:T(8,128)(2,1)}, bf16[32,8,128]{2,1,0:T(8,128)(2,1)S(1)}, u32[]{:S(2)}, u32[]{:S(2)}) collective-permute-start(bf16[32,8,128]{2,1,0:T(8,128)(2,1)} %get-tuple-element.26), channel_id=1, source_target_pairs={{1,2},{2,1},{5,6},{6,5},{9,10},{10,9},{13,14},{14,13},{17,18},{18,... | collective-permute-start | bytes 196616 | tf_op jit(solution)/shard_map/ppermute | solution.py:418
  13.1 36.9 %collective-permute-start.2 = (bf16[62,8,256]{2,1,0:T(8,128)(2,1)}, bf16[62,8,256]{2,1,0:T(8,128)(2,1)S(1)}, u32[]{:S(2)}, u32[]{:S(2)}) collective-permute-start(bf16[62,8,256]{2,1,0:T(8,128)(2,1)} %get-tuple-element.27), channel_id=1, source_target_pairs={{0,4},{4,0},{1,5},{5,1},{2,6},{6,2},{3,7},{7,3},{8,12},{12,8},{9,1... | collective-permute-start | bytes 761864 | tf_op jit(solution)/shard_map/ppermute | solution.py:418
  14.1 35.9 %collective-permute-start.3 = (bf16[62,8,256]{2,1,0:T(8,128)(2,1)}, bf16[62,8,256]{2,1,0:T(8,128)(2,1)S(1)}, u32[]{:S(2)}, u32[]{:S(2)}) collective-permute-start(bf16[62,8,256]{2,1,0:T(8,128)(2,1)} %get-tuple-element.28), channel_id=1, source_target_pairs={{4,8},{8,4},{5,9},{9,5},{6,10},{10,6},{7,11},{11,7},{12,16},{16,12... | collective-permute-start | bytes 761864 | tf_op jit(solution)/shard_map/ppermute | solution.py:418
  21.9 0.7 copy-start.4
  24.1 25.8 %collective-permute-start.5 = (bf16[3,8,128]{2,1,0:T(8,128)(2,1)S(1)}, bf16[3,8,128]{2,1,0:T(8,128)(2,1)S(1)}, u32[]{:S(2)}, u32[]{:S(2)}) collective-permute-start(bf16[3,8,128]{2,1,0:T(8,128)(2,1)S(1)} %get-tuple-element.45), channel_id=1, source_target_pairs={{4,8},{8,4},{5,9},{9,5},{6,10},{10,6},{7,11},{11,7},{12,16},{16,12... | collective-permute-start | bytes 18440 | tf_op jit(solution)/shard_map/ppermute | solution.py:418
  26.0 23.9 %collective-permute-start.4 = (bf16[3,8,128]{2,1,0:T(8,128)(2,1)S(1)}, bf16[3,8,128]{2,1,0:T(8,128)(2,1)S(1)}, u32[]{:S(2)}, u32[]{:S(2)}) collective-permute-start(bf16[3,8,128]{2,1,0:T(8,128)(2,1)S(1)} %get-tuple-element.46), channel_id=1, source_target_pairs={{0,4},{4,0},{1,5},{5,1},{2,6},{6,2},{3,7},{7,3},{8,12},{12,8},{9,1... | collective-permute-start | bytes 18440 | tf_op jit(solution)/shard_map/ppermute | solution.py:418
  49.9 0.6 copy-start.2
  50.0 0.6 copy-start.3
  50.0 0.7 copy-start
  50.0 0.8 copy-start.1

commit v3 on v2

--- a/solution.py
+++ b/solution.py
@@ -26,7 +26,9 @@
     PLANE[_comp] = _plane
     _lane += 2 * _w
     _plane += _w
-PLANES = _plane
+LOW_BITS = _plane
+CORNERS = LOW_BITS + 3
+PLANES = CORNERS + 2
 LANES = 384
 EDGE = 9
 
@@ -83,6 +85,11 @@
             if comp[0] == "lab":
                 value = value + 1.0
             messages[side][PLANE[comp] + k] = value.astype(BF16)
+        if comp[0] == "Hs":
+            last = even if side == 0 else jnp.logical_not(even)
+            value = jnp.where(last, held[side, at + 1], held[side, at])
+            low = value - value.astype(BF16).astype(F32)
+            messages[side][LOW_BITS + comp[1]] = low.astype(BF16)
 
 
 def pack_columns(*refs):
@@ -91,19 +98,22 @@
     even = lax.rem(lax.axis_index("gz"), 2) == 0
     lane = lane_of((8, 128))
 
-    def row(y, carry):
-        low = jnp.zeros((8, 128), F32)
-        high = jnp.zeros((8, 128), F32)
+    def some(block, carry):
+        ys = [block * 4 + k for k in range(4)]
+        low = [jnp.zeros((8, 128), F32) for y in ys]
+        high = [jnp.zeros((8, 128), F32) for y in ys]
         for comp in reversed(COMPS):
-            value = pull(given[comp[0]], comp, y)
             inside = lane < SPOT[comp] + WIDTH[comp[0]]
-            low = jnp.where(inside, pltpu.roll(value[:, :128], SPOT[comp], 1), low)
-            high = jnp.where(inside, pltpu.roll(value[:, 128:], SPOT[comp], 1), high)
-        first[y] = jnp.where(even, high, low).astype(BF16)
-        second[y] = jnp.where(even, low, high).astype(BF16)
+            for k, y in enumerate(ys):
+                value = pull(given[comp[0]], comp, y)
+                low[k] = jnp.where(inside, pltpu.roll(value[:, :128], SPOT[comp], 1), low[k])
+                high[k] = jnp.where(inside, pltpu.roll(value[:, 128:], SPOT[comp], 1), high[k])
+        for k, y in enumerate(ys):
+            first[y] = jnp.where(even, high[k], low[k]).astype(BF16)
+            second[y] = jnp.where(even, low[k], high[k]).astype(BF16)
         return carry
 
-    lax.fori_loop(0, first.shape[0], row, 0)
+    lax.fori_loop(0, first.shape[0] // 4, some, 0)
 
 
 def curl_ahead(v, above):
@@ -139,36 +149,33 @@
     ]
 
 
-SCRATCH = dict(M=3, E1=3, Q1=3, F1=3, Q2=3, aE=3, aC=3, bH=3, cC=3, cE=3, hg=3, inv=1, g2=1, k0=1, k1=1)
-
-
-def six_stages(get, put, held, bases, count, table, push_first, push_second, keep_row, keep_lane):
+SCRATCH = dict(
+    M=3, W=3, E1=3, Q1=3, F1=3, Q2=3, aE=3, aC=3, bH=3, cC=3, cE=3, hg=3, inv=1, g2=1, k0=1, k1=1
+)
+
+
+def six_stages(
+    get, put, tally, held, bases, count, table, push_first, push_second, keep_row, keep_lane, flushes
+):
     def load(name, row):
         return [held[name][c, row] for c in range(SCRATCH[name])]
+
+    def pair(name, row):
+        return {0: held[name][0, row], 2: held[name][2, row]}
 
     def store(name, row, values):
         for c, value in enumerate(values):
             held[name][c, row] = value
 
     def kept(values, row):
-        return [value * (keep_lane * keep_row(row)) for value in values]
+        done = []
+        for value in values:
+            value = jnp.concatenate([value[:, :256], value[:, 256:] * keep_lane], 1)
+            done.append(value if keep_row is None else value * keep_row(row))
+        return done
 
     def trio(name, row):
         return [get((name, c), row) for c in range(3)]
-
-    def over(low, high, body):
-        if len(bases) == 1:
-            lax.fori_loop(low, high, lambda r, carry: (body(r), carry)[1], 0)
-        else:
-            span = high - low
-            step = bases[1] - bases[0]
-
-            def walk(i, carry):
-                chunk = i // span
-                body(chunk * step + (i - chunk * span) + low + bases[0])
-                return carry
-
-            lax.fori_loop(0, span * len(bases), walk, 0)
 
     def stage_one(r):
         above = {0: get(("E", 0), r + 1), 2: get(("E", 2), r + 1)}
@@ -186,7 +193,7 @@
         k0 = g4 * (upper - lower)
         q1 = [0.9 * q - 0.3 * p + k0 * e for q, p, e in zip(rate, polar, electric)]
         p1 = [p + 0.5 * q for p, q in zip(polar, q1)]
-        curl = curl_back(load("M", r), {0: held["M"][0, r - 1], 2: held["M"][2, r - 1]})
+        curl = curl_back(load("M", r), pair("M", r - 1))
         f1 = [0.5 * (c - q) for c, q in zip(curl, q1)]
         f1[2] = f1[2] - push_first * source
         e1 = [e + inverse * f for e, f in zip(electric, f1)]
@@ -210,76 +217,95 @@
         store("k1", r, [k1])
 
     def stage_three(r):
-        e1 = curl_ahead(load("E1", r), {0: held["E1"][0, r + 1], 2: held["E1"][2, r + 1]})
-        store("M", r, kept([m - 0.5 * c for m, c in zip(load("M", r), e1)], r))
-        a_c = curl_ahead(load("aC", r), {0: held["aC"][0, r + 1], 2: held["aC"][2, r + 1]})
-        store("bH", r, kept([h + c for h, c in zip(trio("Hs", r), a_c)], r))
+        curl = curl_ahead(load("E1", r), pair("E1", r + 1))
+        store("W", r, kept([m - 0.5 * c for m, c in zip(load("M", r), curl)], r))
+        curl = curl_ahead(load("aC", r), pair("aC", r + 1))
+        store("bH", r, kept([h + c for h, c in zip(trio("Hs", r), curl)], r))
 
     def stage_four(r):
         (inverse,), (g2,), (k0,), (k1,) = load("inv", r), load("g2", r), load("k0", r), load("k1", r)
         up, low = get(("Ns", 0), r), get(("Ns", 1), r)
         sb = g2 * (low - up)
-        curl = curl_back(load("M", r), {0: held["M"][0, r - 1], 2: held["M"][2, r - 1]})
+        curl = curl_back(load("W", r), pair("W", r - 1))
         q2, e1, a_e = load("Q2", r), load("E1", r), load("aE", r)
         f2 = [0.5 * (c - q) for c, q in zip(curl, q2)]
         f2[2] = f2[2] - push_second * get(("src", 0), r)
         e2 = [e + inverse * f for e, f in zip(e1, f2)]
-        grad = sum(a * f for a, f in zip(a_e, f2))
+        grad = sum(a[:, :256] * f[:, :256] for a, f in zip(a_e, f2))
         p_seed = trio("Ps", r)
         qt = [
             q + sb * e + 0.5 * (p - inverse * a)
             for q, e, p, a in zip(trio("Qs", r), e2, p_seed, a_e)
         ]
-        a_p = [p - 0.3 * q for p, q in zip(p_seed, qt)]
         dn = 2.0 * g2 * sum(q * e for q, e in zip(qt, e1))
         a_up = 0.965 * up + 0.01 * low + dn
         a_low = 0.85 * low - 0.025 * up - dn
-        curl = curl_back(load("bH", r), {0: held["bH"][0, r - 1], 2: held["bH"][2, r - 1]})
+        curl = curl_back(load("bH", r), pair("bH", r - 1))
         sb = g2 * (a_low - a_up)
-        q1 = load("Q1", r)
         c_e = [
-            a + k1 * q - 0.5 * c + sb * p for a, q, c, p in zip(a_e, qt, curl, q1)
+            a + k1 * q - 0.5 * c + sb * p for a, q, c, p in zip(a_e, qt, curl, load("Q1", r))
         ]
         half = 0.5 * inverse
         store("cC", r, [half * c for c in c_e])
-        grad = grad + sum(c * f for c, f in zip(c_e, load("F1", r)))
 
         def own(value):
             return value[:, :256]
 
+        grad = grad + sum(own(c) * own(f) for c, f in zip(c_e, load("F1", r)))
         inverse, g2, k0, sb = own(inverse), own(g2), own(k0), own(sb)
-        q_out, e_out = [], []
+        p_out, q_out = [], []
         dn = 0.0
         for c in range(3):
-            pt = own(a_p[c]) - inverse * own(c_e[c])
+            a_p = own(p_seed[c]) - 0.3 * own(qt[c])
+            pt = a_p - inverse * own(c_e[c])
             q = 0.9 * own(qt[c]) + sb * own(e1[c]) + 0.5 * pt
-            q_out.append(q)
+            p_out.append(a_p - 0.3 * q)
+            q_out.append(0.9 * q)
             dn = dn + q * own(get(("E", c), r))
             held["cE"][c, r] = own(c_e[c]) + k0 * q
         dn = 2.0 * g2 * dn
         a_up, a_low = own(a_up), own(a_low)
-        put("polar", r, [own(p) - 0.3 * q for p, q in zip(a_p, q_out)])
-        put("rate", r, [0.9 * q for q in q_out])
+        put("polar", r, p_out)
+        put("rate", r, q_out)
         put("levels", r, [0.965 * a_up + 0.01 * a_low + dn, 0.85 * a_low - 0.025 * a_up - dn])
-        put("cell", r, [own(grad)])
+        put("cell", r, [grad])
 
     def stage_five(r):
-        curl = curl_ahead(load("cC", r), {0: held["cC"][0, r + 1], 2: held["cC"][2, r + 1]})
-        hg = kept([h + c for h, c in zip(load("bH", r), curl)], r)
-        store("hg", r, hg)
+        curl = curl_ahead(load("cC", r), pair("cC", r + 1))
+        store("hg", r, kept([h + c for h, c in zip(load("bH", r), curl)], r))
 
     def stage_six(r):
         hg = load("hg", r)
-        curl = curl_back(hg, {0: held["hg"][0, r - 1], 2: held["hg"][2, r - 1]})
+        curl = curl_back(hg, pair("hg", r - 1))
         put("h", r, [h[:, :256] for h in hg])
         put("e", r, [held["cE"][c, r] - 0.5 * curl[c][:, :256] for c in range(3)])
-
-    over(0, count - 1, stage_one)
-    over(1, count - 1, stage_two)
-    over(1, count - 2, stage_three)
-    over(2, count - 2, stage_four)
-    over(2, count - 3, stage_five)
-    over(3, count - 3, stage_six)
+        tally(r)
+
+    plan = (
+        (stage_six, 7, 3, count - 3),
+        (stage_five, 6, 2, count - 3),
+        (stage_four, 4, 2, count - 2),
+        (stage_three, 3, 1, count - 2),
+        (stage_two, 1, 1, count - 1),
+        (stage_one, 0, 0, count - 1),
+    )
+    marks = {low + lag for _, lag, low, high in plan} | {high + lag for _, lag, low, high in plan}
+    marks = sorted(marks | {row + 7 for row in flushes})
+    for begin, end in zip(marks, marks[1:]):
+        active = [(f, lag) for f, lag, low, high in plan if low + lag <= begin and end <= high + lag]
+
+        def body(i, carry, active=active):
+            for f, lag in active:
+                for base in bases:
+                    f(i - lag + base)
+            return carry
+
+        if end - begin == 1:
+            body(begin, 0)
+        else:
+            lax.fori_loop(begin, end, body, 0)
+        if end - 7 in flushes:
+            flushes[end - 7]()
 
 
 OUTS = ("e", "h", "polar", "rate", "levels", "cell")
@@ -288,8 +314,8 @@
 
 
 def lane_keep():
-    lane = lane_of((1, LANES))
-    outside = jnp.logical_and(lax.axis_index("gz") == 0, lane >= 320)
+    lane = lane_of((1, 128))
+    outside = jnp.logical_and(lax.axis_index("gz") == 0, lane >= 64)
     return jnp.where(outside, 0.0, 1.0).astype(F32)
 
 
@@ -302,9 +328,14 @@
     n = len(NAMES)
     given = dict(zip(NAMES, refs[:n]))
     tiles, table_ref, push_ref = refs[n : n + 3]
-    outs = dict(zip(OUTS, refs[n + 3 : n + 3 + len(OUTS)]))
-    totals = refs[n + 3 + len(OUTS)]
-    held = dict(zip(HELD, refs[n + 4 + len(OUTS) :]))
+    at = n + 3
+    outs = dict(zip(OUTS, refs[at : at + len(OUTS)]))
+    totals = refs[at + len(OUTS)]
+    at += len(OUTS) + 1
+    staged = dict(zip(OUTS, refs[at : at + len(OUTS)]))
+    at += len(OUTS)
+    held = dict(zip(HELD, refs[at : at + len(HELD)]))
+    sems = refs[at + len(HELD)]
     totals[...] = jnp.zeros_like(totals)
 
     def get(comp, r):
@@ -312,29 +343,55 @@
         return jnp.concatenate([pull(given[comp[0]], comp, r), third], 1)
 
     def put(name, r, values):
-        if OUT_COMPS[name] == 1:
-            outs[name][r] = values[0]
-        else:
-            for c, value in enumerate(values):
-                outs[name][c, r] = value
-
+        for c, value in enumerate(values):
+            staged[name][c, r] = value
+
+    def tally(r):
+        material_sums(totals, given["lab"][r].astype(F32) + 1.0, staged["cell"][0, r])
+
+    copies = []
+
+    def leave(piece, low, high):
+        for i, name in enumerate(OUTS):
+            if OUT_COMPS[name] == 1:
+                source = staged[name].at[0, pl.ds(low, high - low)]
+                target = outs[name].at[pl.ds(low, high - low)]
+            else:
+                source = staged[name].at[:, pl.ds(low, high - low)]
+                target = outs[name].at[:, pl.ds(low, high - low)]
+            copy = pltpu.make_async_copy(source, target, sems.at[piece, i])
+            copy.start()
+            copies.append(copy)
+
+    cuts = [3, 14, 22, rows - 3]
+    flushes = {
+        high: (lambda piece=piece, low=low, high=high: leave(piece, low, high))
+        for piece, (low, high) in enumerate(zip(cuts, cuts[1:]))
+    }
     table = [table_ref[m] for m in range(table_ref.shape[0])]
     six_stages(
-        get, put, held, (0,), rows, table, push_ref[0], push_ref[1], lambda r: 1.0, lane_keep()
+        get,
+        put,
+        tally,
+        held,
+        (0,),
+        rows,
+        table,
+        push_ref[0],
+        push_ref[1],
+        None,
+        lane_keep(),
+        flushes,
     )
-
-    def add(r, carry):
-        material_sums(totals, given["lab"][r].astype(F32) + 1.0, outs["cell"][r])
-        return carry
-
-    lax.fori_loop(3, rows - 3, add, 0)
+    for copy in copies:
+        copy.wait()
 
 
 def edge_kernel(rows, *refs):
     n = len(NAMES)
     given = dict(zip(NAMES, refs[:n]))
-    tiles, near, far, near_tiles, far_tiles, table_ref, push_ref, inner_totals = refs[n : n + 8]
-    at = n + 8 + len(OUTS)
+    tiles, near, far, table_ref, push_ref, inner_totals = refs[n : n + 6]
+    at = n + 6 + len(OUTS)
     outs = dict(zip(OUTS, refs[at : at + len(OUTS)]))
     totals = refs[at + len(OUTS)]
     at += len(OUTS) + 1
@@ -345,6 +402,9 @@
     sems = refs[at + len(HELD)]
     even = lax.rem(lax.axis_index("gy"), 2) == 0
     top = lax.axis_index("gy") == 0
+
+    def arrived(use_far, plane):
+        return jnp.where(use_far, far[plane].astype(F32), near[plane].astype(F32))
 
     for side in range(2):
         for comp in COMPS:
@@ -358,14 +418,13 @@
                     k = r - (3 - w) if side == 0 else r - 6
                     if not 0 <= k < w:
                         continue
-                    at_plane = PLANE[comp] + k
-                    main_near = near[at_plane].astype(F32)
-                    main_far = far[at_plane].astype(F32)
+                    use_far = even if side == 0 else jnp.logical_not(even)
+                    main = arrived(use_far, PLANE[comp] + k)
+                    if comp[0] == "Hs" and r == (2 if side == 0 else 6):
+                        main = main + arrived(use_far, LOW_BITS + comp[1])
                     t = r if side == 0 else r - 6
-                    tile_near, tile_far = near_tiles[t].astype(F32), far_tiles[t].astype(F32)
-                    use_far = even if side == 0 else jnp.logical_not(even)
-                    main = jnp.where(use_far, main_far, main_near)
-                    tile = jnp.where(use_far, tile_far, tile_near)
+                    tile = arrived(use_far, CORNERS + t // 2)
+                    tile = tile[:, (t % 2) * 128 : (t % 2) * 128 + 128]
                 third = pltpu.roll(tile, 128 - SPOT[comp], 1)
                 ext[INDEX[comp], side * EDGE + r] = jnp.concatenate([main, third], 1)
 
@@ -379,9 +438,25 @@
     def keep_row(r):
         return jnp.where(jnp.logical_and(top, r < 3), 0.0, 1.0).astype(F32)
 
+    totals[...] = inner_totals[...]
+
+    def tally(r):
+        material_sums(totals, ext[INDEX[("lab", 0)], r, :, :256], staged["cell"][0, r])
+
     table = [table_ref[m] for m in range(table_ref.shape[0])]
     six_stages(
-        get, put, held, (0, EDGE), EDGE, table, push_ref[0], push_ref[1], keep_row, lane_keep()
+        get,
+        put,
+        tally,
+        held,
+        (0, EDGE),
+        EDGE,
+        table,
+        push_ref[0],
+        push_ref[1],
+        keep_row,
+        lane_keep(),
+        {},
     )
     copies = []
     for side in range(2):
@@ -396,16 +471,11 @@
             copy = pltpu.make_async_copy(source, target, sems.at[side, i])
             copy.start()
             copies.append(copy)
-    totals[...] = inner_totals[...]
-    for side in range(2):
-        for k in range(3):
-            r = side * EDGE + 3 + k
-            material_sums(totals, ext[INDEX[("lab", 0)], r, :, :256], staged["cell"][0, r])
     for copy in copies:
         copy.wait()
 
 
-def swapped(block, axes, reach, odd):
+def swapped(block, axes, odd):
     size = [lax.axis_size(a) for a in ("gy", "gz")]
     pairs = []
     for y in range(size[0]):
@@ -458,40 +528,54 @@
     vmem = pl.BlockSpec(memory_space=pltpu.VMEM)
     smem = pl.BlockSpec(memory_space=pltpu.SMEM)
     message = jax.ShapeDtypeStruct((PLANES, 8, 256), BF16)
-    limit = pltpu.CompilerParams(vmem_limit_bytes=60 * 1024 * 1024)
-
+    limit = pltpu.CompilerParams(vmem_limit_bytes=30 * 1024 * 1024)
+
+    tile_shape = jax.ShapeDtypeStruct((rows, 8, 128), BF16)
+    blocks = 4
+
+    def row_block(array):
+        if array.ndim == 3:
+            return pl.BlockSpec((rows // blocks, 8, 256), lambda i: (i, 0, 0))
+        return pl.BlockSpec((array.shape[0], rows // blocks, 8, 256), lambda i: (0, i, 0, 0))
+
+    tile_block = pl.BlockSpec((rows // blocks, 8, 128), lambda i: (i, 0, 0))
+    send_first, send_second = pl.pallas_call(
+        pack_columns,
+        grid=(blocks,),
+        out_shape=(tile_shape, tile_shape),
+        in_specs=[row_block(array) for array in given],
+        out_specs=(tile_block, tile_block),
+        compiler_params=pltpu.CompilerParams(vmem_limit_bytes=6 * 1024 * 1024),
+        name="pack_columns",
+    )(*given)
+    first = swapped(send_first, "gz", 0)
+    second = swapped(send_second, "gz", 1)
     send_near, send_far = pl.pallas_call(
         lambda *refs: pack_rows(rows, *refs),
         out_shape=(message, message),
         in_specs=[anywhere] * len(given),
         out_specs=(vmem, vmem),
         scratch_shapes=[
-            pltpu.VMEM((2, 26, 8, 256), F32),
+            pltpu.VMEM((2, 24, 8, 256), F32),
             pltpu.VMEM((2, 4, 8, 256), jnp.int32),
             pltpu.SemaphoreType.DMA((2, len(COMPS))),
         ],
+        compiler_params=pltpu.CompilerParams(vmem_limit_bytes=6 * 1024 * 1024),
         name="pack_rows",
     )(*given)
-    far = swapped(send_far, "gy", 1, 1)
-    near = swapped(send_near, "gy", 1, 0)
-
-    tile_shape = jax.ShapeDtypeStruct((rows, 8, 128), BF16)
-    send_first, send_second = pl.pallas_call(
-        pack_columns,
-        out_shape=(tile_shape, tile_shape),
-        in_specs=[vmem] * len(given),
-        out_specs=(vmem, vmem),
-        compiler_params=limit,
-        name="pack_columns",
-    )(*given)
-    first = swapped(send_first, "gz", 1, 0)
-    second = swapped(send_second, "gz", 1, 1)
     even_z = lax.rem(lax.axis_index("gz"), 2) == 0
     even_y = lax.rem(lax.axis_index("gy"), 2) == 0
     tiles = jnp.where((IS_FRONT[None] == 1) == even_z, first, second)
-    last, begin = tiles[rows - 3 :], tiles[:3]
-    far_tiles = swapped(jnp.where(even_y, begin, last), "gy", 1, 1)
-    near_tiles = swapped(jnp.where(even_y, last, begin), "gy", 1, 0)
+
+    def corners(of):
+        upper = jnp.concatenate([of[0], of[1]], 1)
+        return jnp.stack([upper, jnp.concatenate([of[2], of[2]], 1)])
+
+    last, begin = corners(tiles[rows - 3 :]), corners(tiles[:3])
+    send_far = send_far.at[CORNERS:].set(jnp.where(even_y, begin, last))
+    send_near = send_near.at[CORNERS:].set(jnp.where(even_y, last, begin))
+    far = swapped(send_far, "gy", 1)
+    near = swapped(send_near, "gy", 0)
     tiles = tiles.astype(F32)
 
     def out_shape(name):
@@ -509,18 +593,20 @@
         lambda *refs: inner_kernel(rows, *refs),
         out_shape=tuple(out_shape(name) for name in OUTS) + (sums,),
         in_specs=[vmem] * (len(given) + 1) + [smem, smem],
-        out_specs=(vmem,) * (len(OUTS) + 1),
-        scratch_shapes=held(rows),
+        out_specs=(anywhere,) * len(OUTS) + (vmem,),
+        scratch_shapes=[pltpu.VMEM((OUT_COMPS[name], rows, 8, 256), F32) for name in OUTS]
+        + held(rows)
+        + [pltpu.SemaphoreType.DMA((3, len(OUTS)))],
         compiler_params=limit,
         cost_estimate=pl.CostEstimate(flops=40_000_000, bytes_accessed=12_000_000, transcendentals=0),
         name="inner_rows",
     )(*given, tiles, inverse_table, pushes)
 
-    n = len(given) + 8
+    n = len(given) + 6
     *outs, totals = pl.pallas_call(
         lambda *refs: edge_kernel(rows, *refs),
         out_shape=tuple(out_shape(name) for name in OUTS) + (sums,),
-        in_specs=[vmem] * (len(given) + 5) + [smem, smem, vmem] + [anywhere] * len(OUTS),
+        in_specs=[vmem] * (len(given) + 3) + [smem, smem, vmem] + [anywhere] * len(OUTS),
         out_specs=(anywhere,) * len(OUTS) + (vmem,),
         scratch_shapes=[pltpu.VMEM((len(COMPS), 2 * EDGE, 8, LANES), F32)]
         + [pltpu.VMEM((OUT_COMPS[name], 2 * EDGE, 8, 256), F32) for name in OUTS]
@@ -530,7 +616,7 @@
         compiler_params=limit,
         cost_estimate=pl.CostEstimate(flops=16_000_000, bytes_accessed=6_000_000, transcendentals=0),
         name="edge_rows",
-    )(*given, tiles, near, far, near_tiles, far_tiles, inverse_table, pushes, totals, *inner)
+    )(*given, tiles, near, far, inverse_table, pushes, totals, *inner)
 
     devices = lax.axis_size("gy") * lax.axis_size("gz")
     cells = rows * material_labels.shape[1] * material_labels.shape[2] * devices

time: 95.4 us -> 91.4 us (0.958); the launches traced: 95 us -> 90.1 us
  local copies, waits for them, and re-layouts: 1.49 us -> 31.4 us
  Pallas kernels: 44.2 us -> 17.5 us
  blocking collectives: 30.9 us -> 23.6 us
  starting transfers between devices: 14 us -> 12.6 us
    unnamed x10 -> x78, local copies, waits for them, and re-layouts: 1.41 us -> 31.3 us
    pallas_call x1, Pallas kernels: 23.2 us -> 8.42 us  [on_device(): pl.pallas_call(lambda *refs: inner_kernel(rows, *refs), out_shape=tuple((...]
    all_to_all x1, blocking collectives: 30.9 us -> 23.6 us  [on_device(): lax.all_to_all(sent, ('gy', 'gz'), 0, 0)]
    pallas_call x1, Pallas kernels: 11.6 us -> 4.45 us  [on_device(): pl.pallas_call(lambda *refs: edge_kernel(rows, *refs), out_shape=tuple((o...]
    pallas_call x1, Pallas kernels: 6.83 us -> 2.96 us  [on_device(): pl.pallas_call(pack_columns, grid=(blocks,), out_shape=(tile_shape, tile_...]
    ppermute x6 -> x4, starting transfers between devices: 14 us -> 12.6 us  [swapped(): return lax.ppermute(block, ('gy', 'gz'), pairs)]
  transfers between devices with their start and end apart: 6 -> 4, of which waited for: 0 -> 0; matrix products, arithmetic and copies ran while one was open for 1% -> 0% of each run, Pallas kernels for 27% -> 11%
where the time goes in v3:
time: 91.4 us; the launch traced here: 90.1 us
  local copies, waits for them, and re-layouts  31.4 us (34%)
  blocking collectives  23.6 us (26%)
  Pallas kernels  17.5 us (19%)
  starting transfers between devices  12.6 us (14%)
  other arithmetic  3.32 us (4%)
  between operations  1.63 us (2%)
    unnamed x78, local copies, waits for them, and re-layouts  31.3 us
    all_to_all x1, blocking collectives, on_device(): lax.all_to_all(sent, ('gy', 'gz'), 0, 0)  23.6 us
    ppermute x4, starting transfers between devices, swapped(): return lax.ppermute(block, ('gy', 'gz'), pairs)  12.6 us
    pallas_call x1, Pallas kernels, on_device(): pl.pallas_call(lambda *refs: inner_kernel(rows, *refs), out_shape=tuple((...  8.42 us
    pallas_call x1, Pallas kernels, on_device(): pl.pallas_call(lambda *refs: edge_kernel(rows, *refs), out_shape=tuple((o...  4.45 us
    pallas_call x1, Pallas kernels, on_device(): pl.pallas_call(pack_columns, grid=(blocks,), out_shape=(tile_shape, tile_...  2.96 us
  transfers between devices with their start and end apart: 4, of which 0 were waited for; matrix products, arithmetic and copies ran while one was open for 0% of the time, Pallas kernels for 11%

profile of v3, /device:TPU:1, one launch (start us, length us, event | category | flops | bytes accessed | tf_op | source)
XLA Modules:
  0.0 90.1 jit_solution(4445838256920438771)
XLA Ops:
  0.6 1.1 %copy-done = f32[3,32,8,256]{3,2,1,0:T(8,128)S(1)} copy-done((f32[3,32,8,256]{3,2,1,0:T(8,128)S(1)}, f32[3,32,8,256]{3,2,1,0:T(8,128)}, u32[]{:S(2)}) %copy-start) | copy-done | bytes 786456
  1.8 1.1 %copy-done.2 = f32[3,32,8,256]{3,2,1,0:T(8,128)S(1)} copy-done((f32[3,32,8,256]{3,2,1,0:T(8,128)S(1)}, f32[3,32,8,256]{3,2,1,0:T(8,128)}, u32[]{:S(2)}) %copy-start.2) | copy-done | bytes 786456
  2.9 1.1 %copy-done.4 = f32[3,32,8,256]{3,2,1,0:T(8,128)S(1)} copy-done((f32[3,32,8,256]{3,2,1,0:T(8,128)S(1)}, f32[3,32,8,256]{3,2,1,0:T(8,128)}, u32[]{:S(2)}) %copy-start.4) | copy-done | bytes 786456
  4.0 1.1 %copy-done.6 = f32[3,32,8,256]{3,2,1,0:T(8,128)S(1)} copy-done((f32[3,32,8,256]{3,2,1,0:T(8,128)S(1)}, f32[3,32,8,256]{3,2,1,0:T(8,128)}, u32[]{:S(2)}) %copy-start.6) | copy-done | bytes 786456
  5.2 1.0 %copy-done.8 = f32[2,32,8,256]{3,2,1,0:T(8,128)S(1)} copy-done((f32[2,32,8,256]{3,2,1,0:T(8,128)S(1)}, f32[2,32,8,256]{3,2,1,0:T(8,128)}, u32[]{:S(2)}) %copy-start.8) | copy-done | bytes 524312
  6.2 1.0 %copy-done.11 = bf16[3,32,8,256]{3,2,1,0:T(8,128)(2,1)S(1)} copy-done((bf16[3,32,8,256]{3,2,1,0:T(8,128)(2,1)S(1)}, bf16[3,32,8,256]{3,2,1,0:T(8,128)(2,1)}, u32[]{:S(2)}) %copy-start.11) | copy-done | bytes 393240
  7.2 1.0 %copy-done.13 = bf16[3,32,8,256]{3,2,1,0:T(8,128)(2,1)S(1)} copy-done((bf16[3,32,8,256]{3,2,1,0:T(8,128)(2,1)S(1)}, bf16[3,32,8,256]{3,2,1,0:T(8,128)(2,1)}, u32[]{:S(2)}) %copy-start.13) | copy-done | bytes 393240
  8.2 1.0 %copy-done.16 = bf16[3,32,8,256]{3,2,1,0:T(8,128)(2,1)S(1)} copy-done((bf16[3,32,8,256]{3,2,1,0:T(8,128)(2,1)S(1)}, bf16[3,32,8,256]{3,2,1,0:T(8,128)(2,1)}, u32[]{:S(2)}) %copy-start.16) | copy-done | bytes 393240
  9.2 1.0 %copy-done.19 = bf16[3,32,8,256]{3,2,1,0:T(8,128)(2,1)S(1)} copy-done((bf16[3,32,8,256]{3,2,1,0:T(8,128)(2,1)S(1)}, bf16[3,32,8,256]{3,2,1,0:T(8,128)(2,1)}, u32[]{:S(2)}) %copy-start.19) | copy-done | bytes 393240
  10.2 0.9 %copy-done.22 = bf16[2,32,8,256]{3,2,1,0:T(8,128)(2,1)S(1)} copy-done((bf16[2,32,8,256]{3,2,1,0:T(8,128)(2,1)S(1)}, bf16[2,32,8,256]{3,2,1,0:T(8,128)(2,1)}, u32[]{:S(2)}) %copy-start.22) | copy-done | bytes 262168
  11.1 0.9 %copy-done.25 = s32[32,8,256]{2,1,0:T(8,128)S(1)} copy-done((s32[32,8,256]{2,1,0:T(8,128)S(1)}, s32[32,8,256]{2,1,0:T(8,128)}, u32[]{:S(2)}) %copy-start.25) | copy-done | bytes 262168
  12.1 0.9 %copy-done.28 = s32[32,8,256]{2,1,0:T(8,128)S(1)} copy-done((s32[32,8,256]{2,1,0:T(8,128)S(1)}, s32[32,8,256]{2,1,0:T(8,128)}, u32[]{:S(2)}) %copy-start.28) | copy-done | bytes 262168
  14.0 3.0 %pack_columns.1 = (bf16[32,8,128]{2,1,0:T(8,128)(2,1)}, bf16[32,8,128]{2,1,0:T(8,128)(2,1)}) custom-call(bf16[3,32,8,256]{3,2,1,0:T(8,128)(2,1)S(1)} %copy-done.11, bf16[3,32,8,256]{3,2,1,0:T(8,128)(2,1)S(1)} %copy-done.13, bf16[3,32,8,256]{3,2,1,0:T(8,128)(2,1)S(1)} %copy-done.16, bf16[3,32,8,256]{3,2,1,0:T(8,128)(2,1)S(1)} %copy-done.19, ...), custom_call_target="tpu_custom_call" | custom-call | tf_op jit(solution)/shard_map/pack_columns/pallas_call | solution.py:542
  17.0 2.5 %collective-permute-start = (bf16[32,8,128]{2,1,0:T(8,128)(2,1)}, bf16[32,8,128]{2,1,0:T(8,128)(2,1)}, u32[]{:S(2)}, u32[]{:S(2)}) collective-permute-start(bf16[32,8,128]{2,1,0:T(8,128)(2,1)} %get-tuple-element.49), channel_id=1, source_target_pairs={{0,1},{1,0},{2,3},{3,2},{4,5},{5,4},{6,7},{7,6},{8,9},{9,8},{10,11... | collective-permute-start | bytes 196616 | tf_op jit(solution)/shard_map/ppermute | solution.py:488
  19.4 1.3 %collective-permute-start.1 = (bf16[32,8,128]{2,1,0:T(8,128)(2,1)}, bf16[32,8,128]{2,1,0:T(8,128)(2,1)}, u32[]{:S(2)}, u32[]{:S(2)}) collective-permute-start(bf16[32,8,128]{2,1,0:T(8,128)(2,1)} %get-tuple-element.50), channel_id=1, source_target_pairs={{1,2},{2,1},{5,6},{6,5},{9,10},{10,9},{13,14},{14,13},{17,18},{18,... | collective-permute-start | bytes 196616 | tf_op jit(solution)/shard_map/ppermute | solution.py:488
  21.4 1.0 %copy-done.9 = f32[2,32,8,256]{3,2,1,0:T(8,128)S(1)} copy-done((f32[2,32,8,256]{3,2,1,0:T(8,128)S(1)}, f32[2,32,8,256]{3,2,1,0:T(8,128)}, u32[]{:S(2)}) %copy-start.9) | copy-done | bytes 524312
  22.5 1.0 %copy-done.14 = bf16[3,32,8,256]{3,2,1,0:T(8,128)(2,1)S(1)} copy-done((bf16[3,32,8,256]{3,2,1,0:T(8,128)(2,1)S(1)}, bf16[3,32,8,256]{3,2,1,0:T(8,128)(2,1)}, u32[]{:S(2)}) %copy-start.14) | copy-done | bytes 393240
  23.5 1.0 %copy-done.17 = bf16[3,32,8,256]{3,2,1,0:T(8,128)(2,1)S(1)} copy-done((bf16[3,32,8,256]{3,2,1,0:T(8,128)(2,1)S(1)}, bf16[3,32,8,256]{3,2,1,0:T(8,128)(2,1)}, u32[]{:S(2)}) %copy-start.17) | copy-done | bytes 393240
  24.5 1.0 %copy-done.20 = bf16[3,32,8,256]{3,2,1,0:T(8,128)(2,1)S(1)} copy-done((bf16[3,32,8,256]{3,2,1,0:T(8,128)(2,1)S(1)}, bf16[3,32,8,256]{3,2,1,0:T(8,128)(2,1)}, u32[]{:S(2)}) %copy-start.20) | copy-done | bytes 393240
  25.4 0.9 %copy-done.23 = bf16[2,32,8,256]{3,2,1,0:T(8,128)(2,1)S(1)} copy-done((bf16[2,32,8,256]{3,2,1,0:T(8,128)(2,1)S(1)}, bf16[2,32,8,256]{3,2,1,0:T(8,128)(2,1)}, u32[]{:S(2)}) %copy-start.23) | copy-done | bytes 262168
  26.4 0.9 %copy-done.26 = s32[32,8,256]{2,1,0:T(8,128)S(1)} copy-done((s32[32,8,256]{2,1,0:T(8,128)S(1)}, s32[32,8,256]{2,1,0:T(8,128)}, u32[]{:S(2)}) %copy-start.26) | copy-done | bytes 262168
  27.3 0.9 %copy-done.29 = s32[32,8,256]{2,1,0:T(8,128)S(1)} copy-done((s32[32,8,256]{2,1,0:T(8,128)S(1)}, s32[32,8,256]{2,1,0:T(8,128)}, u32[]{:S(2)}) %copy-start.29) | copy-done | bytes 262168
  29.2 1.7 %pack_rows.1 = (bf16[67,8,256]{2,1,0:T(8,128)(2,1)S(1)}, bf16[67,8,256]{2,1,0:T(8,128)(2,1)S(1)}) custom-call(bf16[3,32,8,256]{3,2,1,0:T(8,128)(2,1)S(1)} %copy-done.12, bf16[3,32,8,256]{3,2,1,0:T(8,128)(2,1)S(1)} %copy-done.14, bf16[3,32,8,256]{3,2,1,0:T(8,128)(2,1)S(1)} %copy-done.17, bf16[3,32,8,256]{3,2,1,0:T(8,128)(2,1)S(1)} %copy-done.20, ...), custom_call_target="tpu_custom_call" | custom-call | tf_op jit(solution)/shard_map/pack_rows/pallas_call | solution.py:553
  34.0 8.7 %collective-permute-start.3 = (bf16[67,8,256]{2,1,0:T(8,128)(2,1)}, bf16[67,8,256]{2,1,0:T(8,128)(2,1)S(1)}, u32[]{:S(2)}, u32[]{:S(2)}) collective-permute-start(bf16[67,8,256]{2,1,0:T(8,128)(2,1)} %get-tuple-element.75), channel_id=1, source_target_pairs={{4,8},{8,4},{5,9},{9,5},{6,10},{10,6},{7,11},{11,7},{12,16},{16,12... | collective-permute-start | bytes 823304 | tf_op jit(solution)/shard_map/ppermute | solution.py:488
  44.4 1.0 %copy-done.10 = f32[2,32,8,256]{3,2,1,0:T(8,128)S(1)} copy-done((f32[2,32,8,256]{3,2,1,0:T(8,128)S(1)}, f32[2,32,8,256]{3,2,1,0:T(8,128)}, u32[]{:S(2)}) %copy-start.10) | copy-done | bytes 524312
  45.4 1.0 %copy-done.18 = bf16[3,32,8,256]{3,2,1,0:T(8,128)(2,1)S(1)} copy-done((bf16[3,32,8,256]{3,2,1,0:T(8,128)(2,1)S(1)}, bf16[3,32,8,256]{3,2,1,0:T(8,128)(2,1)}, u32[]{:S(2)}) %copy-start.18) | copy-done | bytes 393240
  46.4 1.0 %copy-done.21 = bf16[3,32,8,256]{3,2,1,0:T(8,128)(2,1)S(1)} copy-done((bf16[3,32,8,256]{3,2,1,0:T(8,128)(2,1)S(1)}, bf16[3,32,8,256]{3,2,1,0:T(8,128)(2,1)}, u32[]{:S(2)}) %copy-start.21) | copy-done | bytes 393240
  47.4 0.9 %copy-done.24 = bf16[2,32,8,256]{3,2,1,0:T(8,128)(2,1)S(1)} copy-done((bf16[2,32,8,256]{3,2,1,0:T(8,128)(2,1)S(1)}, bf16[2,32,8,256]{3,2,1,0:T(8,128)(2,1)}, u32[]{:S(2)}) %copy-start.24) | copy-done | bytes 262168
  48.4 0.9 %copy-done.27 = s32[32,8,256]{2,1,0:T(8,128)S(1)} copy-done((s32[32,8,256]{2,1,0:T(8,128)S(1)}, s32[32,8,256]{2,1,0:T(8,128)}, u32[]{:S(2)}) %copy-start.27) | copy-done | bytes 262168
  51.2 8.4 %inner_rows.1 = (f32[3,32,8,256]{3,2,1,0:T(8,128)}, f32[3,32,8,256]{3,2,1,0:T(8,128)}, f32[3,32,8,256]{3,2,1,0:T(8,128)}, f32[3,32,8,256]{3,2,1,0:T(8,128)}, f32...) custom-call(bf16[3,32,8,256]{3,2,1,0:T(8,128)(2,1)S(1)} %copy-done.12, ...), custom_call_target="tpu_custom_call" | custom-call | flops 40000000 | bytes 12000000 | tf_op jit(solution)/shard_map/inner_rows/pallas_call | solution.py:592
  59.7 4.5 %edge_rows.1 = (f32[3,32,8,256]{3,2,1,0:T(8,128)}, f32[3,32,8,256]{3,2,1,0:T(8,128)}, f32[3,32,8,256]{3,2,1,0:T(8,128)}, f32[3,32,8,256]{3,2,1,0:T(8,128)}, f32[...) custom-call(bf16[3,32,8,256]{3,2,1,0:T(8,128)(2,1)S(1)} %copy-done.1, ...), custom_call_target="tpu_custom_call", output_to_operand_aliasing={{0}: (19, {}), {1}: (20, {}), {2}: (21, {}), {3}: (22, {}),... | custom-call | flops 16000000 | bytes 6000000 | tf_op jit(solution)/shard_map/edge_rows/pallas_call | solution.py:606
  65.7 23.6 %all_to_all.5 = f32[256,1,4]{2,1,0:T(1,128)S(1)} all-to-all(f32[256,1,4]{2,1,0:T(1,128)S(1)} %broadcast_in_dim.18), channel_id=1, replica_groups=mesh['gy'=64,'gz'=4] {'gy','gz'}, dimensions={0} | all-to-all | bytes 8192 | tf_op jit(solution)/shard_map/all_to_all | solution.py:625
  (70 shorter events, 10.7 us)
Async XLA Ops:
  0.6 1.1 %copy-start = (f32[3,32,8,256]{3,2,1,0:T(8,128)S(1)}, f32[3,32,8,256]{3,2,1,0:T(8,128)}, u32[]{:S(2)}) copy-start(f32[3,32,8,256]{3,2,1,0:T(8,128)} %refs_8_.7) | copy-start | bytes 2359300
  1.8 1.1 %copy-start.2 = (f32[3,32,8,256]{3,2,1,0:T(8,128)S(1)}, f32[3,32,8,256]{3,2,1,0:T(8,128)}, u32[]{:S(2)}) copy-start(f32[3,32,8,256]{3,2,1,0:T(8,128)} %refs_10_.7) | copy-start | bytes 2359300
  2.9 1.1 %copy-start.4 = (f32[3,32,8,256]{3,2,1,0:T(8,128)S(1)}, f32[3,32,8,256]{3,2,1,0:T(8,128)}, u32[]{:S(2)}) copy-start(f32[3,32,8,256]{3,2,1,0:T(8,128)} %refs_11_.7) | copy-start | bytes 2359300
  4.0 1.1 %copy-start.6 = (f32[3,32,8,256]{3,2,1,0:T(8,128)S(1)}, f32[3,32,8,256]{3,2,1,0:T(8,128)}, u32[]{:S(2)}) copy-start(f32[3,32,8,256]{3,2,1,0:T(8,128)} %refs_12_.7) | copy-start | bytes 2359300
  5.2 1.0 %copy-start.8 = (f32[2,32,8,256]{3,2,1,0:T(8,128)S(1)}, f32[2,32,8,256]{3,2,1,0:T(8,128)}, u32[]{:S(2)}) copy-start(f32[2,32,8,256]{3,2,1,0:T(8,128)} %refs_9_.7) | copy-start | bytes 1572868
  6.2 1.0 %copy-start.11 = (bf16[3,32,8,256]{3,2,1,0:T(8,128)(2,1)S(1)}, bf16[3,32,8,256]{3,2,1,0:T(8,128)(2,1)}, u32[]{:S(2)}) copy-start(bf16[3,32,8,256]{3,2,1,0:T(8,128)(2,1)} %refs_0_.7) | copy-start | bytes 1179652
  7.2 1.0 %copy-start.13 = (bf16[3,32,8,256]{3,2,1,0:T(8,128)(2,1)S(1)}, bf16[3,32,8,256]{3,2,1,0:T(8,128)(2,1)}, u32[]{:S(2)}) copy-start(bf16[3,32,8,256]{3,2,1,0:T(8,128)(2,1)} %refs_1_.7) | copy-start | bytes 1179652
  8.2 1.0 %copy-start.16 = (bf16[3,32,8,256]{3,2,1,0:T(8,128)(2,1)S(1)}, bf16[3,32,8,256]{3,2,1,0:T(8,128)(2,1)}, u32[]{:S(2)}) copy-start(bf16[3,32,8,256]{3,2,1,0:T(8,128)(2,1)} %refs_2_.7) | copy-start | bytes 1179652
  9.2 1.0 %copy-start.19 = (bf16[3,32,8,256]{3,2,1,0:T(8,128)(2,1)S(1)}, bf16[3,32,8,256]{3,2,1,0:T(8,128)(2,1)}, u32[]{:S(2)}) copy-start(bf16[3,32,8,256]{3,2,1,0:T(8,128)(2,1)} %refs_3_.7) | copy-start | bytes 1179652
  10.2 0.9 %copy-start.22 = (bf16[2,32,8,256]{3,2,1,0:T(8,128)(2,1)S(1)}, bf16[2,32,8,256]{3,2,1,0:T(8,128)(2,1)}, u32[]{:S(2)}) copy-start(bf16[2,32,8,256]{3,2,1,0:T(8,128)(2,1)} %refs_4_.7) | copy-start | bytes 786436
  11.1 0.9 %copy-start.25 = (s32[32,8,256]{2,1,0:T(8,128)S(1)}, s32[32,8,256]{2,1,0:T(8,128)}, u32[]{:S(2)}) copy-start(s32[32,8,256]{2,1,0:T(8,128)} %refs_5_.7) | copy-start | bytes 786436
  12.1 0.9 %copy-start.28 = (s32[32,8,256]{2,1,0:T(8,128)S(1)}, s32[32,8,256]{2,1,0:T(8,128)}, u32[]{:S(2)}) copy-start(s32[32,8,256]{2,1,0:T(8,128)} %refs_6_.7) | copy-start | bytes 786436
  13.0 0.9 %copy-start.31 = (f32[32,8,256]{2,1,0:T(8,128)S(1)}, f32[32,8,256]{2,1,0:T(8,128)}, u32[]{:S(2)}) copy-start(f32[32,8,256]{2,1,0:T(8,128)} %refs_7_.7) | copy-start | bytes 786436
  14.0 7.4 %copy-start.1 = (f32[3,32,8,256]{3,2,1,0:T(8,128)S(1)}, f32[3,32,8,256]{3,2,1,0:T(8,128)}, u32[]{:S(2)}) copy-start(f32[3,32,8,256]{3,2,1,0:T(8,128)} %refs_8_.7) | copy-start | bytes 2359300
  14.0 7.4 %copy-start.3 = (f32[3,32,8,256]{3,2,1,0:T(8,128)S(1)}, f32[3,32,8,256]{3,2,1,0:T(8,128)}, u32[]{:S(2)}) copy-start(f32[3,32,8,256]{3,2,1,0:T(8,128)} %refs_10_.7) | copy-start | bytes 2359300
  14.0 7.4 %copy-start.5 = (f32[3,32,8,256]{3,2,1,0:T(8,128)S(1)}, f32[3,32,8,256]{3,2,1,0:T(8,128)}, u32[]{:S(2)}) copy-start(f32[3,32,8,256]{3,2,1,0:T(8,128)} %refs_11_.7) | copy-start | bytes 2359300
  14.0 7.4 %copy-start.7 = (f32[3,32,8,256]{3,2,1,0:T(8,128)S(1)}, f32[3,32,8,256]{3,2,1,0:T(8,128)}, u32[]{:S(2)}) copy-start(f32[3,32,8,256]{3,2,1,0:T(8,128)} %refs_12_.7) | copy-start | bytes 2359300
  14.0 7.4 %copy-start.12 = (bf16[3,32,8,256]{3,2,1,0:T(8,128)(2,1)S(1)}, bf16[3,32,8,256]{3,2,1,0:T(8,128)(2,1)}, u32[]{:S(2)}) copy-start(bf16[3,32,8,256]{3,2,1,0:T(8,128)(2,1)} %refs_0_.7) | copy-start | bytes 1179652
  17.0 15.4 %collective-permute-start = (bf16[32,8,128]{2,1,0:T(8,128)(2,1)}, bf16[32,8,128]{2,1,0:T(8,128)(2,1)}, u32[]{:S(2)}, u32[]{:S(2)}) collective-permute-start(bf16[32,8,128]{2,1,0:T(8,128)(2,1)} %get-tuple-element.49), channel_id=1, source_target_pairs={{0,1},{1,0},{2,3},{3,2},{4,5},{5,4},{6,7},{7,6},{8,9},{9,8},{10,11... | collective-permute-start | bytes 196616 | tf_op jit(solution)/shard_map/ppermute | solution.py:488
  19.4 13.0 %collective-permute-start.1 = (bf16[32,8,128]{2,1,0:T(8,128)(2,1)}, bf16[32,8,128]{2,1,0:T(8,128)(2,1)}, u32[]{:S(2)}, u32[]{:S(2)}) collective-permute-start(bf16[32,8,128]{2,1,0:T(8,128)(2,1)} %get-tuple-element.50), channel_id=1, source_target_pairs={{1,2},{2,1},{5,6},{6,5},{9,10},{10,9},{13,14},{14,13},{17,18},{18,... | collective-permute-start | bytes 196616 | tf_op jit(solution)/shard_map/ppermute | solution.py:488
  21.4 1.0 %copy-start.9 = (f32[2,32,8,256]{3,2,1,0:T(8,128)S(1)}, f32[2,32,8,256]{3,2,1,0:T(8,128)}, u32[]{:S(2)}) copy-start(f32[2,32,8,256]{3,2,1,0:T(8,128)} %refs_9_.7) | copy-start | bytes 1572868
  22.5 1.0 %copy-start.14 = (bf16[3,32,8,256]{3,2,1,0:T(8,128)(2,1)S(1)}, bf16[3,32,8,256]{3,2,1,0:T(8,128)(2,1)}, u32[]{:S(2)}) copy-start(bf16[3,32,8,256]{3,2,1,0:T(8,128)(2,1)} %refs_1_.7) | copy-start | bytes 1179652
  23.5 1.0 %copy-start.17 = (bf16[3,32,8,256]{3,2,1,0:T(8,128)(2,1)S(1)}, bf16[3,32,8,256]{3,2,1,0:T(8,128)(2,1)}, u32[]{:S(2)}) copy-start(bf16[3,32,8,256]{3,2,1,0:T(8,128)(2,1)} %refs_2_.7) | copy-start | bytes 1179652
  24.4 1.0 %copy-start.20 = (bf16[3,32,8,256]{3,2,1,0:T(8,128)(2,1)S(1)}, bf16[3,32,8,256]{3,2,1,0:T(8,128)(2,1)}, u32[]{:S(2)}) copy-start(bf16[3,32,8,256]{3,2,1,0:T(8,128)(2,1)} %refs_3_.7) | copy-start | bytes 1179652
  25.4 0.9 %copy-start.23 = (bf16[2,32,8,256]{3,2,1,0:T(8,128)(2,1)S(1)}, bf16[2,32,8,256]{3,2,1,0:T(8,128)(2,1)}, u32[]{:S(2)}) copy-start(bf16[2,32,8,256]{3,2,1,0:T(8,128)(2,1)} %refs_4_.7) | copy-start | bytes 786436
  26.4 0.9 %copy-start.26 = (s32[32,8,256]{2,1,0:T(8,128)S(1)}, s32[32,8,256]{2,1,0:T(8,128)}, u32[]{:S(2)}) copy-start(s32[32,8,256]{2,1,0:T(8,128)} %refs_5_.7) | copy-start | bytes 786436
  32.4 11.3 %copy-start.15 = (bf16[3,32,8,256]{3,2,1,0:T(8,128)(2,1)S(1)}, bf16[3,32,8,256]{3,2,1,0:T(8,128)(2,1)}, u32[]{:S(2)}) copy-start(bf16[3,32,8,256]{3,2,1,0:T(8,128)(2,1)} %refs_1_.7) | copy-start | bytes 1179652
  34.0 25.7 %collective-permute-start.3 = (bf16[67,8,256]{2,1,0:T(8,128)(2,1)}, bf16[67,8,256]{2,1,0:T(8,128)(2,1)S(1)}, u32[]{:S(2)}, u32[]{:S(2)}) collective-permute-start(bf16[67,8,256]{2,1,0:T(8,128)(2,1)} %get-tuple-element.75), channel_id=1, source_target_pairs={{4,8},{8,4},{5,9},{9,5},{6,10},{10,6},{7,11},{11,7},{12,16},{16,12... | collective-permute-start | bytes 823304 | tf_op jit(solution)/shard_map/ppermute | solution.py:488
  42.8 16.9 %collective-permute-start.2 = (bf16[67,8,256]{2,1,0:T(8,128)(2,1)}, bf16[67,8,256]{2,1,0:T(8,128)(2,1)S(1)}, u32[]{:S(2)}, u32[]{:S(2)}) collective-permute-start(bf16[67,8,256]{2,1,0:T(8,128)(2,1)} %get-tuple-element.76), channel_id=1, source_target_pairs={{0,4},{4,0},{1,5},{5,1},{2,6},{6,2},{3,7},{7,3},{8,12},{12,8},{9,1... | collective-permute-start | bytes 823304 | tf_op jit(solution)/shard_map/ppermute | solution.py:488
  44.4 1.0 %copy-start.10 = (f32[2,32,8,256]{3,2,1,0:T(8,128)S(1)}, f32[2,32,8,256]{3,2,1,0:T(8,128)}, u32[]{:S(2)}) copy-start(f32[2,32,8,256]{3,2,1,0:T(8,128)} %refs_9_.7) | copy-start | bytes 1572868
  45.4 1.0 %copy-start.18 = (bf16[3,32,8,256]{3,2,1,0:T(8,128)(2,1)S(1)}, bf16[3,32,8,256]{3,2,1,0:T(8,128)(2,1)}, u32[]{:S(2)}) copy-start(bf16[3,32,8,256]{3,2,1,0:T(8,128)(2,1)} %refs_2_.7) | copy-start | bytes 1179652
  46.4 1.0 %copy-start.21 = (bf16[3,32,8,256]{3,2,1,0:T(8,128)(2,1)S(1)}, bf16[3,32,8,256]{3,2,1,0:T(8,128)(2,1)}, u32[]{:S(2)}) copy-start(bf16[3,32,8,256]{3,2,1,0:T(8,128)(2,1)} %refs_3_.7) | copy-start | bytes 1179652
  (11 other events, 9.1 us)

commit v4 on v3

--- a/solution.py
+++ b/solution.py
@@ -51,11 +51,28 @@
     return ref.at[comp[1], pl.ds(start, count)]
 
 
+def go(copies):
+    for copy in copies:
+        copy.start()
+    return copies
+
+
+def wait(copies):
+    for copy in copies:
+        copy.wait()
+
+
 def pack_rows(rows, *refs):
-    given = dict(zip(NAMES, refs[: len(NAMES)]))
-    messages = refs[len(NAMES) : len(NAMES) + 2]
-    floats, ints, sems = refs[len(NAMES) + 2 :]
+    n = len(NAMES)
+    given = dict(zip(NAMES, refs[:n]))
+    tile_inputs, front_ref = refs[n : n + 2], refs[n + 2]
+    tile_out, outs = refs[n + 3], refs[n + 4 : n + 6]
+    messages, floats, ints, tile_in, tiles, sems, other_sems = refs[n + 6 :]
     even = lax.rem(lax.axis_index("gy"), 2) == 0
+    even_z = lax.rem(lax.axis_index("gz"), 2) == 0
+    tile_copies = go(
+        [pltpu.make_async_copy(tile_inputs[i], tile_in.at[i], other_sems.at[i]) for i in range(2)]
+    )
     started, later = [], []
     for side in range(2):
         last = even if side == 0 else jnp.logical_not(even)
@@ -65,7 +82,7 @@
             start = jnp.where(last, rows - w, 0)
             source = take(given[comp[0]], comp, start, w)
             if comp[0] in HALF:
-                target = messages[side].at[pl.ds(PLANE[comp], w)]
+                target = messages.at[side, pl.ds(PLANE[comp], w)]
             elif comp[0] in ("lab", "gain"):
                 target = ints.at[side, pl.ds(ints_at, w)]
                 later.append((side, comp, ints, ints_at))
@@ -74,22 +91,42 @@
                 target = floats.at[side, pl.ds(wide, w)]
                 later.append((side, comp, floats, wide))
                 wide += w
-            copy = pltpu.make_async_copy(source, target, sems.at[side, INDEX[comp]])
-            copy.start()
-            started.append(copy)
-    for copy in started:
-        copy.wait()
+            started.append(pltpu.make_async_copy(source, target, sems.at[side, INDEX[comp]]))
+    go(started)
+    wait(tile_copies)
+    from_first = (front_ref[...] == 1) == even_z
+
+    def merge(y, carry):
+        one, two = tile_in[0, y].astype(F32), tile_in[1, y].astype(F32)
+        tiles[y] = jnp.where(from_first, one, two)
+        return carry
+
+    lax.fori_loop(0, rows, merge, 0)
+    leaving = go([pltpu.make_async_copy(tiles, tile_out, other_sems.at[2])])
+    for side in range(2):
+        last = even if side == 0 else jnp.logical_not(even)
+        corner = [jnp.where(last, tiles[rows - 3 + k], tiles[k]) for k in range(3)]
+        messages[side, CORNERS] = jnp.concatenate(corner[:2], 1).astype(BF16)
+        messages[side, CORNERS + 1] = jnp.concatenate([corner[2], corner[2]], 1).astype(BF16)
+    wait(started)
     for side, comp, held, at in later:
         for k in range(WIDTH[comp[0]]):
             value = held[side, at + k].astype(F32)
             if comp[0] == "lab":
                 value = value + 1.0
-            messages[side][PLANE[comp] + k] = value.astype(BF16)
+            messages[side, PLANE[comp] + k] = value.astype(BF16)
         if comp[0] == "Hs":
             last = even if side == 0 else jnp.logical_not(even)
             value = jnp.where(last, held[side, at + 1], held[side, at])
             low = value - value.astype(BF16).astype(F32)
-            messages[side][LOW_BITS + comp[1]] = low.astype(BF16)
+            messages[side, LOW_BITS + comp[1]] = low.astype(BF16)
+    leaving += go(
+        [
+            pltpu.make_async_copy(messages.at[side], outs[side], other_sems.at[3 + side])
+            for side in range(2)
+        ]
+    )
+    wait(leaving)
 
 
 def pack_columns(*refs):
@@ -155,7 +192,7 @@
 
 
 def six_stages(
-    get, put, tally, held, bases, count, table, push_first, push_second, keep_row, keep_lane, flushes
+    get, put, tally, held, bases, count, table, push_first, push_second, keep_row, keep_lane, flushes, arrivals
 ):
     def load(name, row):
         return [held[name][c, row] for c in range(SCRATCH[name])]
@@ -300,6 +337,8 @@
                     f(i - lag + base)
             return carry
 
+        if begin in arrivals:
+            arrivals[begin]()
         if end - begin == 1:
             body(begin, 0)
         else:
@@ -324,18 +363,50 @@
         totals[m] = totals[m] + jnp.where(label == m + 1.0, value, 0.0)
 
 
+def leave(staged, outs, base, target, count, sems):
+    copies = []
+    for i, name in enumerate(OUTS):
+        if OUT_COMPS[name] == 1:
+            source = staged[name].at[0, pl.ds(base, count)]
+            goal = outs[name].at[pl.ds(target, count)]
+        else:
+            source = staged[name].at[:, pl.ds(base, count)]
+            goal = outs[name].at[:, pl.ds(target, count)]
+        copies.append(pltpu.make_async_copy(source, goal, sems.at[i]))
+    return go(copies)
+
+
 def inner_kernel(rows, *refs):
     n = len(NAMES)
-    given = dict(zip(NAMES, refs[:n]))
-    tiles, table_ref, push_ref = refs[n : n + 3]
+    sources = refs[: n + 1]
+    table_ref, push_ref = refs[n + 1 : n + 3]
     at = n + 3
     outs = dict(zip(OUTS, refs[at : at + len(OUTS)]))
     totals = refs[at + len(OUTS)]
     at += len(OUTS) + 1
+    inputs = refs[at : at + n + 1]
+    given, tiles = dict(zip(NAMES, inputs[:n])), inputs[n]
+    at += n + 1
     staged = dict(zip(OUTS, refs[at : at + len(OUTS)]))
     at += len(OUTS)
     held = dict(zip(HELD, refs[at : at + len(HELD)]))
-    sems = refs[at + len(HELD)]
+    load_sems, sems = refs[at + len(HELD) :]
+
+    arrivals = {}
+    begins = {0: 0, 6: 7, 10: 11, 21: 22}
+    bounds = list(begins.values()) + [rows]
+    for piece, mark in enumerate(begins):
+        low, high = bounds[piece], bounds[piece + 1]
+        copies = []
+        for i, (source, target) in enumerate(zip(sources, inputs)):
+            where = pl.ds(low, high - low)
+            if len(source.shape) == 4:
+                source, target = source.at[:, where], target.at[:, where]
+            else:
+                source, target = source.at[where], target.at[where]
+            copies.append(pltpu.make_async_copy(source, target, load_sems.at[piece, i]))
+        go(copies)
+        arrivals[mark] = lambda copies=copies: wait(copies)
     totals[...] = jnp.zeros_like(totals)
 
     def get(comp, r):
@@ -350,25 +421,13 @@
         material_sums(totals, given["lab"][r].astype(F32) + 1.0, staged["cell"][0, r])
 
     copies = []
-
-    def leave(piece, low, high):
-        for i, name in enumerate(OUTS):
-            if OUT_COMPS[name] == 1:
-                source = staged[name].at[0, pl.ds(low, high - low)]
-                target = outs[name].at[pl.ds(low, high - low)]
-            else:
-                source = staged[name].at[:, pl.ds(low, high - low)]
-                target = outs[name].at[:, pl.ds(low, high - low)]
-            copy = pltpu.make_async_copy(source, target, sems.at[piece, i])
-            copy.start()
-            copies.append(copy)
-
     cuts = [3, 14, 22, rows - 3]
-    flushes = {
-        high: (lambda piece=piece, low=low, high=high: leave(piece, low, high))
-        for piece, (low, high) in enumerate(zip(cuts, cuts[1:]))
-    }
-    table = [table_ref[m] for m in range(table_ref.shape[0])]
+
+    def flush(piece):
+        low, high = cuts[piece], cuts[piece + 1]
+        copies.extend(leave(staged, outs, low, low, high - low, sems.at[piece]))
+
+    flushes = {cuts[piece + 1]: (lambda piece=piece: flush(piece)) for piece in range(3)}
     six_stages(
         get,
         put,
@@ -376,56 +435,84 @@
         held,
         (0,),
         rows,
-        table,
+        [table_ref[m] for m in range(table_ref.shape[0])],
         push_ref[0],
         push_ref[1],
         None,
         lane_keep(),
         flushes,
+        arrivals,
     )
-    for copy in copies:
-        copy.wait()
-
-
-def edge_kernel(rows, *refs):
+    wait(copies)
+
+
+def edge_kernel(rows, scale, *refs):
     n = len(NAMES)
     given = dict(zip(NAMES, refs[:n]))
-    tiles, near, far, table_ref, push_ref, inner_totals = refs[n : n + 6]
+    tile_source, near, far, table_ref, push_ref, inner_totals = refs[n : n + 6]
     at = n + 6 + len(OUTS)
     outs = dict(zip(OUTS, refs[at : at + len(OUTS)]))
-    totals = refs[at + len(OUTS)]
+    sent = refs[at + len(OUTS)]
     at += len(OUTS) + 1
-    ext = refs[at]
-    staged = dict(zip(OUTS, refs[at + 1 : at + 1 + len(OUTS)]))
-    at += 1 + len(OUTS)
+    raw = dict(zip(NAMES, refs[at : at + n]))
+    tiles, halos, ext, totals = refs[at + n : at + n + 4]
+    at += n + 4
+    staged = dict(zip(OUTS, refs[at : at + len(OUTS)]))
+    at += len(OUTS)
     held = dict(zip(HELD, refs[at : at + len(HELD)]))
-    sems = refs[at + len(HELD)]
+    load_sems, halo_sems, sems = refs[at + len(HELD) :]
     even = lax.rem(lax.axis_index("gy"), 2) == 0
     top = lax.axis_index("gy") == 0
 
-    def arrived(use_far, plane):
-        return jnp.where(use_far, far[plane].astype(F32), near[plane].astype(F32))
-
+    def halo_copies(low, high):
+        return [
+            pltpu.make_async_copy(low, halos.at[0], halo_sems.at[0]),
+            pltpu.make_async_copy(high, halos.at[1], halo_sems.at[1]),
+        ]
+
+    @pl.when(even)
+    def _():
+        go(halo_copies(far, near))
+
+    @pl.when(jnp.logical_not(even))
+    def _():
+        go(halo_copies(near, far))
+
+    copies = []
+    for side in range(2):
+        where, goal = pl.ds((0, rows - 6)[side], 6), pl.ds(side * 6, 6)
+        for i, name in enumerate(NAMES):
+            if COUNT[name] == 1:
+                source, target = given[name].at[where], raw[name].at[goal]
+            else:
+                source, target = given[name].at[:, where], raw[name].at[:, goal]
+            copies.append(pltpu.make_async_copy(source, target, load_sems.at[side, i]))
+        copies.append(
+            pltpu.make_async_copy(tile_source.at[where], tiles.at[goal], load_sems.at[side, n])
+        )
+    copies.append(pltpu.make_async_copy(inner_totals, totals, halo_sems.at[2]))
+    go(copies)
+    wait(halo_copies(near, far))
     for side in range(2):
         for comp in COMPS:
             w = WIDTH[comp[0]]
-            for r in range(EDGE):
-                own = r - 3 if side == 0 else rows - 6 + r
-                if 0 <= own < rows:
-                    main = pull(given[comp[0]], comp, own)
-                    tile = tiles[own]
-                else:
-                    k = r - (3 - w) if side == 0 else r - 6
-                    if not 0 <= k < w:
-                        continue
-                    use_far = even if side == 0 else jnp.logical_not(even)
-                    main = arrived(use_far, PLANE[comp] + k)
-                    if comp[0] == "Hs" and r == (2 if side == 0 else 6):
-                        main = main + arrived(use_far, LOW_BITS + comp[1])
-                    t = r if side == 0 else r - 6
-                    tile = arrived(use_far, CORNERS + t // 2)
-                    tile = tile[:, (t % 2) * 128 : (t % 2) * 128 + 128]
+            for k in range(w):
+                r = 3 - w + k if side == 0 else 6 + k
+                main = halos[side, PLANE[comp] + k].astype(F32)
+                if comp[0] == "Hs" and r == (2 if side == 0 else 6):
+                    main = main + halos[side, LOW_BITS + comp[1]].astype(F32)
+                t = r if side == 0 else r - 6
+                tile = halos[side, CORNERS + t // 2].astype(F32)
+                tile = tile[:, (t % 2) * 128 : (t % 2) * 128 + 128]
                 third = pltpu.roll(tile, 128 - SPOT[comp], 1)
+                ext[INDEX[comp], side * EDGE + r] = jnp.concatenate([main, third], 1)
+    wait(copies)
+    for side in range(2):
+        for comp in COMPS:
+            for k in range(6):
+                r = 3 + k if side == 0 else k
+                main = pull(raw[comp[0]], comp, side * 6 + k)
+                third = pltpu.roll(tiles[side * 6 + k], 128 - SPOT[comp], 1)
                 ext[INDEX[comp], side * EDGE + r] = jnp.concatenate([main, third], 1)
 
     def get(comp, r):
@@ -438,12 +525,9 @@
     def keep_row(r):
         return jnp.where(jnp.logical_and(top, r < 3), 0.0, 1.0).astype(F32)
 
-    totals[...] = inner_totals[...]
-
     def tally(r):
         material_sums(totals, ext[INDEX[("lab", 0)], r, :, :256], staged["cell"][0, r])
 
-    table = [table_ref[m] for m in range(table_ref.shape[0])]
     six_stages(
         get,
         put,
@@ -451,28 +535,24 @@
         held,
         (0, EDGE),
         EDGE,
-        table,
+        [table_ref[m] for m in range(table_ref.shape[0])],
         push_ref[0],
         push_ref[1],
         keep_row,
         lane_keep(),
         {},
+        {},
     )
     copies = []
     for side in range(2):
-        for i, name in enumerate(OUTS):
-            source = staged[name].at[:, pl.ds(side * EDGE + 3, 3)]
-            start = 0 if side == 0 else rows - 3
-            if OUT_COMPS[name] == 1:
-                source = staged[name].at[0, pl.ds(side * EDGE + 3, 3)]
-                target = outs[name].at[pl.ds(start, 3)]
-            else:
-                target = outs[name].at[:, pl.ds(start, 3)]
-            copy = pltpu.make_async_copy(source, target, sems.at[side, i])
-            copy.start()
-            copies.append(copy)
-    for copy in copies:
-        copy.wait()
+        start = 0 if side == 0 else rows - 3
+        copies += leave(staged, outs, side * EDGE + 3, start, 3, sems.at[side])
+    lane = lane_of((1, 128))
+    line = jnp.zeros((1, 128), F32)
+    for m in range(totals.shape[0]):
+        line = jnp.where(lane == m, jnp.sum(totals[m]) * scale, line)
+    sent[...] = jnp.broadcast_to(line[None], sent.shape)
+    wait(copies)
 
 
 def swapped(block, axes, odd):
@@ -524,12 +604,11 @@
     count = inverse_table.shape[0]
     start = start_step[0].astype(F32)
     pushes = jnp.stack([jnp.sin(SOURCE_OMEGA * start), jnp.sin(SOURCE_OMEGA * (start + 1.0))])
+    hbm = pl.BlockSpec(memory_space=pltpu.HBM)
     anywhere = pl.BlockSpec(memory_space=pl.ANY)
     vmem = pl.BlockSpec(memory_space=pltpu.VMEM)
     smem = pl.BlockSpec(memory_space=pltpu.SMEM)
-    message = jax.ShapeDtypeStruct((PLANES, 8, 256), BF16)
-    limit = pltpu.CompilerParams(vmem_limit_bytes=30 * 1024 * 1024)
-
+    limit = pltpu.CompilerParams(vmem_limit_bytes=60 * 1024 * 1024)
     tile_shape = jax.ShapeDtypeStruct((rows, 8, 128), BF16)
     blocks = 4
 
@@ -545,86 +624,95 @@
         out_shape=(tile_shape, tile_shape),
         in_specs=[row_block(array) for array in given],
         out_specs=(tile_block, tile_block),
-        compiler_params=pltpu.CompilerParams(vmem_limit_bytes=6 * 1024 * 1024),
+        compiler_params=limit,
         name="pack_columns",
     )(*given)
     first = swapped(send_first, "gz", 0)
     second = swapped(send_second, "gz", 1)
-    send_near, send_far = pl.pallas_call(
+    message = jax.ShapeDtypeStruct((PLANES, 8, 256), BF16)
+    tiles, send_near, send_far = pl.pallas_call(
         lambda *refs: pack_rows(rows, *refs),
-        out_shape=(message, message),
-        in_specs=[anywhere] * len(given),
-        out_specs=(vmem, vmem),
+        out_shape=(jax.ShapeDtypeStruct((rows, 8, 128), F32), message, message),
+        in_specs=[hbm] * len(given) + [anywhere, anywhere, vmem],
+        out_specs=(anywhere, anywhere, anywhere),
         scratch_shapes=[
+            pltpu.VMEM((2, PLANES, 8, 256), BF16),
             pltpu.VMEM((2, 24, 8, 256), F32),
             pltpu.VMEM((2, 4, 8, 256), jnp.int32),
+            pltpu.VMEM((2, rows, 8, 128), BF16),
+            pltpu.VMEM((rows, 8, 128), F32),
             pltpu.SemaphoreType.DMA((2, len(COMPS))),
+            pltpu.SemaphoreType.DMA((5,)),
         ],
-        compiler_params=pltpu.CompilerParams(vmem_limit_bytes=6 * 1024 * 1024),
+        compiler_params=limit,
         name="pack_rows",
-    )(*given)
-    even_z = lax.rem(lax.axis_index("gz"), 2) == 0
-    even_y = lax.rem(lax.axis_index("gy"), 2) == 0
-    tiles = jnp.where((IS_FRONT[None] == 1) == even_z, first, second)
-
-    def corners(of):
-        upper = jnp.concatenate([of[0], of[1]], 1)
-        return jnp.stack([upper, jnp.concatenate([of[2], of[2]], 1)])
-
-    last, begin = corners(tiles[rows - 3 :]), corners(tiles[:3])
-    send_far = send_far.at[CORNERS:].set(jnp.where(even_y, begin, last))
-    send_near = send_near.at[CORNERS:].set(jnp.where(even_y, last, begin))
+    )(*given, first, second, jnp.broadcast_to(IS_FRONT, (8, 128)))
     far = swapped(send_far, "gy", 1)
     near = swapped(send_near, "gy", 0)
-    tiles = tiles.astype(F32)
 
     def out_shape(name):
         dims = (rows, 8, 256)
         return jax.ShapeDtypeStruct(dims if OUT_COMPS[name] == 1 else (OUT_COMPS[name],) + dims, F32)
 
-    def held(size):
+    def local(size):
         return [
             pltpu.VMEM((SCRATCH[name], size, 8, 256 if name == "cE" else LANES), F32)
             for name in HELD
         ]
 
+    def copy_of(array, size):
+        return pltpu.VMEM(array.shape[:-3] + (size,) + array.shape[-2:], array.dtype)
+
     sums = jax.ShapeDtypeStruct((count, 8, 256), F32)
     *inner, totals = pl.pallas_call(
         lambda *refs: inner_kernel(rows, *refs),
         out_shape=tuple(out_shape(name) for name in OUTS) + (sums,),
-        in_specs=[vmem] * (len(given) + 1) + [smem, smem],
-        out_specs=(anywhere,) * len(OUTS) + (vmem,),
-        scratch_shapes=[pltpu.VMEM((OUT_COMPS[name], rows, 8, 256), F32) for name in OUTS]
-        + held(rows)
-        + [pltpu.SemaphoreType.DMA((3, len(OUTS)))],
+        in_specs=[hbm] * len(given) + [anywhere, smem, smem],
+        out_specs=(hbm,) * len(OUTS) + (vmem,),
+        scratch_shapes=[copy_of(array, rows) for array in (*given, tiles)]
+        + [pltpu.VMEM((OUT_COMPS[name], rows, 8, 256), F32) for name in OUTS]
+        + local(rows)
+        + [
+            pltpu.SemaphoreType.DMA((4, len(given) + 1)),
+            pltpu.SemaphoreType.DMA((3, len(OUTS))),
+        ],
         compiler_params=limit,
         cost_estimate=pl.CostEstimate(flops=40_000_000, bytes_accessed=12_000_000, transcendentals=0),
         name="inner_rows",
     )(*given, tiles, inverse_table, pushes)
 
+    devices = lax.axis_size("gy") * lax.axis_size("gz")
+    cells = rows * material_labels.shape[1] * material_labels.shape[2] * devices
     n = len(given) + 6
-    *outs, totals = pl.pallas_call(
-        lambda *refs: edge_kernel(rows, *refs),
-        out_shape=tuple(out_shape(name) for name in OUTS) + (sums,),
-        in_specs=[vmem] * (len(given) + 3) + [smem, smem, vmem] + [anywhere] * len(OUTS),
-        out_specs=(anywhere,) * len(OUTS) + (vmem,),
-        scratch_shapes=[pltpu.VMEM((len(COMPS), 2 * EDGE, 8, LANES), F32)]
+    *outs, sent = pl.pallas_call(
+        lambda *refs: edge_kernel(rows, 1.0 / math.sqrt(cells), *refs),
+        out_shape=tuple(out_shape(name) for name in OUTS)
+        + (jax.ShapeDtypeStruct((devices, 1, 128), F32),),
+        in_specs=[hbm] * len(given)
+        + [anywhere] * 3
+        + [smem, smem, anywhere]
+        + [hbm] * len(OUTS),
+        out_specs=(hbm,) * len(OUTS) + (vmem,),
+        scratch_shapes=[copy_of(array, 12) for array in (*given, tiles)]
+        + [
+            pltpu.VMEM((2, PLANES, 8, 256), BF16),
+            pltpu.VMEM((len(COMPS), 2 * EDGE, 8, LANES), F32),
+            pltpu.VMEM((count, 8, 256), F32),
+        ]
         + [pltpu.VMEM((OUT_COMPS[name], 2 * EDGE, 8, 256), F32) for name in OUTS]
-        + held(2 * EDGE)
-        + [pltpu.SemaphoreType.DMA((2, len(OUTS)))],
+        + local(2 * EDGE)
+        + [
+            pltpu.SemaphoreType.DMA((2, len(given) + 1)),
+            pltpu.SemaphoreType.DMA((3,)),
+            pltpu.SemaphoreType.DMA((2, len(OUTS))),
+        ],
         input_output_aliases={n + i: i for i in range(len(OUTS))},
         compiler_params=limit,
         cost_estimate=pl.CostEstimate(flops=16_000_000, bytes_accessed=6_000_000, transcendentals=0),
         name="edge_rows",
     )(*given, tiles, near, far, inverse_table, pushes, totals, *inner)
-
-    devices = lax.axis_size("gy") * lax.axis_size("gz")
-    cells = rows * material_labels.shape[1] * material_labels.shape[2] * devices
-    part = jnp.sum(totals, axis=(1, 2))
-    sent = jnp.broadcast_to(part[None, None], (devices, 1, count))
-    table_grad = jnp.sum(lax.all_to_all(sent, ("gy", "gz"), 0, 0), axis=(0, 1)) * (
-        1.0 / math.sqrt(cells)
-    )
+    parts = lax.all_to_all(sent, ("gy", "gz"), 0, 0)
+    table_grad = jnp.sum(parts[:, 0, :count], axis=0)
     return (*outs, table_grad)
 
 

time: 91.4 us -> 74 us (0.81); the launches traced: 90.1 us -> 73.6 us
  local copies, waits for them, and re-layouts: 31.4 us -> 1.42 us
  Pallas kernels: 17.5 us -> 27.3 us
  blocking collectives: 23.6 us -> 27.1 us
  other arithmetic: 3.32 us -> 1.38 us
  waiting for transfers between devices: 0.01 us -> 1.21 us
  starting transfers between devices: 12.6 us -> 13.6 us
    unnamed x78 -> x10, local copies, waits for them, and re-layouts: 31.3 us -> 0.81 us
    pallas_call x2, Pallas kernels: 6.15 us -> 11.2 us  [the longest x1 7.52 us: on_device(): pl.pallas_call(lambda *refs: edge_kernel(rows, 1.0 / math.sqrt(cells), *r...]
    all_to_all x1, blocking collectives: 23.6 us -> 27.1 us  [on_device(): parts = lax.all_to_all(sent, ('gy', 'gz'), 0, 0)]
    pallas_call x1, Pallas kernels: 8.42 us -> 11.1 us  [on_device(): pl.pallas_call(lambda *refs: inner_kernel(rows, *refs), out_shape=tuple((...]
    pallas_call x1, Pallas kernels: 2.96 us -> 5.01 us  [on_device(): pl.pallas_call(pack_columns, grid=(blocks,), out_shape=(tile_shape, tile_...]
    ppermute x4, waiting for transfers between devices: 0.01 us -> 1.21 us  [swapped(): return lax.ppermute(block, ('gy', 'gz'), pairs)]
    ppermute x4, starting transfers between devices: 12.6 us -> 13.6 us  [swapped(): return lax.ppermute(block, ('gy', 'gz'), pairs)]
    convert_element_type x1 -> x0, other arithmetic: 0.94 us -> none  [on_device(): tiles = tiles.astype(F32)]
  transfers between devices with their start and end apart: 4 -> 4, of which waited for: 0 -> 1; matrix products, arithmetic and copies ran while one was open for 0% -> 1% of each run, Pallas kernels for 11% -> 15%
where the time goes in v4:
time: 74 us; the launch traced here: 73.6 us
  Pallas kernels  27.3 us (37%)
  blocking collectives  27.1 us (37%)
  starting transfers between devices  13.6 us (18%)
  between operations  1.53 us (2%)
  local copies, waits for them, and re-layouts  1.42 us (2%)
  other arithmetic  1.38 us (2%)
  waiting for transfers between devices  1.21 us (2%)
    all_to_all x1, blocking collectives, on_device(): parts = lax.all_to_all(sent, ('gy', 'gz'), 0, 0)  27.1 us
    ppermute x4, starting transfers between devices, swapped(): return lax.ppermute(block, ('gy', 'gz'), pairs)  13.6 us
    pallas_call x1, Pallas kernels, on_device(): pl.pallas_call(lambda *refs: inner_kernel(rows, *refs), out_shape=tuple((...  11.1 us
    pallas_call x1, Pallas kernels, on_device(): pl.pallas_call(lambda *refs: edge_kernel(rows, 1.0 / math.sqrt(cells), *r...  7.52 us
    pallas_call x1, Pallas kernels, on_device(): pl.pallas_call(pack_columns, grid=(blocks,), out_shape=(tile_shape, tile_...  5.01 us
    pallas_call x1, Pallas kernels, on_device(): pl.pallas_call(lambda *refs: pack_rows(rows, *refs), out_shape=(jax.Shape...  3.66 us
  transfers between devices with their start and end apart: 4, of which 1 were waited for; matrix products, arithmetic and copies ran while one was open for 1% of the time, Pallas kernels for 15%

profile of v4, /device:TPU:1, one launch (start us, length us, event | category | flops | bytes accessed | tf_op | source)
XLA Modules:
  0.0 73.6 jit_solution(16885137792478871591)
XLA Ops:
  0.6 5.0 %pack_columns.1 = (bf16[32,8,128]{2,1,0:T(8,128)(2,1)}, bf16[32,8,128]{2,1,0:T(8,128)(2,1)}) custom-call(bf16[3,32,8,256]{3,2,1,0:T(8,128)(2,1)} %refs_0_.7, bf16[3,32,8,256]{3,2,1,0:T(8,128)(2,1)} %refs_1_.7, bf16[3,32,8,256]{3,2,1,0:T(8,128)(2,1)} %refs_2_.7, bf16[3,32,8,256]{3,2,1,0:T(8,128)(2,1)} %refs_3_.7, bf16[2,32,8,256]{3,2,1,0:T(8,128)(2,1)} %refs_4_.7, ...), custom_call_target="tpu_custom_call" | custom-call | tf_op jit(solution)/shard_map/pack_columns/pallas_call | solution.py:621
  5.6 0.0 copy-start.4
  5.7 2.5 %collective-permute-start = (bf16[32,8,128]{2,1,0:T(8,128)(2,1)}, bf16[32,8,128]{2,1,0:T(8,128)(2,1)S(1)}, u32[]{:S(2)}, u32[]{:S(2)}) collective-permute-start(bf16[32,8,128]{2,1,0:T(8,128)(2,1)} %get-tuple-element.26), channel_id=1, source_target_pairs={{0,1},{1,0},{2,3},{3,2},{4,5},{5,4},{6,7},{7,6},{8,9},{9,8},{10,11... | collective-permute-start | bytes 196616 | tf_op jit(solution)/shard_map/ppermute | solution.py:568
  8.2 0.7 collective-permute-start.1
  8.9 1.2 %collective-permute-done.refs_13_ = bf16[32,8,128]{2,1,0:T(8,128)(2,1)S(1)} collective-permute-done((bf16[32,8,128]{2,1,0:T(8,128)(2,1)}, bf16[32,8,128]{2,1,0:T(8,128)(2,1)S(1)}, u32[]{:S(2)}, u32[]{:S(2)}) %collective-permute-start) | collective-permute-done | bytes 65568 | tf_op jit(solution)/shard_map/ppermute | solution.py:568
  10.1 0.0 copy-start.2
  10.1 0.0 collective-permute-done.1.refs_14_
  10.1 0.0 copy-done.4
  10.1 0.0 copy-start.3
  10.1 0.6 broadcast_in_dim.8.refs_15_
  10.7 0.0 copy-done.2
  10.7 0.0 copy-done.3
  10.7 3.7 %pack_rows.1 = (f32[32,8,128]{2,1,0:T(8,128)}, bf16[67,8,256]{2,1,0:T(8,128)(2,1)}, bf16[67,8,256]{2,1,0:T(8,128)(2,1)}) custom-call(bf16[3,32,8,256]{3,2,1,0:T(8,128)(2,1)} %refs_0_.7, bf16[3,32,8,256]{3,2,1,0:T(8,128)(2,1)} %refs_1_.7, bf16[3,32,8,256]{3,2,1,0:T(8,128)(2,1)} %refs_2_.7, bf16[3,32,8,256]{3,2,1,0:T(8,128)(2,1)} %refs_3_.7, ...), custom_call_target="tpu_custom_call" | custom-call | tf_op jit(solution)/shard_map/pack_rows/pallas_call | solution.py:633
  14.4 3.4 %collective-permute-start.2 = (bf16[67,8,256]{2,1,0:T(8,128)(2,1)}, bf16[67,8,256]{2,1,0:T(8,128)(2,1)S(1)}, u32[]{:S(2)}, u32[]{:S(2)}) collective-permute-start(bf16[67,8,256]{2,1,0:T(8,128)(2,1)} %get-tuple-element.29), channel_id=1, source_target_pairs={{0,4},{4,0},{1,5},{5,1},{2,6},{6,2},{3,7},{7,3},{8,12},{12,8},{9,1... | collective-permute-start | bytes 823304 | tf_op jit(solution)/shard_map/ppermute | solution.py:568
  17.8 7.0 %collective-permute-start.3 = (bf16[67,8,256]{2,1,0:T(8,128)(2,1)}, bf16[67,8,256]{2,1,0:T(8,128)(2,1)S(1)}, u32[]{:S(2)}, u32[]{:S(2)}) collective-permute-start(bf16[67,8,256]{2,1,0:T(8,128)(2,1)} %get-tuple-element.30), channel_id=1, source_target_pairs={{4,8},{8,4},{5,9},{9,5},{6,10},{10,6},{7,11},{11,7},{12,16},{16,12... | collective-permute-start | bytes 823304 | tf_op jit(solution)/shard_map/ppermute | solution.py:568
  25.6 0.6 pad_maximum_fusion.refs_15_.refs_17_
  26.2 11.1 %inner_rows.1 = (f32[3,32,8,256]{3,2,1,0:T(8,128)}, f32[3,32,8,256]{3,2,1,0:T(8,128)}, f32[3,32,8,256]{3,2,1,0:T(8,128)}, f32[3,32,8,256]{3,2,1,0:T(8,128)}, f32...) custom-call(bf16[3,32,8,256]{3,2,1,0:T(8,128)(2,1)} %refs_0_.7, ...), custom_call_target="tpu_custom_call" | custom-call | flops 40000000 | bytes 12000000 | tf_op jit(solution)/shard_map/inner_rows/pallas_call | solution.py:667
  37.4 0.0 collective-permute-done.2.refs_14_
  37.4 0.0 copy-start
  37.4 0.0 collective-permute-done.3.refs_15_
  37.4 0.0 copy-start.1
  37.4 0.7 copy-done
  38.1 0.1 copy-done.1
  38.2 7.5 %edge_rows.1 = (f32[3,32,8,256]{3,2,1,0:T(8,128)}, f32[3,32,8,256]{3,2,1,0:T(8,128)}, f32[3,32,8,256]{3,2,1,0:T(8,128)}, f32[3,32,8,256]{3,2,1,0:T(8,128)}, f32[...) custom-call(bf16[3,32,8,256]{3,2,1,0:T(8,128)(2,1)} %refs_0_.7, ...), custom_call_target="tpu_custom_call", output_to_operand_aliasing={{0}: (19, {}), {1}: (20, {}), {2}: (21, {}), {3}: (22, {}),... | custom-call | flops 16000000 | bytes 6000000 | tf_op jit(solution)/shard_map/edge_rows/pallas_call | solution.py:687
  45.7 27.1 %all_to_all.5 = f32[256,1,128]{2,1,0:T(1,128)S(1)} all-to-all(f32[256,1,128]{2,1,0:T(1,128)} %get-tuple-element.44), channel_id=1, replica_groups=mesh['gy'=64,'gz'=4] {'gy','gz'}, dimensions={0} | all-to-all | bytes 262144 | tf_op jit(solution)/shard_map/all_to_all | solution.py:714
  72.8 0.8 %slice_reduce_fusion = f32[4]{0:T(128)} fusion(f32[256,1,128]{2,1,0:T(1,128)S(1)} %all_to_all.5), kind=kLoop, calls=%fused_computation | loop fusion | flops 1020 | bytes 4112 | tf_op jit(solution)/shard_map/reduce_sum | solution.py:715
Async XLA Ops:
  5.6 4.4 %copy-start.4 = (s32[128]{0:T(128)S(1)}, s32[128]{0:T(128)}, u32[]{:S(2)}) copy-start(s32[128]{0:T(128)} %constant.25) | copy-start | bytes 1540
  5.7 4.4 %collective-permute-start = (bf16[32,8,128]{2,1,0:T(8,128)(2,1)}, bf16[32,8,128]{2,1,0:T(8,128)(2,1)S(1)}, u32[]{:S(2)}, u32[]{:S(2)}) collective-permute-start(bf16[32,8,128]{2,1,0:T(8,128)(2,1)} %get-tuple-element.26), channel_id=1, source_target_pairs={{0,1},{1,0},{2,3},{3,2},{4,5},{5,4},{6,7},{7,6},{8,9},{9,8},{10,11... | collective-permute-start | bytes 196616 | tf_op jit(solution)/shard_map/ppermute | solution.py:568
  8.2 1.9 %collective-permute-start.1 = (bf16[32,8,128]{2,1,0:T(8,128)(2,1)}, bf16[32,8,128]{2,1,0:T(8,128)(2,1)S(1)}, u32[]{:S(2)}, u32[]{:S(2)}) collective-permute-start(bf16[32,8,128]{2,1,0:T(8,128)(2,1)} %get-tuple-element.27), channel_id=1, source_target_pairs={{1,2},{2,1},{5,6},{6,5},{9,10},{10,9},{13,14},{14,13},{17,18},{18,... | collective-permute-start | bytes 196616 | tf_op jit(solution)/shard_map/ppermute | solution.py:568
  10.1 0.6 copy-start.2
  10.1 0.6 copy-start.3
  14.4 23.0 %collective-permute-start.2 = (bf16[67,8,256]{2,1,0:T(8,128)(2,1)}, bf16[67,8,256]{2,1,0:T(8,128)(2,1)S(1)}, u32[]{:S(2)}, u32[]{:S(2)}) collective-permute-start(bf16[67,8,256]{2,1,0:T(8,128)(2,1)} %get-tuple-element.29), channel_id=1, source_target_pairs={{0,4},{4,0},{1,5},{5,1},{2,6},{6,2},{3,7},{7,3},{8,12},{12,8},{9,1... | collective-permute-start | bytes 823304 | tf_op jit(solution)/shard_map/ppermute | solution.py:568
  17.8 19.6 %collective-permute-start.3 = (bf16[67,8,256]{2,1,0:T(8,128)(2,1)}, bf16[67,8,256]{2,1,0:T(8,128)(2,1)S(1)}, u32[]{:S(2)}, u32[]{:S(2)}) collective-permute-start(bf16[67,8,256]{2,1,0:T(8,128)(2,1)} %get-tuple-element.30), channel_id=1, source_target_pairs={{4,8},{8,4},{5,9},{9,5},{6,10},{10,6},{7,11},{11,7},{12,16},{16,12... | collective-permute-start | bytes 823304 | tf_op jit(solution)/shard_map/ppermute | solution.py:568
  37.4 0.7 copy-start
  37.4 0.8 %copy-start.1 = (bf16[67,8,256]{2,1,0:T(8,128)(2,1)}, bf16[67,8,256]{2,1,0:T(8,128)(2,1)S(1)}, u32[]{:S(2)}) copy-start(bf16[67,8,256]{2,1,0:T(8,128)(2,1)S(1)} %collective-permute-done.3.refs_15_) | copy-start | bytes 823300

commit v5 on v4

--- a/solution.py
+++ b/solution.py
@@ -7,6 +7,7 @@
 from jax.experimental import pallas as pl
 from jax.experimental.pallas import tpu as pltpu
 from jax.sharding import PartitionSpec as P
+
 
 SOURCE_OMEGA = 0.35
 F32 = jnp.float32
@@ -37,6 +38,17 @@
     return lax.broadcasted_iota(jnp.int32, shape, 1)
 
 
+def go(copies):
+    for copy in copies:
+        copy.start()
+    return copies
+
+
+def wait(copies):
+    for copy in copies:
+        copy.wait()
+
+
 def pull(ref, comp, index):
     name, c = comp
     if COUNT[name] == 1:
@@ -62,25 +74,30 @@
         copy.wait()
 
 
-def pack_rows(rows, *refs):
+def front_lanes():
+    lane = lane_of((8, 128))
+    front = lane < 0
+    for comp in COMPS:
+        inside = jnp.logical_and(lane >= SPOT[comp], lane < SPOT[comp] + WIDTH[comp[0]])
+        front = jnp.logical_or(front, inside)
+    return front
+
+
+def pack_kernel(rows, *refs):
     n = len(NAMES)
-    given = dict(zip(NAMES, refs[:n]))
-    tile_inputs, front_ref = refs[n : n + 2], refs[n + 2]
-    tile_out, outs = refs[n + 3], refs[n + 4 : n + 6]
-    messages, floats, ints, tile_in, tiles, sems, other_sems = refs[n + 6 :]
+    given, whole = dict(zip(NAMES, refs[:n])), dict(zip(NAMES, refs[n : 2 * n]))
+    first, second = refs[2 * n : 2 * n + 2]
+    outs = refs[2 * n + 2 : 2 * n + 4]
+    messages, floats, ints, sems, out_sems = refs[2 * n + 4 :]
+    step = pl.program_id(0)
     even = lax.rem(lax.axis_index("gy"), 2) == 0
-    even_z = lax.rem(lax.axis_index("gz"), 2) == 0
-    tile_copies = go(
-        [pltpu.make_async_copy(tile_inputs[i], tile_in.at[i], other_sems.at[i]) for i in range(2)]
-    )
-    started, later = [], []
+    copies, later = [], []
     for side in range(2):
         last = even if side == 0 else jnp.logical_not(even)
         wide = ints_at = 0
         for comp in COMPS:
             w = WIDTH[comp[0]]
-            start = jnp.where(last, rows - w, 0)
-            source = take(given[comp[0]], comp, start, w)
+            source = take(whole[comp[0]], comp, jnp.where(last, rows - w, 0), w)
             if comp[0] in HALF:
                 target = messages.at[side, pl.ds(PLANE[comp], w)]
             elif comp[0] in ("lab", "gain"):
@@ -91,48 +108,35 @@
                 target = floats.at[side, pl.ds(wide, w)]
                 later.append((side, comp, floats, wide))
                 wide += w
-            started.append(pltpu.make_async_copy(source, target, sems.at[side, INDEX[comp]]))
-    go(started)
-    wait(tile_copies)
-    from_first = (front_ref[...] == 1) == even_z
-
-    def merge(y, carry):
-        one, two = tile_in[0, y].astype(F32), tile_in[1, y].astype(F32)
-        tiles[y] = jnp.where(from_first, one, two)
-        return carry
-
-    lax.fori_loop(0, rows, merge, 0)
-    leaving = go([pltpu.make_async_copy(tiles, tile_out, other_sems.at[2])])
-    for side in range(2):
-        last = even if side == 0 else jnp.logical_not(even)
-        corner = [jnp.where(last, tiles[rows - 3 + k], tiles[k]) for k in range(3)]
-        messages[side, CORNERS] = jnp.concatenate(corner[:2], 1).astype(BF16)
-        messages[side, CORNERS + 1] = jnp.concatenate([corner[2], corner[2]], 1).astype(BF16)
-    wait(started)
-    for side, comp, held, at in later:
-        for k in range(WIDTH[comp[0]]):
-            value = held[side, at + k].astype(F32)
-            if comp[0] == "lab":
-                value = value + 1.0
-            messages[side, PLANE[comp] + k] = value.astype(BF16)
-        if comp[0] == "Hs":
-            last = even if side == 0 else jnp.logical_not(even)
-            value = jnp.where(last, held[side, at + 1], held[side, at])
-            low = value - value.astype(BF16).astype(F32)
-            messages[side, LOW_BITS + comp[1]] = low.astype(BF16)
-    leaving += go(
-        [
-            pltpu.make_async_copy(messages.at[side], outs[side], other_sems.at[3 + side])
-            for side in range(2)
-        ]
-    )
-    wait(leaving)
-
-
-def pack_columns(*refs):
-    given = dict(zip(NAMES, refs[: len(NAMES)]))
-    first, second = refs[len(NAMES) :]
-    even = lax.rem(lax.axis_index("gz"), 2) == 0
+            copies.append(pltpu.make_async_copy(source, target, sems.at[side, INDEX[comp]]))
+    leaving = [
+        pltpu.make_async_copy(
+            messages.at[side, pl.ds(0, CORNERS)], outs[side].at[pl.ds(0, CORNERS)], out_sems.at[side]
+        )
+        for side in range(2)
+    ]
+
+    @pl.when(step == 0)
+    def _():
+        go(copies)
+
+    @pl.when(step == 1)
+    def _():
+        wait(copies)
+        for side, comp, held, at in later:
+            for k in range(WIDTH[comp[0]]):
+                value = held[side, at + k].astype(F32)
+                if comp[0] == "lab":
+                    value = value + 1.0
+                messages[side, PLANE[comp] + k] = value.astype(BF16)
+            if comp[0] == "Hs":
+                last = even if side == 0 else jnp.logical_not(even)
+                value = jnp.where(last, held[side, at + 1], held[side, at])
+                low = value - value.astype(BF16).astype(F32)
+                messages[side, LOW_BITS + comp[1]] = low.astype(BF16)
+        go(leaving)
+
+    even_z = lax.rem(lax.axis_index("gz"), 2) == 0
     lane = lane_of((8, 128))
 
     def some(block, carry):
@@ -146,11 +150,46 @@
                 low[k] = jnp.where(inside, pltpu.roll(value[:, :128], SPOT[comp], 1), low[k])
                 high[k] = jnp.where(inside, pltpu.roll(value[:, 128:], SPOT[comp], 1), high[k])
         for k, y in enumerate(ys):
-            first[y] = jnp.where(even, high[k], low[k]).astype(BF16)
-            second[y] = jnp.where(even, low[k], high[k]).astype(BF16)
+            first[y] = jnp.where(even_z, high[k], low[k]).astype(BF16)
+            second[y] = jnp.where(even_z, low[k], high[k]).astype(BF16)
         return carry
 
     lax.fori_loop(0, first.shape[0] // 4, some, 0)
+
+    @pl.when(step == pl.num_programs(0) - 1)
+    def _():
+        wait(leaving)
+
+
+def corner_kernel(rows, first, second, pushes, *refs):
+    tiles, outs = refs[2], refs[3:5]
+    corners, sems = refs[5:]
+    even = lax.rem(lax.axis_index("gy"), 2) == 0
+    even_z = lax.rem(lax.axis_index("gz"), 2) == 0
+    from_first = front_lanes() == even_z
+
+    def merge(y):
+        tiles[y] = jnp.where(from_first, first[y].astype(F32), second[y].astype(F32))
+
+    ends = list(range(3)) + list(range(rows - 3, rows))
+    for y in ends:
+        merge(y)
+    for side in range(2):
+        last = even if side == 0 else jnp.logical_not(even)
+        corner = [jnp.where(last, tiles[rows - 3 + k], tiles[k]) for k in range(3)]
+        corners[side, 0] = jnp.concatenate(corner[:2], 1).astype(BF16)
+        corners[side, 1] = jnp.concatenate([corner[2], corner[2]], 1).astype(BF16)
+    copies = go(
+        [
+            pltpu.make_async_copy(
+                corners.at[side], outs[side].at[pl.ds(CORNERS, 2)], sems.at[side]
+            )
+            for side in range(2)
+        ]
+    )
+    for y in range(3, rows - 3):
+        merge(y)
+    wait(copies)
 
 
 def curl_ahead(v, above):
@@ -382,8 +421,8 @@
     table_ref, push_ref = refs[n + 1 : n + 3]
     at = n + 3
     outs = dict(zip(OUTS, refs[at : at + len(OUTS)]))
-    totals = refs[at + len(OUTS)]
-    at += len(OUTS) + 1
+    totals, ext = refs[at + len(OUTS) : at + len(OUTS) + 2]
+    at += len(OUTS) + 2
     inputs = refs[at : at + n + 1]
     given, tiles = dict(zip(NAMES, inputs[:n])), inputs[n]
     at += n + 1
@@ -443,77 +482,54 @@
         flushes,
         arrivals,
     )
+
+    def hand_on(k, carry):
+        for comp in COMPS:
+            ext[INDEX[comp], k] = get(comp, k)
+            ext[INDEX[comp], 6 + k] = get(comp, rows - 6 + k)
+        return carry
+
+    lax.fori_loop(0, 6, hand_on, 0)
     wait(copies)
 
 
-def edge_kernel(rows, scale, *refs):
-    n = len(NAMES)
-    given = dict(zip(NAMES, refs[:n]))
-    tile_source, near, far, table_ref, push_ref, inner_totals = refs[n : n + 6]
-    at = n + 6 + len(OUTS)
-    outs = dict(zip(OUTS, refs[at : at + len(OUTS)]))
-    sent = refs[at + len(OUTS)]
-    at += len(OUTS) + 1
-    raw = dict(zip(NAMES, refs[at : at + n]))
-    tiles, halos, ext, totals = refs[at + n : at + n + 4]
-    at += n + 4
+def edge_kernel(rows, scale, near, far, own, inner_totals, table_ref, push_ref, *refs):
+    outs = dict(zip(OUTS, refs[len(OUTS) : 2 * len(OUTS)]))
+    sent, ext, totals = refs[2 * len(OUTS) : 2 * len(OUTS) + 3]
+    at = 2 * len(OUTS) + 3
     staged = dict(zip(OUTS, refs[at : at + len(OUTS)]))
     at += len(OUTS)
     held = dict(zip(HELD, refs[at : at + len(HELD)]))
-    load_sems, halo_sems, sems = refs[at + len(HELD) :]
+    sems = refs[at + len(HELD)]
     even = lax.rem(lax.axis_index("gy"), 2) == 0
     top = lax.axis_index("gy") == 0
-
-    def halo_copies(low, high):
-        return [
-            pltpu.make_async_copy(low, halos.at[0], halo_sems.at[0]),
-            pltpu.make_async_copy(high, halos.at[1], halo_sems.at[1]),
-        ]
-
-    @pl.when(even)
-    def _():
-        go(halo_copies(far, near))
-
-    @pl.when(jnp.logical_not(even))
-    def _():
-        go(halo_copies(near, far))
-
-    copies = []
+    totals[...] = inner_totals[...]
+
+    def arrived(side, plane):
+        use_far = even if side == 0 else jnp.logical_not(even)
+        return jnp.where(use_far, far[plane].astype(F32), near[plane].astype(F32))
+
     for side in range(2):
-        where, goal = pl.ds((0, rows - 6)[side], 6), pl.ds(side * 6, 6)
-        for i, name in enumerate(NAMES):
-            if COUNT[name] == 1:
-                source, target = given[name].at[where], raw[name].at[goal]
-            else:
-                source, target = given[name].at[:, where], raw[name].at[:, goal]
-            copies.append(pltpu.make_async_copy(source, target, load_sems.at[side, i]))
-        copies.append(
-            pltpu.make_async_copy(tile_source.at[where], tiles.at[goal], load_sems.at[side, n])
-        )
-    copies.append(pltpu.make_async_copy(inner_totals, totals, halo_sems.at[2]))
-    go(copies)
-    wait(halo_copies(near, far))
-    for side in range(2):
+        tiles = []
+        for t in range(3):
+            tile = arrived(side, CORNERS + t // 2)
+            tiles.append(tile[:, (t % 2) * 128 : (t % 2) * 128 + 128])
         for comp in COMPS:
             w = WIDTH[comp[0]]
             for k in range(w):
                 r = 3 - w + k if side == 0 else 6 + k
-                main = halos[side, PLANE[comp] + k].astype(F32)
+                main = arrived(side, PLANE[comp] + k)
                 if comp[0] == "Hs" and r == (2 if side == 0 else 6):
-                    main = main + halos[side, LOW_BITS + comp[1]].astype(F32)
-                t = r if side == 0 else r - 6
-                tile = halos[side, CORNERS + t // 2].astype(F32)
-                tile = tile[:, (t % 2) * 128 : (t % 2) * 128 + 128]
-                third = pltpu.roll(tile, 128 - SPOT[comp], 1)
+                    main = main + arrived(side, LOW_BITS + comp[1])
+                third = pltpu.roll(tiles[r if side == 0 else r - 6], 128 - SPOT[comp], 1)
                 ext[INDEX[comp], side * EDGE + r] = jnp.concatenate([main, third], 1)
-    wait(copies)
-    for side in range(2):
+
+    def bring(k, carry):
         for comp in COMPS:
-            for k in range(6):
-                r = 3 + k if side == 0 else k
-                main = pull(raw[comp[0]], comp, side * 6 + k)
-                third = pltpu.roll(tiles[side * 6 + k], 128 - SPOT[comp], 1)
-                ext[INDEX[comp], side * EDGE + r] = jnp.concatenate([main, third], 1)
+            ext[INDEX[comp], 3 + k] = own[INDEX[comp], k]
+        return carry
+
+    lax.fori_loop(0, 12, bring, 0)
 
     def get(comp, r):
         return ext[INDEX[comp], r]
@@ -600,6 +616,7 @@
         polar_seed,
         rate_seed,
     )
+    fixed = [pltpu.with_memory_space_constraint(array, pltpu.HBM) for array in given]
     rows = material_labels.shape[0]
     count = inverse_table.shape[0]
     start = start_step[0].astype(F32)
@@ -608,8 +625,8 @@
     anywhere = pl.BlockSpec(memory_space=pl.ANY)
     vmem = pl.BlockSpec(memory_space=pltpu.VMEM)
     smem = pl.BlockSpec(memory_space=pltpu.SMEM)
-    limit = pltpu.CompilerParams(vmem_limit_bytes=60 * 1024 * 1024)
     tile_shape = jax.ShapeDtypeStruct((rows, 8, 128), BF16)
+    message = jax.ShapeDtypeStruct((PLANES, 8, 256), BF16)
     blocks = 4
 
     def row_block(array):
@@ -617,36 +634,41 @@
             return pl.BlockSpec((rows // blocks, 8, 256), lambda i: (i, 0, 0))
         return pl.BlockSpec((array.shape[0], rows // blocks, 8, 256), lambda i: (0, i, 0, 0))
 
+    def grant(mib):
+        return pltpu.CompilerParams(vmem_limit_bytes=mib * 1024 * 1024)
+
     tile_block = pl.BlockSpec((rows // blocks, 8, 128), lambda i: (i, 0, 0))
-    send_first, send_second = pl.pallas_call(
-        pack_columns,
+    send_first, send_second, send_near, send_far = pl.pallas_call(
+        lambda *refs: pack_kernel(rows, *refs),
         grid=(blocks,),
-        out_shape=(tile_shape, tile_shape),
-        in_specs=[row_block(array) for array in given],
-        out_specs=(tile_block, tile_block),
-        compiler_params=limit,
-        name="pack_columns",
-    )(*given)
-    first = swapped(send_first, "gz", 0)
-    second = swapped(send_second, "gz", 1)
-    message = jax.ShapeDtypeStruct((PLANES, 8, 256), BF16)
-    tiles, send_near, send_far = pl.pallas_call(
-        lambda *refs: pack_rows(rows, *refs),
-        out_shape=(jax.ShapeDtypeStruct((rows, 8, 128), F32), message, message),
-        in_specs=[hbm] * len(given) + [anywhere, anywhere, vmem],
-        out_specs=(anywhere, anywhere, anywhere),
+        out_shape=(tile_shape, tile_shape, message, message),
+        in_specs=[row_block(array) for array in given] + [hbm] * len(given),
+        out_specs=(tile_block, tile_block, hbm, hbm),
         scratch_shapes=[
             pltpu.VMEM((2, PLANES, 8, 256), BF16),
             pltpu.VMEM((2, 24, 8, 256), F32),
             pltpu.VMEM((2, 4, 8, 256), jnp.int32),
-            pltpu.VMEM((2, rows, 8, 128), BF16),
-            pltpu.VMEM((rows, 8, 128), F32),
             pltpu.SemaphoreType.DMA((2, len(COMPS))),
-            pltpu.SemaphoreType.DMA((5,)),
+            pltpu.SemaphoreType.DMA((2,)),
         ],
-        compiler_params=limit,
-        name="pack_rows",
-    )(*given, first, second, jnp.broadcast_to(IS_FRONT, (8, 128)))
+        compiler_params=grant(60),
+        name="pack_kernel",
+    )(*given, *given)
+    first = swapped(send_first, "gz", 0)
+    second = swapped(send_second, "gz", 1)
+    tiles, send_near, send_far = pl.pallas_call(
+        lambda *refs: corner_kernel(rows, *refs),
+        out_shape=(jax.ShapeDtypeStruct((rows, 8, 128), F32), message, message),
+        in_specs=[vmem, vmem, smem, hbm, hbm],
+        out_specs=(vmem, hbm, hbm),
+        scratch_shapes=[
+            pltpu.VMEM((2, 2, 8, 256), BF16),
+            pltpu.SemaphoreType.DMA((2,)),
+        ],
+        input_output_aliases={3: 1, 4: 2},
+        compiler_params=grant(4),
+        name="corner_kernel",
+    )(first, second, pushes, send_near, send_far)
     far = swapped(send_far, "gy", 1)
     near = swapped(send_near, "gy", 0)
 
@@ -664,11 +686,12 @@
         return pltpu.VMEM(array.shape[:-3] + (size,) + array.shape[-2:], array.dtype)
 
     sums = jax.ShapeDtypeStruct((count, 8, 256), F32)
-    *inner, totals = pl.pallas_call(
+    handed = jax.ShapeDtypeStruct((len(COMPS), 12, 8, LANES), F32)
+    *inner, totals, own = pl.pallas_call(
         lambda *refs: inner_kernel(rows, *refs),
-        out_shape=tuple(out_shape(name) for name in OUTS) + (sums,),
+        out_shape=tuple(out_shape(name) for name in OUTS) + (sums, handed),
         in_specs=[hbm] * len(given) + [anywhere, smem, smem],
-        out_specs=(hbm,) * len(OUTS) + (vmem,),
+        out_specs=(hbm,) * len(OUTS) + (vmem, vmem),
         scratch_shapes=[copy_of(array, rows) for array in (*given, tiles)]
         + [pltpu.VMEM((OUT_COMPS[name], rows, 8, 256), F32) for name in OUTS]
         + local(rows)
@@ -676,41 +699,31 @@
             pltpu.SemaphoreType.DMA((4, len(given) + 1)),
             pltpu.SemaphoreType.DMA((3, len(OUTS))),
         ],
-        compiler_params=limit,
+        compiler_params=grant(32),
         cost_estimate=pl.CostEstimate(flops=40_000_000, bytes_accessed=12_000_000, transcendentals=0),
         name="inner_rows",
-    )(*given, tiles, inverse_table, pushes)
+    )(*fixed, tiles, inverse_table, pushes)
 
     devices = lax.axis_size("gy") * lax.axis_size("gz")
     cells = rows * material_labels.shape[1] * material_labels.shape[2] * devices
-    n = len(given) + 6
     *outs, sent = pl.pallas_call(
         lambda *refs: edge_kernel(rows, 1.0 / math.sqrt(cells), *refs),
         out_shape=tuple(out_shape(name) for name in OUTS)
         + (jax.ShapeDtypeStruct((devices, 1, 128), F32),),
-        in_specs=[hbm] * len(given)
-        + [anywhere] * 3
-        + [smem, smem, anywhere]
-        + [hbm] * len(OUTS),
+        in_specs=[vmem] * 4 + [smem, smem] + [hbm] * len(OUTS),
         out_specs=(hbm,) * len(OUTS) + (vmem,),
-        scratch_shapes=[copy_of(array, 12) for array in (*given, tiles)]
-        + [
-            pltpu.VMEM((2, PLANES, 8, 256), BF16),
+        scratch_shapes=[
             pltpu.VMEM((len(COMPS), 2 * EDGE, 8, LANES), F32),
             pltpu.VMEM((count, 8, 256), F32),
         ]
         + [pltpu.VMEM((OUT_COMPS[name], 2 * EDGE, 8, 256), F32) for name in OUTS]
         + local(2 * EDGE)
-        + [
-            pltpu.SemaphoreType.DMA((2, len(given) + 1)),
-            pltpu.SemaphoreType.DMA((3,)),
-            pltpu.SemaphoreType.DMA((2, len(OUTS))),
-        ],
-        input_output_aliases={n + i: i for i in range(len(OUTS))},
-        compiler_params=limit,
+        + [pltpu.SemaphoreType.DMA((2, len(OUTS)))],
+        input_output_aliases={6 + i: i for i in range(len(OUTS))},
+        compiler_params=grant(26),
         cost_estimate=pl.CostEstimate(flops=16_000_000, bytes_accessed=6_000_000, transcendentals=0),
         name="edge_rows",
-    )(*given, tiles, near, far, inverse_table, pushes, totals, *inner)
+    )(near, far, own, totals, inverse_table, pushes, *inner)
     parts = lax.all_to_all(sent, ("gy", "gz"), 0, 0)
     table_grad = jnp.sum(parts[:, 0, :count], axis=0)
     return (*outs, table_grad)

time: 74 us -> 67.9 us (0.918)
  Pallas kernels: 27.3 us -> 22.2 us
  blocking collectives: 27.1 us -> 29.1 us
  local copies, waits for them, and re-layouts: 1.42 us -> 0.01 us
  waiting for transfers between devices: 1.21 us -> 0.34 us
    pallas_call x1, Pallas kernels: 7.52 us -> 4.34 us  [on_device(): pl.pallas_call(lambda *refs: edge_kernel(rows, 1.0 / math.sqrt(cells), *r...]
    all_to_all x1, blocking collectives: 27.1 us -> 29.1 us  [on_device(): parts = lax.all_to_all(sent, ('gy', 'gz'), 0, 0)]
    pallas_call x2, Pallas kernels: 8.67 us -> 7.42 us  [the longest x1 6.23 us: on_device(): pl.pallas_call(lambda *refs: pack_kernel(rows, *refs), grid=(blocks,), ou...]
    ppermute x4, waiting for transfers between devices: 1.21 us -> 0.34 us  [swapped(): return lax.ppermute(block, ('gy', 'gz'), pairs)]
    unnamed x10 -> x2, local copies, waits for them, and re-layouts: 0.81 us -> 0.01 us
  transfers between devices with their start and end apart: 4 -> 4, of which waited for: 1 -> 1; matrix products, arithmetic and copies ran while one was open for 1% -> 0% of each run, Pallas kernels for 15% -> 15%
where the time goes in v5:
time: 67.9 us; the launch traced here: 67.6 us
  blocking collectives  29.1 us (43%)
  Pallas kernels  22.2 us (33%)
  starting transfers between devices  13.6 us (20%)
  between operations  1.52 us (2%)
  other arithmetic  0.87 us (1%)
    all_to_all x1, blocking collectives, on_device(): parts = lax.all_to_all(sent, ('gy', 'gz'), 0, 0)  29.1 us
    ppermute x4, starting transfers between devices, swapped(): return lax.ppermute(block, ('gy', 'gz'), pairs)  13.6 us
    pallas_call x1, Pallas kernels, on_device(): pl.pallas_call(lambda *refs: inner_kernel(rows, *refs), out_shape=tuple((...  10.5 us
    pallas_call x1, Pallas kernels, on_device(): pl.pallas_call(lambda *refs: pack_kernel(rows, *refs), grid=(blocks,), ou...  6.23 us
    pallas_call x1, Pallas kernels, on_device(): pl.pallas_call(lambda *refs: edge_kernel(rows, 1.0 / math.sqrt(cells), *r...  4.34 us
  transfers between devices with their start and end apart: 4, of which 1 were waited for; matrix products, arithmetic and copies ran while one was open for 0% of the time, Pallas kernels for 15%

profile of v5, /device:TPU:1, one launch (start us, length us, event | category | flops | bytes accessed | tf_op | source)
XLA Modules:
  0.0 67.6 jit_solution(6252653318435018800)
XLA Ops:
  0.6 0.0 copy-start
  0.6 6.2 %pack_kernel.1 = (bf16[32,8,128]{2,1,0:T(8,128)(2,1)}, bf16[32,8,128]{2,1,0:T(8,128)(2,1)}, bf16[67,8,256]{2,1,0:T(8,128)(2,1)}, bf16[67,8,256]{2,1,0:T(8,128)(2,1)}) custom-call(bf16[3,32,8,256]{3,2,1,0:T(8,128)(2,1)} %refs_0_.3, bf16[3,32,8,256]{3,2,1,0:T(8,128)(2,1)} %refs_1_.3, bf16[3,32,8,256]{3,2,1,0:T(8,128)(2,1)} %refs_2_.3, ...), custom_call_target="tpu_custom_call" | custom-call | tf_op jit(solution)/shard_map/pack_kernel/pallas_call | solution.py:641
  6.9 2.5 %collective-permute-start = (bf16[32,8,128]{2,1,0:T(8,128)(2,1)}, bf16[32,8,128]{2,1,0:T(8,128)(2,1)S(1)}, u32[]{:S(2)}, u32[]{:S(2)}) collective-permute-start(bf16[32,8,128]{2,1,0:T(8,128)(2,1)} %get-tuple-element.29), channel_id=1, source_target_pairs={{0,1},{1,0},{2,3},{3,2},{4,5},{5,4},{6,7},{7,6},{8,9},{9,8},{10,11... | collective-permute-start | bytes 196616 | tf_op jit(solution)/shard_map/ppermute | solution.py:584
  9.4 0.7 collective-permute-start.1
  10.9 0.1 pad_maximum_fusion.refs_2_.refs_15_.refs_5_
  11.0 0.3 collective-permute-done.refs_0_
  11.3 0.0 collective-permute-done.1.refs_1_
  11.3 1.2 %corner_kernel.1 = (f32[32,8,128]{2,1,0:T(8,128)S(1)}, bf16[67,8,256]{2,1,0:T(8,128)(2,1)}, bf16[67,8,256]{2,1,0:T(8,128)(2,1)}) custom-call(bf16[32,8,128]{2,1,0:T(8,128)(2,1)S(1)} %collective-permute-done.refs_0_, bf16[32,8,128]{2,1,0:T(8,128)(2,1)S(1)} %collective-permute-done.1.refs_1_, ...), custom_call_target="tpu_custom_call", output_to_operand_aliasing={{1}: (3, {}), {2}: (4, {})} | custom-call | tf_op jit(solution)/shard_map/corner_kernel/pallas_call | solution.py:659
  12.5 3.4 %collective-permute-start.2 = (bf16[67,8,256]{2,1,0:T(8,128)(2,1)}, bf16[67,8,256]{2,1,0:T(8,128)(2,1)S(1)}, u32[]{:S(2)}, u32[]{:S(2)}) collective-permute-start(bf16[67,8,256]{2,1,0:T(8,128)(2,1)} %get-tuple-element.33), channel_id=1, source_target_pairs={{0,4},{4,0},{1,5},{5,1},{2,6},{6,2},{3,7},{7,3},{8,12},{12,8},{9,1... | collective-permute-start | bytes 823304 | tf_op jit(solution)/shard_map/ppermute | solution.py:584
  15.9 7.0 %collective-permute-start.3 = (bf16[67,8,256]{2,1,0:T(8,128)(2,1)}, bf16[67,8,256]{2,1,0:T(8,128)(2,1)S(1)}, u32[]{:S(2)}, u32[]{:S(2)}) collective-permute-start(bf16[67,8,256]{2,1,0:T(8,128)(2,1)} %get-tuple-element.34), channel_id=1, source_target_pairs={{4,8},{8,4},{5,9},{9,5},{6,10},{10,6},{7,11},{11,7},{12,16},{16,12... | collective-permute-start | bytes 823304 | tf_op jit(solution)/shard_map/ppermute | solution.py:584
  22.9 0.0 copy-done
  23.0 10.5 %inner_rows.1 = (f32[3,32,8,256]{3,2,1,0:T(8,128)}, f32[3,32,8,256]{3,2,1,0:T(8,128)}, f32[3,32,8,256]{3,2,1,0:T(8,128)}, f32[3,32,8,256]{3,2,1,0:T(8,128)}, f32...) custom-call(bf16[3,32,8,256]{3,2,1,0:T(8,128)(2,1)} %refs_0_.3, ...), custom_call_target="tpu_custom_call" | custom-call | flops 40000000 | bytes 12000000 | tf_op jit(solution)/shard_map/inner_rows/pallas_call | solution.py:690
  33.4 0.0 collective-permute-done.2.refs_0_
  33.4 0.0 collective-permute-done.3.refs_1_
  33.4 4.3 %edge_rows.1 = (f32[3,32,8,256]{3,2,1,0:T(8,128)}, f32[3,32,8,256]{3,2,1,0:T(8,128)}, f32[3,32,8,256]{3,2,1,0:T(8,128)}, f32[3,32,8,256]{3,2,1,0:T(8,128)}, f32[...) custom-call(bf16[67,8,256]{2,1,0:T(8,128)(2,1)S(1)} %collective-perm, ...), custom_call_target="tpu_custom_call", output_to_operand_aliasing={{0}: (6, {}), {1}: (7, {}), {2}: (8, {}), {3}: (9, {}), {4}... | custom-call | flops 16000000 | bytes 6000000 | tf_op jit(solution)/shard_map/edge_rows/pallas_call | solution.py:709
  37.8 29.1 %all_to_all.5 = f32[256,1,128]{2,1,0:T(1,128)S(1)} all-to-all(f32[256,1,128]{2,1,0:T(1,128)S(1)} %get-tuple-element.50), channel_id=1, replica_groups=mesh['gy'=64,'gz'=4] {'gy','gz'}, dimensions={0} | all-to-all | bytes 262144 | tf_op jit(solution)/shard_map/all_to_all | solution.py:727
  66.8 0.8 %slice_reduce_fusion = f32[4]{0:T(128)} fusion(f32[256,1,128]{2,1,0:T(1,128)S(1)} %all_to_all.5), kind=kLoop, calls=%fused_computation | loop fusion | flops 1020 | bytes 4112 | tf_op jit(solution)/shard_map/reduce_sum | solution.py:728
Async XLA Ops:
  0.6 22.3 %copy-start = (f32[4]{0:T(128)S(1)}, f32[4]{0:T(128)}, u32[]{:S(2)}) copy-start(f32[4]{0:T(128)} %refs_4_.5) | copy-start | bytes 52
  6.9 4.4 %collective-permute-start = (bf16[32,8,128]{2,1,0:T(8,128)(2,1)}, bf16[32,8,128]{2,1,0:T(8,128)(2,1)S(1)}, u32[]{:S(2)}, u32[]{:S(2)}) collective-permute-start(bf16[32,8,128]{2,1,0:T(8,128)(2,1)} %get-tuple-element.29), channel_id=1, source_target_pairs={{0,1},{1,0},{2,3},{3,2},{4,5},{5,4},{6,7},{7,6},{8,9},{9,8},{10,11... | collective-permute-start | bytes 196616 | tf_op jit(solution)/shard_map/ppermute | solution.py:584
  9.4 1.9 %collective-permute-start.1 = (bf16[32,8,128]{2,1,0:T(8,128)(2,1)}, bf16[32,8,128]{2,1,0:T(8,128)(2,1)S(1)}, u32[]{:S(2)}, u32[]{:S(2)}) collective-permute-start(bf16[32,8,128]{2,1,0:T(8,128)(2,1)} %get-tuple-element.30), channel_id=1, source_target_pairs={{1,2},{2,1},{5,6},{6,5},{9,10},{10,9},{13,14},{14,13},{17,18},{18,... | collective-permute-start | bytes 196616 | tf_op jit(solution)/shard_map/ppermute | solution.py:584
  12.5 20.9 %collective-permute-start.2 = (bf16[67,8,256]{2,1,0:T(8,128)(2,1)}, bf16[67,8,256]{2,1,0:T(8,128)(2,1)S(1)}, u32[]{:S(2)}, u32[]{:S(2)}) collective-permute-start(bf16[67,8,256]{2,1,0:T(8,128)(2,1)} %get-tuple-element.33), channel_id=1, source_target_pairs={{0,4},{4,0},{1,5},{5,1},{2,6},{6,2},{3,7},{7,3},{8,12},{12,8},{9,1... | collective-permute-start | bytes 823304 | tf_op jit(solution)/shard_map/ppermute | solution.py:584
  15.9 17.5 %collective-permute-start.3 = (bf16[67,8,256]{2,1,0:T(8,128)(2,1)}, bf16[67,8,256]{2,1,0:T(8,128)(2,1)S(1)}, u32[]{:S(2)}, u32[]{:S(2)}) collective-permute-start(bf16[67,8,256]{2,1,0:T(8,128)(2,1)} %get-tuple-element.34), channel_id=1, source_target_pairs={{4,8},{8,4},{5,9},{9,5},{6,10},{10,6},{7,11},{11,7},{12,16},{16,12... | collective-permute-start | bytes 823304 | tf_op jit(solution)/shard_map/ppermute | solution.py:584

commit v6 on v5

--- a/solution.py
+++ b/solution.py
@@ -86,9 +86,8 @@
 def pack_kernel(rows, *refs):
     n = len(NAMES)
     given, whole = dict(zip(NAMES, refs[:n])), dict(zip(NAMES, refs[n : 2 * n]))
-    first, second = refs[2 * n : 2 * n + 2]
-    outs = refs[2 * n + 2 : 2 * n + 4]
-    messages, floats, ints, sems, out_sems = refs[2 * n + 4 :]
+    edges, *outs = refs[2 * n : 2 * n + 3]
+    messages, floats, ints, sems, out_sems = refs[2 * n + 3 :]
     step = pl.program_id(0)
     even = lax.rem(lax.axis_index("gy"), 2) == 0
     copies, later = [], []
@@ -136,25 +135,22 @@
                 messages[side, LOW_BITS + comp[1]] = low.astype(BF16)
         go(leaving)
 
-    even_z = lax.rem(lax.axis_index("gz"), 2) == 0
     lane = lane_of((8, 128))
 
     def some(block, carry):
         ys = [block * 4 + k for k in range(4)]
-        low = [jnp.zeros((8, 128), F32) for y in ys]
-        high = [jnp.zeros((8, 128), F32) for y in ys]
+        packed = [jnp.zeros((8, 128), F32) for y in ys]
         for comp in reversed(COMPS):
             inside = lane < SPOT[comp] + WIDTH[comp[0]]
             for k, y in enumerate(ys):
                 value = pull(given[comp[0]], comp, y)
-                low[k] = jnp.where(inside, pltpu.roll(value[:, :128], SPOT[comp], 1), low[k])
-                high[k] = jnp.where(inside, pltpu.roll(value[:, 128:], SPOT[comp], 1), high[k])
+                value = jnp.where(lane < 64, value[:, :128], value[:, 128:])
+                packed[k] = jnp.where(inside, pltpu.roll(value, SPOT[comp], 1), packed[k])
         for k, y in enumerate(ys):
-            first[y] = jnp.where(even_z, high[k], low[k]).astype(BF16)
-            second[y] = jnp.where(even_z, low[k], high[k]).astype(BF16)
+            edges[y] = packed[k].astype(BF16)
         return carry
 
-    lax.fori_loop(0, first.shape[0] // 4, some, 0)
+    lax.fori_loop(0, edges.shape[0] // 4, some, 0)
 
     @pl.when(step == pl.num_programs(0) - 1)
     def _():
@@ -638,12 +634,12 @@
         return pltpu.CompilerParams(vmem_limit_bytes=mib * 1024 * 1024)
 
     tile_block = pl.BlockSpec((rows // blocks, 8, 128), lambda i: (i, 0, 0))
-    send_first, send_second, send_near, send_far = pl.pallas_call(
+    send_edges, send_near, send_far = pl.pallas_call(
         lambda *refs: pack_kernel(rows, *refs),
         grid=(blocks,),
-        out_shape=(tile_shape, tile_shape, message, message),
+        out_shape=(tile_shape, message, message),
         in_specs=[row_block(array) for array in given] + [hbm] * len(given),
-        out_specs=(tile_block, tile_block, hbm, hbm),
+        out_specs=(tile_block, hbm, hbm),
         scratch_shapes=[
             pltpu.VMEM((2, PLANES, 8, 256), BF16),
             pltpu.VMEM((2, 24, 8, 256), F32),
@@ -654,8 +650,8 @@
         compiler_params=grant(60),
         name="pack_kernel",
     )(*given, *given)
-    first = swapped(send_first, "gz", 0)
-    second = swapped(send_second, "gz", 1)
+    first = swapped(send_edges, "gz", 0)
+    second = swapped(send_edges, "gz", 1)
     tiles, send_near, send_far = pl.pallas_call(
         lambda *refs: corner_kernel(rows, *refs),
         out_shape=(jax.ShapeDtypeStruct((rows, 8, 128), F32), message, message),

time: 67.9 us -> 69.5 us (1.024)
  starting transfers between devices: 13.6 us -> 14.9 us
    ppermute x4, starting transfers between devices: 13.6 us -> 14.9 us  [swapped(): return lax.ppermute(block, ('gy', 'gz'), pairs)]
where the time goes in v6:
time: 69.5 us; the launch traced here: 69.2 us
  blocking collectives  29 us (42%)
  Pallas kernels  21.9 us (32%)
  starting transfers between devices  14.9 us (21%)
  between operations  1.52 us (2%)
  waiting for transfers between devices  0.99 us (1%)
  other arithmetic  0.87 us (1%)
    all_to_all x1, blocking collectives, on_device(): parts = lax.all_to_all(sent, ('gy', 'gz'), 0, 0)  29 us
    ppermute x4, starting transfers between devices, swapped(): return lax.ppermute(block, ('gy', 'gz'), pairs)  14.9 us
    pallas_call x1, Pallas kernels, on_device(): pl.pallas_call(lambda *refs: inner_kernel(rows, *refs), out_shape=tuple((...  10.5 us
    pallas_call x1, Pallas kernels, on_device(): pl.pallas_call(lambda *refs: pack_kernel(rows, *refs), grid=(blocks,), ou...  5.92 us
    pallas_call x1, Pallas kernels, on_device(): pl.pallas_call(lambda *refs: edge_kernel(rows, 1.0 / math.sqrt(cells), *r...  4.34 us
  transfers between devices with their start and end apart: 4, of which 1 were waited for; matrix products, arithmetic and copies ran while one was open for 0% of the time, Pallas kernels for 15%

profile of v6, /device:TPU:1, one launch (start us, length us, event | category | flops | bytes accessed | tf_op | source)
XLA Modules:
  0.0 69.2 jit_solution(10767885954384625525)
XLA Ops:
  0.6 0.0 copy-start
  0.6 5.9 %pack_kernel.1 = (bf16[32,8,128]{2,1,0:T(8,128)(2,1)}, bf16[67,8,256]{2,1,0:T(8,128)(2,1)}, bf16[67,8,256]{2,1,0:T(8,128)(2,1)}) custom-call(bf16[3,32,8,256]{3,2,1,0:T(8,128)(2,1)} %refs_0_.3, bf16[3,32,8,256]{3,2,1,0:T(8,128)(2,1)} %refs_1_.3, bf16[3,32,8,256]{3,2,1,0:T(8,128)(2,1)} %refs_2_.3, bf16[3,32,8,256]{3,2,1,0:T(8,128)(2,1)} %refs_3_.3, ...), custom_call_target="tpu_custom_call" | custom-call | tf_op jit(solution)/shard_map/pack_kernel/pallas_call | solution.py:637
  6.6 0.7 collective-permute-start.1
  7.2 5.4 %collective-permute-start = (bf16[32,8,128]{2,1,0:T(8,128)(2,1)}, bf16[32,8,128]{2,1,0:T(8,128)(2,1)S(1)}, u32[]{:S(2)}, u32[]{:S(2)}) collective-permute-start(bf16[32,8,128]{2,1,0:T(8,128)(2,1)} %get-tuple-element.28), channel_id=1, source_target_pairs={{0,1},{1,0},{2,3},{3,2},{4,5},{5,4},{6,7},{7,6},{8,9},{9,8},{10,11... | collective-permute-start | bytes 196616 | tf_op jit(solution)/shard_map/ppermute | solution.py:580
  13.5 0.1 pad_maximum_fusion.refs_2_.refs_15_.refs_5_
  13.5 0.0 collective-permute-done.1.refs_1_
  13.5 1.0 %collective-permute-done.refs_0_ = bf16[32,8,128]{2,1,0:T(8,128)(2,1)S(1)} collective-permute-done((bf16[32,8,128]{2,1,0:T(8,128)(2,1)}, bf16[32,8,128]{2,1,0:T(8,128)(2,1)S(1)}, u32[]{:S(2)}, u32[]{:S(2)}) %collective-permute-start) | collective-permute-done | bytes 65568 | tf_op jit(solution)/shard_map/ppermute | solution.py:580
  14.5 1.2 %corner_kernel.1 = (f32[32,8,128]{2,1,0:T(8,128)S(1)}, bf16[67,8,256]{2,1,0:T(8,128)(2,1)}, bf16[67,8,256]{2,1,0:T(8,128)(2,1)}) custom-call(bf16[32,8,128]{2,1,0:T(8,128)(2,1)S(1)} %collective-permute-done.refs_0_, bf16[32,8,128]{2,1,0:T(8,128)(2,1)S(1)} %collective-permute-done.1.refs_1_, ...), custom_call_target="tpu_custom_call", output_to_operand_aliasing={{1}: (3, {}), {2}: (4, {})} | custom-call | tf_op jit(solution)/shard_map/corner_kernel/pallas_call | solution.py:655
  15.7 1.9 %collective-permute-start.2 = (bf16[67,8,256]{2,1,0:T(8,128)(2,1)}, bf16[67,8,256]{2,1,0:T(8,128)(2,1)S(1)}, u32[]{:S(2)}, u32[]{:S(2)}) collective-permute-start(bf16[67,8,256]{2,1,0:T(8,128)(2,1)} %get-tuple-element.31), channel_id=1, source_target_pairs={{0,4},{4,0},{1,5},{5,1},{2,6},{6,2},{3,7},{7,3},{8,12},{12,8},{9,1... | collective-permute-start | bytes 823304 | tf_op jit(solution)/shard_map/ppermute | solution.py:580
  17.6 6.9 %collective-permute-start.3 = (bf16[67,8,256]{2,1,0:T(8,128)(2,1)}, bf16[67,8,256]{2,1,0:T(8,128)(2,1)S(1)}, u32[]{:S(2)}, u32[]{:S(2)}) collective-permute-start(bf16[67,8,256]{2,1,0:T(8,128)(2,1)} %get-tuple-element.32), channel_id=1, source_target_pairs={{4,8},{8,4},{5,9},{9,5},{6,10},{10,6},{7,11},{11,7},{12,16},{16,12... | collective-permute-start | bytes 823304 | tf_op jit(solution)/shard_map/ppermute | solution.py:580
  24.6 0.0 copy-done
  24.6 10.5 %inner_rows.1 = (f32[3,32,8,256]{3,2,1,0:T(8,128)}, f32[3,32,8,256]{3,2,1,0:T(8,128)}, f32[3,32,8,256]{3,2,1,0:T(8,128)}, f32[3,32,8,256]{3,2,1,0:T(8,128)}, f32...) custom-call(bf16[3,32,8,256]{3,2,1,0:T(8,128)(2,1)} %refs_0_.3, ...), custom_call_target="tpu_custom_call" | custom-call | flops 40000000 | bytes 12000000 | tf_op jit(solution)/shard_map/inner_rows/pallas_call | solution.py:686
  35.0 0.0 collective-permute-done.2.refs_0_
  35.0 0.0 collective-permute-done.3.refs_1_
  35.1 4.3 %edge_rows.1 = (f32[3,32,8,256]{3,2,1,0:T(8,128)}, f32[3,32,8,256]{3,2,1,0:T(8,128)}, f32[3,32,8,256]{3,2,1,0:T(8,128)}, f32[3,32,8,256]{3,2,1,0:T(8,128)}, f32[...) custom-call(bf16[67,8,256]{2,1,0:T(8,128)(2,1)S(1)} %collective-perm, ...), custom_call_target="tpu_custom_call", output_to_operand_aliasing={{0}: (6, {}), {1}: (7, {}), {2}: (8, {}), {3}: (9, {}), {4}... | custom-call | flops 16000000 | bytes 6000000 | tf_op jit(solution)/shard_map/edge_rows/pallas_call | solution.py:705
  39.4 29.0 %all_to_all.5 = f32[256,1,128]{2,1,0:T(1,128)S(1)} all-to-all(f32[256,1,128]{2,1,0:T(1,128)S(1)} %get-tuple-element.48), channel_id=1, replica_groups=mesh['gy'=64,'gz'=4] {'gy','gz'}, dimensions={0} | all-to-all | bytes 262144 | tf_op jit(solution)/shard_map/all_to_all | solution.py:723
  68.4 0.8 %slice_reduce_fusion = f32[4]{0:T(128)} fusion(f32[256,1,128]{2,1,0:T(1,128)S(1)} %all_to_all.5), kind=kLoop, calls=%fused_computation | loop fusion | flops 1020 | bytes 4112 | tf_op jit(solution)/shard_map/reduce_sum | solution.py:724
Async XLA Ops:
  0.6 23.9 %copy-start = (f32[4]{0:T(128)S(1)}, f32[4]{0:T(128)}, u32[]{:S(2)}) copy-start(f32[4]{0:T(128)} %refs_4_.5) | copy-start | bytes 52
  6.6 7.0 %collective-permute-start.1 = (bf16[32,8,128]{2,1,0:T(8,128)(2,1)}, bf16[32,8,128]{2,1,0:T(8,128)(2,1)S(1)}, u32[]{:S(2)}, u32[]{:S(2)}) collective-permute-start(bf16[32,8,128]{2,1,0:T(8,128)(2,1)} %get-tuple-element.28), channel_id=1, source_target_pairs={{1,2},{2,1},{5,6},{6,5},{9,10},{10,9},{13,14},{14,13},{17,18},{18,... | collective-permute-start | bytes 196616 | tf_op jit(solution)/shard_map/ppermute | solution.py:580
  7.2 7.3 %collective-permute-start = (bf16[32,8,128]{2,1,0:T(8,128)(2,1)}, bf16[32,8,128]{2,1,0:T(8,128)(2,1)S(1)}, u32[]{:S(2)}, u32[]{:S(2)}) collective-permute-start(bf16[32,8,128]{2,1,0:T(8,128)(2,1)} %get-tuple-element.28), channel_id=1, source_target_pairs={{0,1},{1,0},{2,3},{3,2},{4,5},{5,4},{6,7},{7,6},{8,9},{9,8},{10,11... | collective-permute-start | bytes 196616 | tf_op jit(solution)/shard_map/ppermute | solution.py:580
  15.7 19.3 %collective-permute-start.2 = (bf16[67,8,256]{2,1,0:T(8,128)(2,1)}, bf16[67,8,256]{2,1,0:T(8,128)(2,1)S(1)}, u32[]{:S(2)}, u32[]{:S(2)}) collective-permute-start(bf16[67,8,256]{2,1,0:T(8,128)(2,1)} %get-tuple-element.31), channel_id=1, source_target_pairs={{0,4},{4,0},{1,5},{5,1},{2,6},{6,2},{3,7},{7,3},{8,12},{12,8},{9,1... | collective-permute-start | bytes 823304 | tf_op jit(solution)/shard_map/ppermute | solution.py:580
  17.6 17.4 %collective-permute-start.3 = (bf16[67,8,256]{2,1,0:T(8,128)(2,1)}, bf16[67,8,256]{2,1,0:T(8,128)(2,1)S(1)}, u32[]{:S(2)}, u32[]{:S(2)}) collective-permute-start(bf16[67,8,256]{2,1,0:T(8,128)(2,1)} %get-tuple-element.32), channel_id=1, source_target_pairs={{4,8},{8,4},{5,9},{9,5},{6,10},{10,6},{7,11},{11,7},{12,16},{16,12... | collective-permute-start | bytes 823304 | tf_op jit(solution)/shard_map/ppermute | solution.py:580
